TPU v7x, 128 devices: a whole 4x4x4 slice. The times are simulated.
128 devices in a mesh: ctx: 16 (over x, y), role: 2 (over z_hi), exp: 4 (over z_lo, core).
Axes of the slice: x: 4, y: 4, z: 4 (z_hi: 2, z_lo: 2; z = z_hi * 2 + z_lo), core: 2. Of those that a mesh axis runs over, the one named last changes fastest.
Arguments:
- queries: bfloat16 [2048, 32768], P('ctx', ('role', 'exp')), may hold values from -56 to 56
- latent: bfloat16 [2048, 512], P('ctx'), may hold values from -5 to 5
- frames: int32 [2048], replicated, may hold values from 0 to 31, never falling along the last dimension, each value on 1 to 128 neighbouring positions
- w_uv: bfloat16 [64, 512, 128], P(('role', 'exp')), may hold values from -0.5 to 0.5
- w_out: bfloat16 [8192, 7168], P(('role', 'exp'), 'ctx'), may hold values from -0.25 to 0.25
- residual: bfloat16 [2048, 7168], P('ctx', ('role', 'exp')), may hold values from -40 to 40
- norm_gain: float32 [7168], replicated, may hold values from 0.5 to 2
- expert_ids: int32 [2048, 2], P('ctx'), may hold values from 0 to 15, all different within a row; in each aligned block of 128 rows (0 to 127, 128 to 255, ...) at most 20 rows name the same one
- mix_codes: int32 [2048, 2], P('ctx'), may hold values from 1 to 256
- w_gate: bfloat16 [16, 7168, 1024], P('ctx', None, ('role', 'exp')), may hold values from -0.0625 to 0.0625
- w_up: bfloat16 [16, 7168, 1024], P('ctx', None, ('role', 'exp')), may hold values from -0.0625 to 0.0625
- w_down: bfloat16 [16, 1024, 7168], P('ctx', ('role', 'exp')), may hold values from -0.375 to 0.375
- grad_out: bfloat16 [2048, 7168], P('ctx', ('role', 'exp')), may hold values from -6 to 6
Outputs:
- layer_out: bfloat16 [2048, 7168], P('ctx', ('role', 'exp'))
- grad_pre_norm: bfloat16 [2048, 7168], P('ctx', ('role', 'exp'))
- grad_gate: bfloat16 [16, 7168, 1024], P('ctx', None, ('role', 'exp'))
- grad_up: bfloat16 [16, 7168, 1024], P('ctx', None, ('role', 'exp'))
- grad_down: bfloat16 [16, 1024, 7168], P('ctx', ('role', 'exp'))
Inputs may be any that keep to these rules, and one draw needn't show every extreme that they name: `expert_ids`: each row names 2 different experts. Among the 128 rows of one index of ctx no expert is named more than 20 times, and in some such block one expert is named exactly 20 times. `frames`: never falls along the scene; each frame holds 1 to 128 tokens and one holds exactly 128.
All inputs are finite; a program needn't handle non-finite values.
Results may differ from a plain program's by a relative error of at most 0.03.
Values may be sent and summed in bfloat16 or wider, within the bound.
No kernel may reach another device: no remote copies, remote signals or barrier semaphores. Data moves between devices by JAX's collectives and lax.ppermute only.
A program may use at most 128 MiB of HBM per device.

v0:
```python
import functools

import jax
import jax.numpy as jnp
from jax import lax
from jax.experimental import pallas as pl
from jax.experimental.pallas import tpu as pltpu
from jax.sharding import PartitionSpec as P

ALL = ("ctx", "role", "exp")
GROUP = ("role", "exp")
BF16 = jnp.bfloat16
F32 = jnp.float32
SIDE = 4
LANES = 128


def dot(a, b, dims=((1,), (0,))):
    return lax.dot_general(a, b, (dims, ((), ())), preferred_element_type=F32)


def shift_z(block, step):
    return lax.ppermute(block, GROUP, [(g, (g + 2 * step) % 8) for g in range(8)])


def swap_core(block):
    return lax.ppermute(block, GROUP, [(g, g ^ 1) for g in range(8)])


def shift_plane(block, phase, step):
    pairs = []
    for c in range(SIDE * SIDE):
        x, y = divmod(c, SIDE)
        for g in range(8):
            if g % 2 == phase:
                to = x * SIDE + (y + step) % SIDE
            else:
                to = (x + step) % SIDE * SIDE + y
            pairs.append((c * 8 + g, to * 8 + g))
    return lax.ppermute(block, ALL, pairs)


def ring_list(block, shift):
    half = block.shape[0] // 2
    before = shift(block, 1)
    after = shift(block, -1)
    far = [shift(before[:half], 1), shift(after[half:], -1)]
    return [block, after, far, before]


def ctx_gather(block):
    own, after, far, before = ring_list(block, lambda b, s: shift_plane(b, 0, s))
    first = jnp.stack([own, after, jnp.concatenate(far, 0), before])
    own, after, far, before = ring_list(first, lambda b, s: shift_plane(b, 1, s))
    return [own, after, *far, before]


def group_gather(block):
    return lax.all_gather(block, GROUP, axis=0)


def group_exchange(blocks):
    received = [
        blocks[0],
        shift_z(blocks[3], -1),
        shift_z(blocks[2], 2),
        shift_z(blocks[1], 1),
    ]
    return [part for pair in received for part in (pair, swap_core(pair))]


def roll_lead(array, shift, axis):
    twice = jnp.concatenate([array, array], axis)
    return lax.dynamic_slice_in_dim(twice, shift, SIDE, axis)


def split3(value):
    high = lax.reduce_precision(value, 8, 7)
    rest = value - high
    middle = lax.reduce_precision(rest, 8, 7)
    low = lax.reduce_precision(rest - middle, 8, 7)
    return [term.astype(BF16) for term in (high, middle, low)]


def pad_lanes(terms):
    rows = terms[0].shape[0]
    blank = jnp.zeros((rows, LANES - len(terms)), BF16)
    return jnp.concatenate([t.reshape(rows, 1) for t in terms] + [blank], 1)


def lanes3(value):
    lane = lax.broadcasted_iota(jnp.int32, (value.shape[0], LANES), 1)
    high = value.astype(BF16).astype(F32)
    rest = value - high
    middle = rest.astype(BF16).astype(F32)
    low = rest - middle
    wide = jnp.where(lane == 0, high, jnp.where(lane == 1, middle, jnp.where(lane == 2, low, 0.0)))
    return wide.astype(BF16)


def call(kernel, outs, scalars=0, unread=0, **params):
    def run(*operands):
        whole = len(operands) - scalars - unread
        spaces = [pltpu.SMEM] * scalars + [pltpu.VMEM] * whole + [pl.ANY] * unread
        return pl.pallas_call(
            kernel,
            out_shape=outs,
            in_specs=[pl.BlockSpec(memory_space=space) for space in spaces],
            **params,
        )(*operands)

    return run


def member(place_ref, step, other):
    z = lax.rem(place_ref[0] + step, SIDE)
    return 2 * z + place_ref[1] + other - 2 * place_ref[1] * other


def prepare_kernel(place_ref, down_ref, gate_ref, up_ref, *outs):
    slice_width = outs[0].shape[1]
    hidden = down_ref.shape[0]
    for step in range(SIDE):
        for other in range(2):
            start = pl.multiple_of(member(place_ref, step, other) * slice_width, LANES)
            outs[step][other, :, :hidden] = gate_ref[pl.ds(start, slice_width), :]
            outs[step][other, :, hidden : 2 * hidden] = up_ref[pl.ds(start, slice_width), :]
            outs[step][other, :, 2 * hidden :] = down_ref[:, pl.ds(start, slice_width)].T


def attend_kernel(scale, q_ref, near_ref, far_ref, key_frame_ref, own_frame_ref, uv_ref, out_ref):
    heads, latent_width, value_width = uv_ref.shape
    tokens = q_ref.shape[0]
    keys = [near_ref[...], far_ref[...]]
    count = keys[0].shape[0]
    query = jnp.concatenate(
        [q_ref[:, h * latent_width : (h + 1) * latent_width] for h in range(heads)], 0
    )
    own = own_frame_ref[...]
    scores = []
    for part in range(2):
        visible = key_frame_ref[:, part * count : (part + 1) * count] <= own
        visible = jnp.concatenate([visible.astype(F32)] * heads, 0) > 0.5
        scores.append(jnp.where(visible, dot(query, keys[part], ((1,), (1,))) * scale, -1e30))
    top = jnp.maximum(*[jnp.max(s, axis=1, keepdims=True) for s in scores])
    weights = [jnp.exp(s - top) for s in scores]
    total = sum(jnp.sum(w, axis=1, keepdims=True) for w in weights)
    mix = sum(dot(w.astype(BF16), k) for w, k in zip(weights, keys))
    mix = (mix / total).astype(BF16)
    for h in range(heads):
        out_ref[:, h * value_width : (h + 1) * value_width] = dot(
            mix[h * tokens : (h + 1) * tokens], uv_ref[h]
        ).astype(BF16)


def out_proj_kernel(rows_ref, weight_ref, *refs):
    out_ref = refs[-1]
    members, columns, depth = weight_ref.shape
    total = jnp.zeros((rows_ref.shape[0] * rows_ref.shape[1], columns), F32)
    for place in range(members):
        rows = rows_ref[:, :, place * depth : (place + 1) * depth]
        rows = rows.reshape(total.shape[0], depth)
        total = total + dot(rows, weight_ref[place], ((1,), (1,)))
    out_ref[...] = total.astype(BF16).reshape(out_ref.shape)


def expert_kernel(place_ref, rows_ref, grads_ref, *refs):
    weight_refs, out_ref = refs[:4], refs[4]
    hidden = weight_refs[0].shape[2] // 3
    both, hidden_grad = 0.0, 0.0
    for place in range(8):
        weight_ref, other = weight_refs[place // 2], place % 2
        source = member(place_ref, place // 2, other)
        both = both + dot(rows_ref[source], weight_ref[other, :, : 2 * hidden])
        hidden_grad = hidden_grad + dot(grads_ref[source], weight_ref[other, :, 2 * hidden :])
    gate_in, up_in = both[:, :hidden], both[:, hidden:]
    gate_sig = 1.0 / (1.0 + jnp.exp(-gate_in))
    silu = gate_in * gate_sig
    gate_grad = hidden_grad * up_in * gate_sig * (1.0 + gate_in * (1.0 - gate_sig))
    up_grad = hidden_grad * silu
    center = jnp.sum(gate_grad * gate_in + up_grad * up_in, axis=1, keepdims=True)
    out_ref[:, :hidden] = gate_grad.astype(BF16)
    out_ref[:, hidden : 2 * hidden] = up_grad.astype(BF16)
    out_ref[:, 2 * hidden : 3 * hidden] = (silu * up_in).astype(BF16)
    out_ref[:, 3 * hidden :] = lanes3(center)


def weight_grad_kernel(rows_ref, grads_ref, hidden_ref, gate_ref, up_ref, down_ref):
    hidden = gate_ref.shape[1]
    members, _, slice_width = rows_ref.shape
    grads = hidden_ref[:, : 2 * hidden]
    units = hidden_ref[:, 2 * hidden : 3 * hidden]
    for place in range(members):
        part = slice(place * slice_width, (place + 1) * slice_width)
        both = dot(rows_ref[place], grads, ((0,), (0,)))
        gate_ref[part, :] = both[:, :hidden].astype(BF16)
        up_ref[part, :] = both[:, hidden:].astype(BF16)
        down_ref[:, part] = dot(units, grads_ref[place], ((0,), (0,))).astype(BF16)


def project_kernel(place_ref, hidden_ref, *refs):
    weight_refs, out_ref = refs[:8], refs[8]
    slice_width, wide = weight_refs[0].shape[1:]
    hidden = wide // 3
    rows, grads, center = 0.0, 0.0, 0.0
    for place in range(8):
        source = member(place_ref, place // 2, place % 2)
        weight = weight_refs[place][place % 2]
        units = hidden_ref[source]
        grads = grads + dot(units[:, : 2 * hidden], weight[:, : 2 * hidden], ((1,), (1,)))
        rows = rows + dot(units[:, 2 * hidden : 3 * hidden], weight[:, 2 * hidden :], ((1,), (1,)))
        center = center + jnp.sum(units[:, 3 * hidden :].astype(F32), axis=1, keepdims=True)
    rows, grads, center = rows.astype(BF16), grads.astype(BF16), lanes3(center)
    sources, capacity = out_ref.shape[:2]
    for source in range(sources):
        part = slice(source * capacity, (source + 1) * capacity)
        out_ref[source, :, :slice_width] = rows[part]
        out_ref[source, :, slice_width : 2 * slice_width] = grads[part]
        out_ref[source, :, 2 * slice_width :] = center[part]


def per_device(
    queries,
    latent,
    frames,
    w_uv,
    w_out,
    residual,
    norm_gain,
    expert_ids,
    mix_codes,
    w_gate,
    w_up,
    w_down,
    grad_out,
):
    ctx_count = lax.axis_size("ctx")
    ctx_place = lax.axis_index("ctx")
    plane_x, plane_y = ctx_place // SIDE, ctx_place % SIDE
    group_place = lax.axis_index(GROUP)
    place_z, core = group_place // 2, group_place % 2
    group_count = 8
    token_count = queries.shape[0]
    head_count, latent_width, value_width = w_uv.shape
    model_width = w_gate.shape[1]
    slice_width = residual.shape[1]
    top_count = expert_ids.shape[1]
    hidden_width = w_gate.shape[2]
    column_width = w_out.shape[1]
    part_tokens = token_count // group_count
    capacity = token_count * top_count // ctx_count * 5 // 4
    slot_total = ctx_count * capacity

    def shape(*dims):
        return jax.ShapeDtypeStruct(dims, BF16)

    places = jnp.stack([place_z, core]).astype(jnp.int32)

    out_weight = group_gather(w_out.T)
    weight_blocks = call(
        prepare_kernel, [shape(2, slice_width, 3 * hidden_width)] * SIDE, 1
    )(places, w_down[0], w_gate[0], w_up[0])
    slice_weights = group_exchange(weight_blocks)

    residual_part = lax.all_to_all(
        residual.reshape(group_count, part_tokens, slice_width), GROUP, 0, 0, tiled=True
    )

    chosen = expert_ids.reshape(-1)
    pair_range = jnp.arange(token_count * top_count, dtype=jnp.int32)
    same = (chosen[:, None] == chosen[None, :]) & (pair_range[None, :] < pair_range[:, None])
    earlier = jnp.sum(same.astype(jnp.int32), axis=1)
    slot_index = (chosen * capacity + earlier).reshape(token_count, top_count)
    slot_range = jnp.arange(slot_total, dtype=jnp.int32)
    code_values = mix_codes.astype(F32)
    mix_weight = code_values / jnp.sum(code_values, axis=1, keepdims=True)
    hits = [slot_index[:, k][None, :] == slot_range[:, None] for k in range(top_count)]
    pick = sum(hit.astype(F32) for hit in hits).astype(BF16)
    slot_weight = sum(
        jnp.sum(jnp.where(hits[k], mix_weight[:, k][None, :], 0.0), axis=1) for k in range(top_count)
    )
    returns = [
        (slot_index[:, k][:, None] == slot_range[None, :]).astype(BF16) for k in range(top_count)
    ]

    def to_experts(rows):
        return lax.all_to_all(rows, "ctx", split_axis=0, concat_axis=0, tiled=True)

    grad_rows = (dot(pick, grad_out) * slot_weight[:, None]).astype(BF16)
    grad_rows = to_experts(grad_rows)
    out_grad = group_gather(grad_rows)

    half = token_count // 2
    own_keys = ctx_gather(lax.dynamic_slice_in_dim(latent, core * half, half, 0))
    own_keys = jnp.concatenate(own_keys, 0).reshape(ctx_count * half, latent_width)
    other_keys = swap_core(own_keys)
    own_frames = lax.dynamic_slice_in_dim(frames, ctx_place * token_count, token_count)
    frame_grid = frames.reshape(SIDE, SIDE, 2, half)
    frame_grid = roll_lead(roll_lead(frame_grid, plane_x, 0), plane_y, 1)
    by_x = jnp.transpose(frame_grid, (2, 0, 1, 3))
    by_y = jnp.transpose(frame_grid, (2, 1, 0, 3))
    key_frames = jnp.where(
        core == 0,
        jnp.concatenate([by_x[0].reshape(-1), by_y[1].reshape(-1)]),
        jnp.concatenate([by_y[1].reshape(-1), by_x[0].reshape(-1)]),
    )
    heads = 2
    head_out = pl.pallas_call(
        functools.partial(attend_kernel, latent_width ** (-0.5)),
        out_shape=shape(token_count, head_count * value_width),
        grid=(head_count // heads,),
        in_specs=[
            pl.BlockSpec((token_count, heads * latent_width), lambda h: (0, h)),
            pl.BlockSpec(own_keys.shape, lambda h: (0, 0)),
            pl.BlockSpec(other_keys.shape, lambda h: (0, 0)),
            pl.BlockSpec((1, ctx_count * token_count), lambda h: (0, 0)),
            pl.BlockSpec((token_count, 1), lambda h: (0, 0)),
            pl.BlockSpec((heads, latent_width, value_width), lambda h: (h, 0, 0)),
        ],
        out_specs=pl.BlockSpec((token_count, heads * value_width), lambda h: (0, h)),
        name="attend",
    )(queries, own_keys, other_keys, key_frames[None], own_frames[:, None], w_uv)
    head_out = head_out.reshape(group_count, part_tokens, head_count * value_width)

    head_part = lax.all_to_all(head_out, GROUP, 0, 0, tiled=True)
    head_part = jnp.transpose(head_part, (1, 0, 2)).reshape(part_tokens, -1)
    all_heads = lax.all_gather(head_part, "ctx", axis=0)
    columns = call(
        out_proj_kernel, shape(ctx_count, part_tokens, column_width), unread=2 + SIDE
    )(all_heads, out_weight, residual_part, grad_rows, *weight_blocks)
    residual_part = jnp.transpose(residual_part, (1, 0, 2)).reshape(part_tokens, model_width)
    columns = to_experts(columns)
    attn_part = jnp.transpose(columns, (1, 0, 2)).reshape(part_tokens, model_width)
    pre_part = (residual_part.astype(F32) + attn_part.astype(F32)).astype(BF16)
    pre_wide = pre_part.astype(F32)
    inv_part = lax.rsqrt(jnp.mean(pre_wide * pre_wide, axis=-1, keepdims=True) + 1e-06)
    inv_lanes = pad_lanes(split3(inv_part))
    pre_send = jnp.concatenate(
        [
            jnp.transpose(pre_part.reshape(part_tokens, group_count, slice_width), (1, 0, 2)),
            jnp.broadcast_to(inv_lanes[None], (group_count, part_tokens, 128)),
        ],
        2,
    )
    pre_back = lax.all_to_all(pre_send, GROUP, 0, 0, tiled=True).reshape(token_count, -1)
    pre_norm = pre_back[:, :slice_width].astype(F32)
    inv_scale = jnp.sum(pre_back[:, slice_width : slice_width + 3].astype(F32), axis=1, keepdims=True)
    unit_rows = pre_norm * inv_scale
    local_gain = lax.dynamic_slice_in_dim(norm_gain, group_place * slice_width, slice_width)
    normed = (unit_rows * local_gain).astype(BF16)

    expert_rows = group_gather(to_experts(dot(pick, normed).astype(BF16)))
    hidden_send = call(expert_kernel, shape(slot_total, 3 * hidden_width + LANES), 1)(
        places, expert_rows, out_grad, *weight_blocks
    )
    hidden_all = group_gather(hidden_send)
    grad_gate, grad_up, grad_down = call(
        weight_grad_kernel,
        [shape(model_width, hidden_width)] * 2 + [shape(hidden_width, model_width)],
    )(expert_rows, out_grad, hidden_send)
    grad_gate, grad_up, grad_down = grad_gate[None], grad_up[None], grad_down[None]
    back = call(
        project_kernel, shape(ctx_count, capacity, 2 * slice_width + LANES), 1
    )(places, hidden_all, *slice_weights)
    back = to_experts(back).reshape(slot_total, 2 * slice_width + LANES)

    routed = sum(
        dot(returns[k], back[:, :slice_width]) * mix_weight[:, k : k + 1] for k in range(top_count)
    )
    layer_out = (pre_norm + routed).astype(BF16)
    summed = dot(returns[0] + returns[1], back[:, slice_width:])
    normed_grad = summed[:, :slice_width].astype(BF16).astype(F32)
    center = jnp.sum(summed[:, slice_width : slice_width + 3], axis=1, keepdims=True) / model_width
    scaled_grad = normed_grad * local_gain
    grad_pre_norm = (
        grad_out.astype(F32) + inv_scale * (scaled_grad - unit_rows * center)
    ).astype(BF16)
    return (layer_out, grad_pre_norm, grad_gate, grad_up, grad_down)


def solution(mesh):
    placed = (
        P("ctx", ("role", "exp")),
        P("ctx", None),
        P(),
        P(("role", "exp"), None, None),
        P(("role", "exp"), "ctx"),
        P("ctx", ("role", "exp")),
        P(),
        P("ctx", None),
        P("ctx", None),
        P("ctx", None, ("role", "exp")),
        P("ctx", None, ("role", "exp")),
        P("ctx", ("role", "exp"), None),
        P("ctx", ("role", "exp")),
    )

    return jax.shard_map(
        per_device,
        mesh=mesh,
        in_specs=placed,
        out_specs=(
            P("ctx", ("role", "exp")),
            P("ctx", ("role", "exp")),
            P("ctx", None, ("role", "exp")),
            P("ctx", None, ("role", "exp")),
            P("ctx", ("role", "exp"), None),
        ),
        check_vma=False,
    )
```

profile of v0, /device:TPU:1, one launch (start us, length us, event | category | flops | bytes accessed | tf_op | source)
XLA Modules:
  0.0 383.1 jit_solution(11630597115114293292)
XLA Ops:
  7.2 0.9 constant_dynamic-update-slice_fusion.7
  8.1 2.1 collective-permute-start.1
  10.2 1.3 collective-permute-start
  11.5 1.6 collective-permute-done.1
  13.3 2.6 collective-permute-start.3
  15.9 1.2 collective-permute-done.2
  17.2 1.6 collective-permute-start.5
  18.7 1.5 collective-permute-start.4
  20.3 3.7 collective-permute-done.5
  24.1 2.7 collective-permute-start.7
  26.8 2.2 collective-permute-done.6
  29.1 5.2 %collective-permute-start.8 = (bf16[1024,512]{1,0:T(8,128)(2,1)S(1)}, bf16[1024,512]{1,0:T(8,128)(2,1)S(1)}, u32[]{:S(2)}, u32[]{:S(2)}) collective-permute-start(bf16[1024,512]{1,0:T(8,128)(2,1)S(1)} %bitcast.69), channel_id=1, source_target_pairs={{0,1},{1,0},{2,3},{3,2},{4,5},{5,4},{6,7},{7,6},{8,9},{9,8},{10,11... | collective-permute-start | bytes 3145736 | tf_op jit(solution)/shard_map/ppermute | solution.py:27
  34.8 0.7 copy.79.own_frame_ref
  35.5 0.6 broadcast_select_fusion.key_frame_ref
  36.1 0.4 collective-permute-done.8.far_ref
  36.6 1.0 copy-done.12
  37.5 10.0 %attend.1 = bf16[128,1024]{1,0:T(8,128)(2,1)} custom-call(bf16[128,4096]{1,0:T(8,128)(2,1)} %q_ref.1, bf16[1024,512]{1,0:T(8,128)(2,1)} %bitcast.70, bf16[1024,512]{1,0:T(8,128)(2,1)} %copy-done.12, s32[1,2048]{1,0:T(1,128)} %broadcast_select_fusion.key_frame_ref, s32[128,1]{1,0:T(8,128)} %copy.79.own_frame_ref, bf16[8,512,128]{2,1,0:T(8,128)(2,1)} %uv_ref.1), custom_call_target="tpu_custom_call" | custom-call | tf_op jit(solution)/shard_map/attend/pallas_call | solution.py:308
  47.5 12.4 %all_to_all.45 = bf16[8,16,1024]{2,1,0:T(8,128)(2,1)S(1)} all-to-all(bf16[8,16,1024]{2,1,0:T(8,128)(2,1)} %bitcast.71), channel_id=1, replica_groups=mesh['ctx'=16,'role'=2,'exp'=4] {'role','exp'}, dimensions={0} | all-to-all | bytes 524288 | tf_op jit(solution)/shard_map/all_to_all | solution.py:325
  60.1 0.8 all_gather_reshape.3
  61.0 0.7 all-gather.14.cloned.1.call-update
  62.7 0.3 fusion
  63.1 21.3 %all_to_all.46 = bf16[16,20,896]{2,1,0:T(8,128)(2,1)S(1)} all-to-all(bf16[16,20,896]{2,1,0:T(8,128)(2,1)S(1)} %all_to_all.30), channel_id=1, replica_groups=mesh['ctx'=16,'role'=2,'exp'=4] {'ctx'}, dimensions={0} | all-to-all | bytes 1146880 | tf_op jit(solution)/shard_map/all_to_all | solution.py:287
  84.4 0.9 all_gather.32
  85.4 6.2 %all-to-all-start = ((bf16[8,16,896]{2,1,0:T(8,128)(2,1)}), bf16[8,16,896]{2,1,0:T(8,128)(2,1)S(1)}, u32[]{:S(2)}, u32[]{:S(2)}) async-start(bf16[8,16,896]{2,1,0:T(8,128)(2,1)} %bitcast), calls=%async_computation | async-start | bytes 458752 | tf_op jit(solution)/shard_map/all_to_all | solution.py:265
  91.6 0.6 pad_add_fusion.place_ref
  92.2 5.7 %shard_map.164 = (bf16[2,896,384]{2,1,0:T(8,128)(2,1)}, bf16[2,896,384]{2,1,0:T(8,128)(2,1)}, bf16[2,896,384]{2,1,0:T(8,128)(2,1)}, bf16[2,896,384]{2,1,0:T(8,128)(2,1)}) custom-call(s32[2]{0:T(128)} %pad_add_fusion.place_ref, bf16[128,7168]{1,0:T(8,128)(2,1)} %bitcast.66, bf16[7168,128]{1,0:T(8,128)(2,1)} %bitcast.67, bf16[7168,128]{1,0:T(8,128)(2,1)} %bitcast.68), custom_call_target="tpu_custom_call" | custom-call | tf_op jit(solution)/shard_map/pallas_call | solution.py:105
  97.9 0.9 all_to_all.32.refs_1_
  98.8 16.1 %all-gather.8.cloned.1.call-done.rows_ref = bf16[16,16,8192]{2,1,0:T(8,128)(2,1)} async-done(((bf16[1,16,8192]{2,1,0:T(8,128)(2,1)}), bf16[16,16,8192]{2,1,0:T(8,128)(2,1)}) %all-gather.8.cloned.1.call-update) | async-done | bytes 4194320 | tf_op jit(solution)/shard_map/all_gather | solution.py:327
  115.0 47.5 %all-gather.14.cloned.1.call-done = bf16[3584,1024]{1,0:T(8,128)(2,1)} async-done(((bf16[448,1024]{1,0:T(8,128)(2,1)}), bf16[3584,1024]{1,0:T(8,128)(2,1)}) %all-gather.14.cloned.1.call-update) | async-done | bytes 7340048 | tf_op jit(solution)/shard_map/all_gather | solution.py:59
  162.5 7.4 %shard_map.165 = bf16[16,16,448]{2,1,0:T(8,128)(2,1)} custom-call(bf16[16,16,8192]{2,1,0:T(8,128)(2,1)} %all-gather.8.cloned.1.call-done.rows_ref, bf16[8,448,1024]{2,1,0:T(8,128)(2,1)} %bitcast.60, bf16[8,16,896]{2,1,0:T(8,128)(2,1)} %copy-done.2, bf16[320,896]{1,0:T(8,128)(2,1)} %all_to_all.32.refs_1_, ...), custom_call_target="tpu_custom_call" | custom-call | tf_op jit(solution)/shard_map/pallas_call | solution.py:105
  169.9 6.5 %all-to-all-start.3 = ((bf16[16,16,448]{2,1,0:T(8,128)(2,1)}), bf16[16,16,448]{2,1,0:T(8,128)(2,1)S(1)}, u32[]{:S(2)}, u32[]{:S(2)}) async-start(bf16[16,16,448]{2,1,0:T(8,128)(2,1)} %shard_map.165), calls=%async_computation.3 | async-start | bytes 524288 | tf_op jit(solution)/shard_map/all_to_all | solution.py:287
  176.5 7.6 %all-to-all-done.3 = bf16[16,16,448]{2,1,0:T(8,128)(2,1)S(1)} async-done(((bf16[16,16,448]{2,1,0:T(8,128)(2,1)}), bf16[16,16,448]{2,1,0:T(8,128)(2,1)S(1)}, u32[]{:S(2)}, u32[]{:S(2)}) %all-to-all-start.3) | async-done | bytes 229408 | tf_op jit(solution)/shard_map/all_to_all | solution.py:287
  184.2 0.3 copy.83
  185.2 0.8 pad_maximum_fusion.1
  186.0 5.1 %all-to-all-start.4 = ((bf16[8,16,1024]{2,1,0:T(8,128)(2,1)}), bf16[8,16,1024]{2,1,0:T(8,128)(2,1)S(1)}, u32[]{:S(2)}, u32[]{:S(2)}) async-start(bf16[8,16,1024]{2,1,0:T(8,128)(2,1)} %pad_maximum_fusion.1), calls=%async_computation.4 | async-start | bytes 524288 | tf_op jit(solution)/shard_map/all_to_all | solution.py:345
  191.1 0.8 dynamic_slice.19
  191.9 7.3 %all-to-all-done.4 = bf16[8,16,1024]{2,1,0:T(8,128)(2,1)S(1)} async-done(((bf16[8,16,1024]{2,1,0:T(8,128)(2,1)}), bf16[8,16,1024]{2,1,0:T(8,128)(2,1)S(1)}, u32[]{:S(2)}, u32[]{:S(2)}) %all-to-all-start.4) | async-done | bytes 262176 | tf_op jit(solution)/shard_map/all_to_all | solution.py:345
  199.3 0.4 convolution_convert_fusion
  199.8 16.8 %all_to_all.47 = bf16[16,20,896]{2,1,0:T(8,128)(2,1)S(1)} all-to-all(bf16[16,20,896]{2,1,0:T(8,128)(2,1)S(1)} %all_to_all.35), channel_id=1, replica_groups=mesh['ctx'=16,'role'=2,'exp'=4] {'ctx'}, dimensions={0} | all-to-all | bytes 1146880 | tf_op jit(solution)/shard_map/all_to_all | solution.py:287
  216.6 0.9 all_gather.30
  217.6 32.1 %all-gather.10.cloned.1.call-done.rows_ref = bf16[8,320,896]{2,1,0:T(8,128)(2,1)} async-done(((bf16[1,320,896]{2,1,0:T(8,128)(2,1)}), bf16[8,320,896]{2,1,0:T(8,128)(2,1)}) %all-gather.10.cloned.1.call-update) | async-done | bytes 4587536 | tf_op jit(solution)/shard_map/all_gather | solution.py:59
  249.7 8.8 %shard_map.166.hidden_ref = bf16[320,512]{1,0:T(8,128)(2,1)} custom-call(s32[2]{0:T(128)} %pad_add_fusion.place_ref, bf16[8,320,896]{2,1,0:T(8,128)(2,1)} %all-gather.10.cloned.1.call-done.rows_ref, bf16[8,320,896]{2,1,0:T(8,128)(2,1)} %all-gather.12.cloned.1.call-done.grads_ref, bf16[2,896,384]{2,1,0:T(8,128)(2,1)} %get-tuple-element.12.refs_2_.refs_0_, ...), custom_call_target="tpu_custom_call" | custom-call | tf_op jit(solution)/shard_map/pallas_call | solution.py:105
  258.6 0.6 collective-permute-start.10
  259.1 1.4 collective-permute-start.12
  260.6 0.4 collective-permute-start.14
  260.9 1.1 collective-permute-start.9
  262.1 37.2 %collective-permute-done.10.refs_2_ = bf16[2,896,384]{2,1,0:T(8,128)(2,1)S(1)} collective-permute-done((bf16[2,896,384]{2,1,0:T(8,128)(2,1)}, bf16[2,896,384]{2,1,0:T(8,128)(2,1)S(1)}, u32[]{:S(2)}, u32[]{:S(2)}) %collective-permute-start.10) | collective-permute-done | bytes 1376288 | tf_op jit(solution)/shard_map/ppermute | solution.py:23
  299.2 1.7 collective-permute-start.11
  301.1 31.9 %collective-permute-done.14.refs_6_ = bf16[2,896,384]{2,1,0:T(8,128)(2,1)S(1)} collective-permute-done((bf16[2,896,384]{2,1,0:T(8,128)(2,1)S(1)}, bf16[2,896,384]{2,1,0:T(8,128)(2,1)S(1)}, u32[]{:S(2)}, u32[]{:S(2)}) %collective-permute-start.14) | collective-permute-done | bytes 1376288 | tf_op jit(solution)/shard_map/ppermute | solution.py:23
  333.0 0.5 collective-permute-start.15
  333.5 0.5 copy-done.6
  334.1 0.5 copy-done.7
  334.6 0.5 copy-done.8
  335.0 1.1 copy-done.9
  336.2 1.1 copy-done.10
  337.3 8.9 %shard_map.167 = bf16[16,20,1920]{2,1,0:T(8,128)(2,1)} custom-call(s32[2]{0:T(128)} %pad_add_fusion.place_ref, bf16[8,320,512]{2,1,0:T(8,128)(2,1)} %bitcast.65, bf16[2,896,384]{2,1,0:T(8,128)(2,1)} %get-tuple-element.12.refs_2_.refs_0_, bf16[2,896,384]{2,1,0:T(8,128)(2,1)} %copy-done.7, bf16[2,896,384]{2,1,0:T(8,128)(2,1)} %copy-done.4, ...), custom_call_target="tpu_custom_call" | custom-call | tf_op jit(solution)/shard_map/pallas_call | solution.py:105
  346.2 6.5 %all-to-all-start.6 = ((bf16[16,20,1920]{2,1,0:T(8,128)(2,1)}), bf16[16,20,1920]{2,1,0:T(8,128)(2,1)S(1)}, u32[]{:S(2)}, u32[]{:S(2)}) async-start(bf16[16,20,1920]{2,1,0:T(8,128)(2,1)} %shard_map.167), calls=%async_computation.6 | async-start | bytes 2949120 | tf_op jit(solution)/shard_map/all_to_all | solution.py:287
  352.8 9.4 %shard_map.168 = (bf16[7168,128]{1,0:T(8,128)(2,1)}, bf16[7168,128]{1,0:T(8,128)(2,1)}, bf16[128,7168]{1,0:T(8,128)(2,1)}) custom-call(bf16[8,320,896]{2,1,0:T(8,128)(2,1)} %all-gather.10.cloned.1.call-done.rows_ref, bf16[8,320,896]{2,1,0:T(8,128)(2,1)} %all-gather.12.cloned.1.call-done.grads_ref, bf16[320,512]{1,0:T(8,128)(2,1)} %shard_map.166.hidden_ref), custom_call_target="tpu_custom_call" | custom-call | tf_op jit(solution)/shard_map/pallas_call | solution.py:105
  362.2 11.3 %all-to-all-done.6 = bf16[16,20,1920]{2,1,0:T(8,128)(2,1)S(1)} async-done(((bf16[16,20,1920]{2,1,0:T(8,128)(2,1)}), bf16[16,20,1920]{2,1,0:T(8,128)(2,1)S(1)}, u32[]{:S(2)}, u32[]{:S(2)}) %all-to-all-start.6) | async-done | bytes 1228832 | tf_op jit(solution)/shard_map/all_to_all | solution.py:287
  373.5 0.3 reshape.188
  373.8 0.3 fusion.4
  374.1 0.3 convolution_multiply_fusion.2
  374.6 0.9 fusion.14
  375.5 1.0 fusion.3
  (104 shorter events, 3.8 us)
Async XLA Ops:
  7.2 107.8 %all-gather.8.cloned.1.call-start = ((), (), s32[]{:S(2)}) async-start(), calls=%async_computation.7 | async-start | bytes 4456448 | tf_op jit(solution)/shard_map/all_gather | solution.py:327
  8.1 5.0 %collective-permute-start.1 = (bf16[64,512]{1,0:T(8,128)(2,1)S(1)}, bf16[64,512]{1,0:T(8,128)(2,1)S(1)}, u32[]{:S(2)}, u32[]{:S(2)}) collective-permute-start(bf16[64,512]{1,0:T(8,128)(2,1)S(1)} %get-tuple-element.20), channel_id=1, source_target_pairs={{0,8},{1,33},{2,10},{3,35},{4,12},{5,37},{6,14},{7,39},{8,16},{9,4... | collective-permute-start | bytes 196616 | tf_op jit(solution)/shard_map/ppermute | solution.py:40
  10.2 3.1 collective-permute-start
  13.1 4.0 %collective-permute-start.2 = (bf16[32,512]{1,0:T(8,128)(2,1)S(1)}, bf16[32,512]{1,0:T(8,128)(2,1)S(1)}, u32[]{:S(2)}, u32[]{:S(2)}) collective-permute-start(bf16[32,512]{1,0:T(8,128)(2,1)S(1)} %slice.72), channel_id=1, source_target_pairs={{0,8},{1,33},{2,10},{3,35},{4,12},{5,37},{6,14},{7,39},{8,16},{9,4... | collective-permute-start | bytes 98312 | tf_op jit(solution)/shard_map/ppermute | solution.py:40
  13.3 3.8 collective-permute-start.3
  17.1 17.1 %copy-start.14 = (s32[2048]{0:T(1024)S(1)}, s32[2048]{0:T(1024)}, u32[]{:S(2)}) copy-start(s32[2048]{0:T(1024)} %param.15) | copy-start | bytes 24580
  17.2 6.8 %collective-permute-start.5 = (bf16[4,64,512]{2,1,0:T(8,128)(2,1)S(1)}, bf16[4,64,512]{2,1,0:T(8,128)(2,1)S(1)}, u32[]{:S(2)}, u32[]{:S(2)}) collective-permute-start(bf16[4,64,512]{2,1,0:T(8,128)(2,1)S(1)} %pad_maximum_fusion), channel_id=1, source_target_pairs={{0,32},{1,9},{2,34},{3,11},{4,36},{5,13},{6,38},{7,15},{8,40},{9,1... | collective-permute-start | bytes 786440 | tf_op jit(solution)/shard_map/ppermute | solution.py:40
  18.7 5.3 %collective-permute-start.4 = (bf16[4,64,512]{2,1,0:T(8,128)(2,1)S(1)}, bf16[4,64,512]{2,1,0:T(8,128)(2,1)S(1)}, u32[]{:S(2)}, u32[]{:S(2)}) collective-permute-start(bf16[4,64,512]{2,1,0:T(8,128)(2,1)S(1)} %pad_maximum_fusion), channel_id=1, source_target_pairs={{0,96},{1,25},{2,98},{3,27},{4,100},{5,29},{6,102},{7,31},{8,104},... | collective-permute-start | bytes 786440 | tf_op jit(solution)/shard_map/ppermute | solution.py:40
  23.9 5.1 %collective-permute-start.6 = (bf16[2,64,512]{2,1,0:T(8,128)(2,1)S(1)}, bf16[2,64,512]{2,1,0:T(8,128)(2,1)S(1)}, u32[]{:S(2)}, u32[]{:S(2)}) collective-permute-start(bf16[2,64,512]{2,1,0:T(8,128)(2,1)S(1)} %slice.74), channel_id=1, source_target_pairs={{0,32},{1,9},{2,34},{3,11},{4,36},{5,13},{6,38},{7,15},{8,40},{9,1... | collective-permute-start | bytes 393224 | tf_op jit(solution)/shard_map/ppermute | solution.py:40
  24.1 5.0 %collective-permute-start.7 = (bf16[2,64,512]{2,1,0:T(8,128)(2,1)S(1)}, bf16[2,64,512]{2,1,0:T(8,128)(2,1)S(1)}, u32[]{:S(2)}, u32[]{:S(2)}) collective-permute-start(bf16[2,64,512]{2,1,0:T(8,128)(2,1)S(1)} %slice.75), channel_id=1, source_target_pairs={{0,96},{1,25},{2,98},{3,27},{4,100},{5,29},{6,102},{7,31},{8,104},... | collective-permute-start | bytes 393224 | tf_op jit(solution)/shard_map/ppermute | solution.py:40
  29.1 7.5 %copy-start.11 = (bf16[16,64,512]{2,1,0:T(8,128)(2,1)}, bf16[16,64,512]{2,1,0:T(8,128)(2,1)S(1)}, u32[]{:S(2)}) copy-start(bf16[16,64,512]{2,1,0:T(8,128)(2,1)S(1)} %constant_dynamic-update-slice_fusion) | copy-start | bytes 3145732
  29.1 7.5 %collective-permute-start.8 = (bf16[1024,512]{1,0:T(8,128)(2,1)S(1)}, bf16[1024,512]{1,0:T(8,128)(2,1)S(1)}, u32[]{:S(2)}, u32[]{:S(2)}) collective-permute-start(bf16[1024,512]{1,0:T(8,128)(2,1)S(1)} %bitcast.69), channel_id=1, source_target_pairs={{0,1},{1,0},{2,3},{3,2},{4,5},{5,4},{6,7},{7,6},{8,9},{9,8},{10,11... | collective-permute-start | bytes 3145736 | tf_op jit(solution)/shard_map/ppermute | solution.py:27
  36.6 1.0 copy-start.12
  47.5 14.2 %copy-start.15 = (s32[128,2]{0,1:T(2,128)S(1)}, s32[128,2]{0,1:T(2,128)}, u32[]{:S(2)}) copy-start(s32[128,2]{0,1:T(2,128)} %param.20) | copy-start | bytes 3076
  59.9 2.5 copy-start.16
  59.9 2.8 copy-start.13
  60.9 101.5 %all-gather.14.cloned.1.call-start = ((), (), s32[]{:S(2)}) async-start(), calls=%async_computation.10 | async-start | bytes 8257536 | tf_op jit(solution)/shard_map/all_gather | solution.py:59
  61.7 156.0 %all-gather.12.cloned.1.call-start = ((), (), s32[]{:S(2)}) async-start(), calls=%async_computation.9 | async-start | bytes 5160960 | tf_op jit(solution)/shard_map/all_gather | solution.py:59
  85.4 13.4 %all-to-all-start = ((bf16[8,16,896]{2,1,0:T(8,128)(2,1)}), bf16[8,16,896]{2,1,0:T(8,128)(2,1)S(1)}, u32[]{:S(2)}, u32[]{:S(2)}) async-start(bf16[8,16,896]{2,1,0:T(8,128)(2,1)} %bitcast), calls=%async_computation | async-start | bytes 458752 | tf_op jit(solution)/shard_map/all_to_all | solution.py:265
  98.8 63.6 %copy-start.2 = (bf16[8,16,896]{2,1,0:T(8,128)(2,1)}, bf16[8,16,896]{2,1,0:T(8,128)(2,1)S(1)}, u32[]{:S(2)}) copy-start(bf16[8,16,896]{2,1,0:T(8,128)(2,1)S(1)} %all-to-all-done.refs_0_) | copy-start | bytes 688132
  169.9 14.2 %all-to-all-start.3 = ((bf16[16,16,448]{2,1,0:T(8,128)(2,1)}), bf16[16,16,448]{2,1,0:T(8,128)(2,1)S(1)}, u32[]{:S(2)}, u32[]{:S(2)}) async-start(bf16[16,16,448]{2,1,0:T(8,128)(2,1)} %shard_map.165), calls=%async_computation.3 | async-start | bytes 524288 | tf_op jit(solution)/shard_map/all_to_all | solution.py:287
  176.5 8.1 %copy-start.3 = (bf16[8,16,896]{2,1,0:T(8,128)(2,1)S(1)}, bf16[8,16,896]{2,1,0:T(8,128)(2,1)}, u32[]{:S(2)}) copy-start(bf16[8,16,896]{2,1,0:T(8,128)(2,1)} %copy-done.2) | copy-start | bytes 688132
  186.0 13.2 %all-to-all-start.4 = ((bf16[8,16,1024]{2,1,0:T(8,128)(2,1)}), bf16[8,16,1024]{2,1,0:T(8,128)(2,1)S(1)}, u32[]{:S(2)}, u32[]{:S(2)}) async-start(bf16[8,16,1024]{2,1,0:T(8,128)(2,1)} %pad_maximum_fusion.1), calls=%async_computation.4 | async-start | bytes 524288 | tf_op jit(solution)/shard_map/all_to_all | solution.py:345
  191.1 58.6 %all-gather.10.cloned.1.call-start = ((), (), s32[]{:S(2)}) async-start(), calls=%async_computation.8 | async-start | bytes 5160960 | tf_op jit(solution)/shard_map/all_gather | solution.py:59
  217.5 43.0 %copy-start.1 = (bf16[2,896,384]{2,1,0:T(8,128)(2,1)S(1)}, bf16[2,896,384]{2,1,0:T(8,128)(2,1)}, u32[]{:S(2)}) copy-start(bf16[2,896,384]{2,1,0:T(8,128)(2,1)} %get-tuple-element.13.refs_3_.refs_1_) | copy-start | bytes 4128772
  217.6 43.4 %copy-start = (bf16[2,896,384]{2,1,0:T(8,128)(2,1)S(1)}, bf16[2,896,384]{2,1,0:T(8,128)(2,1)}, u32[]{:S(2)}) copy-start(bf16[2,896,384]{2,1,0:T(8,128)(2,1)} %get-tuple-element.12.refs_2_.refs_0_) | copy-start | bytes 4128772
  217.6 118.7 %all-gather.16.cloned.1.call-start = ((), (), s32[]{:S(2)}) async-start(), calls=%async_computation.11 | async-start | bytes 2949120 | tf_op jit(solution)/shard_map/all_gather | solution.py:59
  258.6 40.6 %collective-permute-start.10 = (bf16[2,896,384]{2,1,0:T(8,128)(2,1)}, bf16[2,896,384]{2,1,0:T(8,128)(2,1)S(1)}, u32[]{:S(2)}, u32[]{:S(2)}) collective-permute-start(bf16[2,896,384]{2,1,0:T(8,128)(2,1)} %get-tuple-element.15.refs_5_.refs_3_), channel_id=1, source_target_pairs={{0,6},{1,7},{2,0},{3,1},{4,2},{5,3},{6,4},{7,5},{8,14},{9,15},{10,... | collective-permute-start | bytes 4128776 | tf_op jit(solution)/shard_map/ppermute | solution.py:23
  259.1 41.8 %collective-permute-start.12 = (bf16[2,896,384]{2,1,0:T(8,128)(2,1)}, bf16[2,896,384]{2,1,0:T(8,128)(2,1)S(1)}, u32[]{:S(2)}, u32[]{:S(2)}) collective-permute-start(bf16[2,896,384]{2,1,0:T(8,128)(2,1)} %get-tuple-element.14.refs_4_.refs_2_), channel_id=1, source_target_pairs={{0,4},{1,5},{2,6},{3,7},{4,0},{5,1},{6,2},{7,3},{8,12},{9,13},{10,... | collective-permute-start | bytes 4128776 | tf_op jit(solution)/shard_map/ppermute | solution.py:23
  260.6 72.4 %collective-permute-start.14 = (bf16[2,896,384]{2,1,0:T(8,128)(2,1)S(1)}, bf16[2,896,384]{2,1,0:T(8,128)(2,1)S(1)}, u32[]{:S(2)}, u32[]{:S(2)}) collective-permute-start(bf16[2,896,384]{2,1,0:T(8,128)(2,1)S(1)} %copy-done.1), channel_id=1, source_target_pairs={{0,2},{1,3},{2,4},{3,5},{4,6},{5,7},{6,0},{7,1},{8,10},{9,11},{10,... | collective-permute-start | bytes 4128776 | tf_op jit(solution)/shard_map/ppermute | solution.py:23
  260.9 72.5 %collective-permute-start.9 = (bf16[2,896,384]{2,1,0:T(8,128)(2,1)S(1)}, bf16[2,896,384]{2,1,0:T(8,128)(2,1)S(1)}, u32[]{:S(2)}, u32[]{:S(2)}) collective-permute-start(bf16[2,896,384]{2,1,0:T(8,128)(2,1)S(1)} %copy-done), channel_id=1, source_target_pairs={{0,1},{1,0},{2,3},{3,2},{4,5},{5,4},{6,7},{7,6},{8,9},{9,8},{10,11... | collective-permute-start | bytes 4128776 | tf_op jit(solution)/shard_map/ppermute | solution.py:27
  299.2 34.3 %copy-start.4 = (bf16[2,896,384]{2,1,0:T(8,128)(2,1)}, bf16[2,896,384]{2,1,0:T(8,128)(2,1)S(1)}, u32[]{:S(2)}) copy-start(bf16[2,896,384]{2,1,0:T(8,128)(2,1)S(1)} %collective-permute-done.10.refs_2_) | copy-start | bytes 4128772
  299.2 34.3 %collective-permute-start.11 = (bf16[2,896,384]{2,1,0:T(8,128)(2,1)S(1)}, bf16[2,896,384]{2,1,0:T(8,128)(2,1)S(1)}, u32[]{:S(2)}, u32[]{:S(2)}) collective-permute-start(bf16[2,896,384]{2,1,0:T(8,128)(2,1)S(1)} %collective-permute-done.10.refs_2_), channel_id=1, source_target_pairs={{0,1},{1,0},{2,3},{3,2},{4,5},{5,4},{6,7},{7,6},{8,9},{9,8},{10,11... | collective-permute-start | bytes 4128776 | tf_op jit(solution)/shard_map/ppermute | solution.py:27
  301.0 32.5 %copy-start.5 = (bf16[2,896,384]{2,1,0:T(8,128)(2,1)}, bf16[2,896,384]{2,1,0:T(8,128)(2,1)S(1)}, u32[]{:S(2)}) copy-start(bf16[2,896,384]{2,1,0:T(8,128)(2,1)S(1)} %collective-permute-done.12.refs_4_) | copy-start | bytes 4128772
  301.0 32.5 %collective-permute-start.13 = (bf16[2,896,384]{2,1,0:T(8,128)(2,1)S(1)}, bf16[2,896,384]{2,1,0:T(8,128)(2,1)S(1)}, u32[]{:S(2)}, u32[]{:S(2)}) collective-permute-start(bf16[2,896,384]{2,1,0:T(8,128)(2,1)S(1)} %collective-permute-done.12.refs_4_), channel_id=1, source_target_pairs={{0,1},{1,0},{2,3},{3,2},{4,5},{5,4},{6,7},{7,6},{8,9},{9,8},{10,11... | collective-permute-start | bytes 4128776 | tf_op jit(solution)/shard_map/ppermute | solution.py:27
  333.0 1.1 copy-start.6
  333.0 3.2 collective-permute-start.15
  333.5 1.1 copy-start.7
  333.5 1.5 copy-start.8
  335.0 1.1 copy-start.9
  336.2 1.1 copy-start.10
  346.2 27.2 %all-to-all-start.6 = ((bf16[16,20,1920]{2,1,0:T(8,128)(2,1)}), bf16[16,20,1920]{2,1,0:T(8,128)(2,1)S(1)}, u32[]{:S(2)}, u32[]{:S(2)}) async-start(bf16[16,20,1920]{2,1,0:T(8,128)(2,1)} %shard_map.167), calls=%async_computation.6 | async-start | bytes 2949120 | tf_op jit(solution)/shard_map/all_to_all | solution.py:287
Sparse Core Ops, SparseCore 0:
  61.0 53.8 all-gather.7
  116.7 45.7 all-gather.13
  164.2 35.4 all-gather.11
  217.7 32.0 all-gather.9
  258.7 76.9 all-gather.15
where the time goes:
time: 386 us; the launch traced here: 383 us
  waiting for transfers between devices  201 us (52%)
  blocking collectives  50.5 us (13%)
  Pallas kernels  50.2 us (13%)
  starting transfers between devices  47.6 us (12%)
  between operations  14.2 us (4%)
  local copies, waits for them, and re-layouts  13.2 us (3%)
  other arithmetic  3.97 us (1%)
    all_gather x4, waiting for transfers between devices, group_gather(): return lax.all_gather(block, GROUP, axis=0)  79.6 us
    ppermute x3, waiting for transfers between devices, shift_z(): lax.ppermute(block, GROUP, [(g, (g + 2 * step) % 8) for g in range(8)])  69.1 us
    pallas_call x5, Pallas kernels, run(): pl.pallas_call(kernel, out_shape=outs, in_specs=[pl.BlockSpec(memory_spac...  40.2 us
    all_to_all x2, blocking collectives, to_experts(): return lax.all_to_all(rows, 'ctx', split_axis=0, concat_axis=0, tiled=True)  38.1 us
    all_to_all x2, waiting for transfers between devices, to_experts(): return lax.all_to_all(rows, 'ctx', split_axis=0, concat_axis=0, tiled=True)  18.9 us
    all_gather x1, waiting for transfers between devices, per_device(): all_heads = lax.all_gather(head_part, 'ctx', axis=0)  16.1 us
    all_to_all x2, starting transfers between devices, to_experts(): return lax.all_to_all(rows, 'ctx', split_axis=0, concat_axis=0, tiled=True)  13.1 us
    all_to_all x1, blocking collectives, per_device(): head_part = lax.all_to_all(head_out, GROUP, 0, 0, tiled=True)  12.4 us
  transfers between devices with their start and end apart: 25, of which 14 were waited for; matrix products, arithmetic and copies ran while one was open for 2% of the time, Pallas kernels for 6%

commit v1 on v0

--- a/solution.py
+++ b/solution.py
@@ -98,10 +98,11 @@
     return wide.astype(BF16)
 
 
-def call(kernel, outs, scalars=0, unread=0, **params):
+def call(kernel, outs, scalars=0, whole=None, **params):
     def run(*operands):
-        whole = len(operands) - scalars - unread
-        spaces = [pltpu.SMEM] * scalars + [pltpu.VMEM] * whole + [pl.ANY] * unread
+        count = len(operands) - scalars if whole is None else whole
+        left = len(operands) - scalars - count
+        spaces = [pltpu.SMEM] * scalars + [pltpu.VMEM] * count + [pl.ANY] * left
         return pl.pallas_call(
             kernel,
             out_shape=outs,
@@ -112,20 +113,44 @@
     return run
 
 
+def buffers(*shapes):
+    return [pltpu.VMEM(shape, BF16) for shape in shapes] + [
+        pltpu.SemaphoreType.DMA((len(shapes), shapes[0][0]))
+    ]
+
+
+def start_copies(lists, bufs, sems):
+    copies = [
+        [
+            pltpu.make_async_copy(source, buf.at[place], sems.at[n, place])
+            for place, source in enumerate(sources)
+        ]
+        for n, (sources, buf) in enumerate(zip(lists, bufs))
+    ]
+    for group in zip(*copies):
+        for copy in group:
+            copy.start()
+    return copies
+
+
 def member(place_ref, step, other):
     z = lax.rem(place_ref[0] + step, SIDE)
     return 2 * z + place_ref[1] + other - 2 * place_ref[1] * other
 
 
-def prepare_kernel(place_ref, down_ref, gate_ref, up_ref, *outs):
-    slice_width = outs[0].shape[1]
+def prepare_kernel(place_ref, down_ref, gate_ref, up_ref, all_ref, *outs):
+    slice_width = all_ref.shape[1]
     hidden = down_ref.shape[0]
-    for step in range(SIDE):
-        for other in range(2):
-            start = pl.multiple_of(member(place_ref, step, other) * slice_width, LANES)
-            outs[step][other, :, :hidden] = gate_ref[pl.ds(start, slice_width), :]
-            outs[step][other, :, hidden : 2 * hidden] = up_ref[pl.ds(start, slice_width), :]
-            outs[step][other, :, 2 * hidden :] = down_ref[:, pl.ds(start, slice_width)].T
+    for place in range(8):
+        step, other = place // 2, place % 2
+        start = pl.multiple_of(member(place_ref, step, other) * slice_width, LANES)
+        gate = gate_ref[pl.ds(start, slice_width), :]
+        up = up_ref[pl.ds(start, slice_width), :]
+        down = down_ref[:, pl.ds(start, slice_width)].T
+        for at, ref in ((place, all_ref), (other, outs[step])):
+            ref[at, :, :hidden] = gate
+            ref[at, :, hidden : 2 * hidden] = up
+            ref[at, :, 2 * hidden :] = down
 
 
 def attend_kernel(scale, q_ref, near_ref, far_ref, key_frame_ref, own_frame_ref, uv_ref, out_ref):
@@ -154,25 +179,44 @@
 
 
 def out_proj_kernel(rows_ref, weight_ref, *refs):
-    out_ref = refs[-1]
+    out_ref, row_buf, weight_buf, sems = refs[-4:]
     members, columns, depth = weight_ref.shape
+    copies = start_copies(
+        [
+            [rows_ref.at[:, :, pl.ds(p * depth, depth)] for p in range(members)],
+            [weight_ref.at[p] for p in range(members)],
+        ],
+        [row_buf, weight_buf],
+        sems,
+    )
     total = jnp.zeros((rows_ref.shape[0] * rows_ref.shape[1], columns), F32)
     for place in range(members):
-        rows = rows_ref[:, :, place * depth : (place + 1) * depth]
-        rows = rows.reshape(total.shape[0], depth)
-        total = total + dot(rows, weight_ref[place], ((1,), (1,)))
+        for copy in copies:
+            copy[place].wait()
+        rows = row_buf[place].reshape(total.shape[0], depth)
+        total = total + dot(rows, weight_buf[place], ((1,), (1,)))
     out_ref[...] = total.astype(BF16).reshape(out_ref.shape)
 
 
-def expert_kernel(place_ref, rows_ref, grads_ref, *refs):
-    weight_refs, out_ref = refs[:4], refs[4]
-    hidden = weight_refs[0].shape[2] // 3
+def expert_kernel(place_ref, rows_ref, grads_ref, weight_ref, out_ref, *scratch):
+    row_buf, grad_buf, weight_buf, sems = scratch
+    sources = [member(place_ref, p // 2, p % 2) for p in range(8)]
+    copies = start_copies(
+        [
+            [grads_ref.at[source] for source in sources],
+            [rows_ref.at[source] for source in sources],
+            [weight_ref.at[p] for p in range(8)],
+        ],
+        [grad_buf, row_buf, weight_buf],
+        sems,
+    )
+    hidden = weight_ref.shape[2] // 3
     both, hidden_grad = 0.0, 0.0
     for place in range(8):
-        weight_ref, other = weight_refs[place // 2], place % 2
-        source = member(place_ref, place // 2, other)
-        both = both + dot(rows_ref[source], weight_ref[other, :, : 2 * hidden])
-        hidden_grad = hidden_grad + dot(grads_ref[source], weight_ref[other, :, 2 * hidden :])
+        for copy in copies:
+            copy[place].wait()
+        both = both + dot(row_buf[place], weight_buf[place, :, : 2 * hidden])
+        hidden_grad = hidden_grad + dot(grad_buf[place], weight_buf[place, :, 2 * hidden :])
     gate_in, up_in = both[:, :hidden], both[:, hidden:]
     gate_sig = 1.0 / (1.0 + jnp.exp(-gate_in))
     silu = gate_in * gate_sig
@@ -199,14 +243,23 @@
 
 
 def project_kernel(place_ref, hidden_ref, *refs):
-    weight_refs, out_ref = refs[:8], refs[8]
+    weight_refs, out_ref, unit_buf, weight_buf, sems = refs[:8], *refs[8:]
+    copies = start_copies(
+        [
+            [hidden_ref.at[member(place_ref, p // 2, p % 2)] for p in range(8)],
+            [weight_refs[p].at[p % 2] for p in range(8)],
+        ],
+        [unit_buf, weight_buf],
+        sems,
+    )
     slice_width, wide = weight_refs[0].shape[1:]
     hidden = wide // 3
     rows, grads, center = 0.0, 0.0, 0.0
     for place in range(8):
-        source = member(place_ref, place // 2, place % 2)
-        weight = weight_refs[place][place % 2]
-        units = hidden_ref[source]
+        for copy in copies:
+            copy[place].wait()
+        units = unit_buf[place]
+        weight = weight_buf[place]
         grads = grads + dot(units[:, : 2 * hidden], weight[:, : 2 * hidden], ((1,), (1,)))
         rows = rows + dot(units[:, 2 * hidden : 3 * hidden], weight[:, 2 * hidden :], ((1,), (1,)))
         center = center + jnp.sum(units[:, 3 * hidden :].astype(F32), axis=1, keepdims=True)
@@ -257,10 +310,10 @@
     places = jnp.stack([place_z, core]).astype(jnp.int32)
 
     out_weight = group_gather(w_out.T)
-    weight_blocks = call(
-        prepare_kernel, [shape(2, slice_width, 3 * hidden_width)] * SIDE, 1
+    block = (slice_width, 3 * hidden_width)
+    weight_blocks, *weight_pairs = call(
+        prepare_kernel, [shape(8, *block)] + [shape(2, *block)] * SIDE, 1
     )(places, w_down[0], w_gate[0], w_up[0])
-    slice_weights = group_exchange(weight_blocks)
 
     residual_part = lax.all_to_all(
         residual.reshape(group_count, part_tokens, slice_width), GROUP, 0, 0, tiled=True
@@ -287,8 +340,10 @@
         return lax.all_to_all(rows, "ctx", split_axis=0, concat_axis=0, tiled=True)
 
     grad_rows = (dot(pick, grad_out) * slot_weight[:, None]).astype(BF16)
+    grad_rows, *weight_pairs = lax.optimization_barrier((grad_rows, *weight_pairs))
     grad_rows = to_experts(grad_rows)
     out_grad = group_gather(grad_rows)
+    slice_weights = group_exchange(weight_pairs)
 
     half = token_count // 2
     own_keys = ctx_gather(lax.dynamic_slice_in_dim(latent, core * half, half, 0))
@@ -326,8 +381,14 @@
     head_part = jnp.transpose(head_part, (1, 0, 2)).reshape(part_tokens, -1)
     all_heads = lax.all_gather(head_part, "ctx", axis=0)
     columns = call(
-        out_proj_kernel, shape(ctx_count, part_tokens, column_width), unread=2 + SIDE
-    )(all_heads, out_weight, residual_part, grad_rows, *weight_blocks)
+        out_proj_kernel,
+        shape(ctx_count, part_tokens, column_width),
+        whole=0,
+        scratch_shapes=buffers(
+            (group_count, ctx_count, part_tokens, head_count * value_width),
+            (group_count, column_width, head_count * value_width),
+        ),
+    )(all_heads, out_weight, residual_part, grad_rows, weight_blocks)
     residual_part = jnp.transpose(residual_part, (1, 0, 2)).reshape(part_tokens, model_width)
     columns = to_experts(columns)
     attn_part = jnp.transpose(columns, (1, 0, 2)).reshape(part_tokens, model_width)
@@ -350,9 +411,13 @@
     normed = (unit_rows * local_gain).astype(BF16)
 
     expert_rows = group_gather(to_experts(dot(pick, normed).astype(BF16)))
-    hidden_send = call(expert_kernel, shape(slot_total, 3 * hidden_width + LANES), 1)(
-        places, expert_rows, out_grad, *weight_blocks
-    )
+    hidden_send = call(
+        expert_kernel,
+        shape(slot_total, 3 * hidden_width + LANES),
+        1,
+        0,
+        scratch_shapes=buffers(*[(8, slot_total, slice_width)] * 2, (8, *block)),
+    )(places, expert_rows, out_grad, weight_blocks)
     hidden_all = group_gather(hidden_send)
     grad_gate, grad_up, grad_down = call(
         weight_grad_kernel,
@@ -360,7 +425,11 @@
     )(expert_rows, out_grad, hidden_send)
     grad_gate, grad_up, grad_down = grad_gate[None], grad_up[None], grad_down[None]
     back = call(
-        project_kernel, shape(ctx_count, capacity, 2 * slice_width + LANES), 1
+        project_kernel,
+        shape(ctx_count, capacity, 2 * slice_width + LANES),
+        1,
+        0,
+        scratch_shapes=buffers((8, slot_total, 3 * hidden_width + LANES), (8, *block)),
     )(places, hidden_all, *slice_weights)
     back = to_experts(back).reshape(slot_total, 2 * slice_width + LANES)
 

time: 386 us -> 382 us (0.990)
  waiting for transfers between devices: 201 us -> 206 us
    all_to_all x1, waiting for transfers between devices: 0.01 us -> 5.32 us  [per_device(): lax.all_to_all(residual.reshape(group_count, part_tokens, slice_width), G...]
  transfers between devices with their start and end apart: 25 -> 25, of which waited for: 14 -> 15; matrix products, arithmetic and copies ran while one was open for 2% -> 2% of each run, Pallas kernels for 6% -> 6%
where the time goes in v1:
time: 382 us; the launch traced here: 380 us
  waiting for transfers between devices  206 us (54%)
  Pallas kernels  47.5 us (12%)
  blocking collectives  47 us (12%)
  starting transfers between devices  46.7 us (12%)
  between operations  14.2 us (4%)
  local copies, waits for them, and re-layouts  12.1 us (3%)
  other arithmetic  3.98 us (1%)
    all_gather x4, waiting for transfers between devices, group_gather(): return lax.all_gather(block, GROUP, axis=0)  79.6 us
    ppermute x3, waiting for transfers between devices, shift_z(): lax.ppermute(block, GROUP, [(g, (g + 2 * step) % 8) for g in range(8)])  69.1 us
    pallas_call x5, Pallas kernels, run(): pl.pallas_call(kernel, out_shape=outs, in_specs=[pl.BlockSpec(memory_spac...  37.5 us
    all_to_all x2, blocking collectives, to_experts(): return lax.all_to_all(rows, 'ctx', split_axis=0, concat_axis=0, tiled=True)  34.7 us
    all_to_all x2, waiting for transfers between devices, to_experts(): return lax.all_to_all(rows, 'ctx', split_axis=0, concat_axis=0, tiled=True)  19 us
    all_gather x1, waiting for transfers between devices, per_device(): all_heads = lax.all_gather(head_part, 'ctx', axis=0)  13.9 us
    all_to_all x2, starting transfers between devices, to_experts(): return lax.all_to_all(rows, 'ctx', split_axis=0, concat_axis=0, tiled=True)  13.1 us
    all_to_all x1, blocking collectives, per_device(): head_part = lax.all_to_all(head_out, GROUP, 0, 0, tiled=True)  12.4 us
  transfers between devices with their start and end apart: 25, of which 15 were waited for; matrix products, arithmetic and copies ran while one was open for 2% of the time, Pallas kernels for 6%

profile of v1, /device:TPU:1, one launch (start us, length us, event | category | flops | bytes accessed | tf_op | source)
XLA Modules:
  0.0 379.9 jit_solution(13132890898834004454)
XLA Ops:
  7.2 0.9 constant_dynamic-update-slice_fusion.7
  8.1 2.1 collective-permute-start.1
  10.2 1.3 collective-permute-start
  11.5 1.6 collective-permute-done.1
  13.3 2.6 collective-permute-start.3
  15.9 1.2 collective-permute-done.2
  17.2 1.6 collective-permute-start.5
  18.7 1.5 collective-permute-start.4
  20.3 3.7 collective-permute-done.5
  24.1 2.7 collective-permute-start.7
  26.8 2.2 collective-permute-done.6
  29.1 5.2 %collective-permute-start.8 = (bf16[1024,512]{1,0:T(8,128)(2,1)S(1)}, bf16[1024,512]{1,0:T(8,128)(2,1)S(1)}, u32[]{:S(2)}, u32[]{:S(2)}) collective-permute-start(bf16[1024,512]{1,0:T(8,128)(2,1)S(1)} %bitcast.69), channel_id=1, source_target_pairs={{0,1},{1,0},{2,3},{3,2},{4,5},{5,4},{6,7},{7,6},{8,9},{9,8},{10,11... | collective-permute-start | bytes 3145736 | tf_op jit(solution)/shard_map/ppermute | solution.py:27
  34.8 0.7 copy.79.own_frame_ref
  35.5 0.6 broadcast_select_fusion.key_frame_ref
  36.1 0.4 collective-permute-done.8.far_ref
  36.6 1.0 copy-done.10
  37.5 10.0 %attend.1 = bf16[128,1024]{1,0:T(8,128)(2,1)} custom-call(bf16[128,4096]{1,0:T(8,128)(2,1)} %q_ref.1, bf16[1024,512]{1,0:T(8,128)(2,1)} %bitcast.70, bf16[1024,512]{1,0:T(8,128)(2,1)} %copy-done.10, s32[1,2048]{1,0:T(1,128)} %broadcast_select_fusion.key_frame_ref, s32[128,1]{1,0:T(8,128)} %copy.79.own_frame_ref, bf16[8,512,128]{2,1,0:T(8,128)(2,1)} %uv_ref.1), custom_call_target="tpu_custom_call" | custom-call | tf_op jit(solution)/shard_map/attend/pallas_call | solution.py:363
  47.5 12.4 %all_to_all.45 = bf16[8,16,1024]{2,1,0:T(8,128)(2,1)S(1)} all-to-all(bf16[8,16,1024]{2,1,0:T(8,128)(2,1)} %bitcast.71), channel_id=1, replica_groups=mesh['ctx'=16,'role'=2,'exp'=4] {'role','exp'}, dimensions={0} | all-to-all | bytes 524288 | tf_op jit(solution)/shard_map/all_to_all | solution.py:380
  60.1 0.8 all_gather_reshape.3
  61.0 0.7 all-gather.14.cloned.1.call-update
  62.7 0.6 pad_add_fusion.place_ref
  63.3 7.7 %shard_map.164 = (bf16[8,896,384]{2,1,0:T(8,128)(2,1)}, bf16[2,896,384]{2,1,0:T(8,128)(2,1)}, bf16[2,896,384]{2,1,0:T(8,128)(2,1)}, bf16[2,896,384]{2,1,0:T(8,128)(2,1)}, bf16[2,896,384]{2,1,0:T(8,128)(2,1)}) custom-call(s32[2]{0:T(128)} %pad_add_fusion.place_ref, bf16[128,7168]{1,0:T(8,128)(2,1)} %bitcast.66, bf16[7168,128]{1,0:T(8,128)(2,1)} %bitcast.67, ...), custom_call_target="tpu_custom_call" | custom-call | tf_op jit(solution)/shard_map/pallas_call | solution.py:106
  71.0 0.3 fusion
  71.4 19.5 %all_to_all.46 = bf16[16,20,896]{2,1,0:T(8,128)(2,1)S(1)} all-to-all(bf16[16,20,896]{2,1,0:T(8,128)(2,1)S(1)} %all_to_all.30), channel_id=1, replica_groups=mesh['ctx'=16,'role'=2,'exp'=4] {'ctx'}, dimensions={0} | all-to-all | bytes 1146880 | tf_op jit(solution)/shard_map/all_to_all | solution.py:340
  90.9 0.9 all_gather.32
  91.9 5.3 %all-to-all-start = ((bf16[8,16,896]{2,1,0:T(8,128)(2,1)}), bf16[8,16,896]{2,1,0:T(8,128)(2,1)S(1)}, u32[]{:S(2)}, u32[]{:S(2)}) async-start(bf16[8,16,896]{2,1,0:T(8,128)(2,1)} %bitcast), calls=%async_computation | async-start | bytes 458752 | tf_op jit(solution)/shard_map/all_to_all | solution.py:318
  97.2 0.9 all_to_all.32.refs_1_
  98.1 5.3 %all-to-all-done.refs_0_ = bf16[8,16,896]{2,1,0:T(8,128)(2,1)S(1)} async-done(((bf16[8,16,896]{2,1,0:T(8,128)(2,1)}), bf16[8,16,896]{2,1,0:T(8,128)(2,1)S(1)}, u32[]{:S(2)}, u32[]{:S(2)}) %all-to-all-start) | async-done | bytes 229408 | tf_op jit(solution)/shard_map/all_to_all | solution.py:318
  103.4 13.9 %all-gather.8.cloned.1.call-done.rows_ref = bf16[16,16,8192]{2,1,0:T(8,128)(2,1)} async-done(((bf16[1,16,8192]{2,1,0:T(8,128)(2,1)}), bf16[16,16,8192]{2,1,0:T(8,128)(2,1)}) %all-gather.8.cloned.1.call-update) | async-done | bytes 4194320 | tf_op jit(solution)/shard_map/all_gather | solution.py:382
  117.3 47.5 %all-gather.14.cloned.1.call-done = bf16[3584,1024]{1,0:T(8,128)(2,1)} async-done(((bf16[448,1024]{1,0:T(8,128)(2,1)}), bf16[3584,1024]{1,0:T(8,128)(2,1)}) %all-gather.14.cloned.1.call-update) | async-done | bytes 7340048 | tf_op jit(solution)/shard_map/all_gather | solution.py:59
  164.8 5.6 %shard_map.165 = bf16[16,16,448]{2,1,0:T(8,128)(2,1)} custom-call(bf16[16,16,8192]{2,1,0:T(8,128)(2,1)} %all-gather.8.cloned.1.call-done.rows_ref, bf16[8,448,1024]{2,1,0:T(8,128)(2,1)} %bitcast.60, bf16[8,16,896]{2,1,0:T(8,128)(2,1)} %copy-done, bf16[320,896]{1,0:T(8,128)(2,1)} %all_to_all.32.refs_1_, bf16[8,896,384]{2,1,0:T(8,128)(2,1)} %get-tuple-element.23.refs_2_.weight_ref), custom_call_target="tpu_custom_call" | custom-call | tf_op jit(solution)/shard_map/pallas_call | solution.py:106
  170.4 6.5 %all-to-all-start.3 = ((bf16[16,16,448]{2,1,0:T(8,128)(2,1)}), bf16[16,16,448]{2,1,0:T(8,128)(2,1)S(1)}, u32[]{:S(2)}, u32[]{:S(2)}) async-start(bf16[16,16,448]{2,1,0:T(8,128)(2,1)} %shard_map.165), calls=%async_computation.3 | async-start | bytes 524288 | tf_op jit(solution)/shard_map/all_to_all | solution.py:340
  177.1 7.6 %all-to-all-done.3 = bf16[16,16,448]{2,1,0:T(8,128)(2,1)S(1)} async-done(((bf16[16,16,448]{2,1,0:T(8,128)(2,1)}), bf16[16,16,448]{2,1,0:T(8,128)(2,1)S(1)}, u32[]{:S(2)}, u32[]{:S(2)}) %all-to-all-start.3) | async-done | bytes 229408 | tf_op jit(solution)/shard_map/all_to_all | solution.py:340
  184.7 0.3 copy.83
  185.8 0.8 pad_maximum_fusion.1
  186.5 5.1 %all-to-all-start.4 = ((bf16[8,16,1024]{2,1,0:T(8,128)(2,1)}), bf16[8,16,1024]{2,1,0:T(8,128)(2,1)S(1)}, u32[]{:S(2)}, u32[]{:S(2)}) async-start(bf16[8,16,1024]{2,1,0:T(8,128)(2,1)} %pad_maximum_fusion.1), calls=%async_computation.4 | async-start | bytes 524288 | tf_op jit(solution)/shard_map/all_to_all | solution.py:406
  191.6 0.8 dynamic_slice.19
  192.4 8.9 %all-to-all-done.4 = bf16[8,16,1024]{2,1,0:T(8,128)(2,1)S(1)} async-done(((bf16[8,16,1024]{2,1,0:T(8,128)(2,1)}), bf16[8,16,1024]{2,1,0:T(8,128)(2,1)S(1)}, u32[]{:S(2)}, u32[]{:S(2)}) %all-to-all-start.4) | async-done | bytes 262176 | tf_op jit(solution)/shard_map/all_to_all | solution.py:406
  201.5 0.4 convolution_convert_fusion
  202.0 15.1 %all_to_all.47 = bf16[16,20,896]{2,1,0:T(8,128)(2,1)S(1)} all-to-all(bf16[16,20,896]{2,1,0:T(8,128)(2,1)S(1)} %all_to_all.35), channel_id=1, replica_groups=mesh['ctx'=16,'role'=2,'exp'=4] {'ctx'}, dimensions={0} | all-to-all | bytes 1146880 | tf_op jit(solution)/shard_map/all_to_all | solution.py:340
  217.1 1.0 all_gather.30
  218.2 32.1 %all-gather.10.cloned.1.call-done.rows_ref = bf16[8,320,896]{2,1,0:T(8,128)(2,1)} async-done(((bf16[1,320,896]{2,1,0:T(8,128)(2,1)}), bf16[8,320,896]{2,1,0:T(8,128)(2,1)}) %all-gather.10.cloned.1.call-update) | async-done | bytes 4587536 | tf_op jit(solution)/shard_map/all_gather | solution.py:59
  250.3 7.5 %shard_map.166.hidden_ref = bf16[320,512]{1,0:T(8,128)(2,1)} custom-call(s32[2]{0:T(128)} %pad_add_fusion.place_ref, bf16[8,320,896]{2,1,0:T(8,128)(2,1)} %all-gather.10.cloned.1.call-done.rows_ref, bf16[8,320,896]{2,1,0:T(8,128)(2,1)} %all-gather.12.cloned.1.call-done.grads_ref, bf16[8,896,384]{2,1,0:T(8,128)(2,1)} %get-tuple-element.23.refs_2_.weight_ref), custom_call_target="tpu_custom_call" | custom-call | tf_op jit(solution)/shard_map/pallas_call | solution.py:106
  257.8 0.6 collective-permute-start.10
  258.4 1.4 collective-permute-start.12
  259.8 0.4 collective-permute-start.14
  260.2 1.1 collective-permute-start.9
  261.3 37.2 %collective-permute-done.10.refs_2_ = bf16[2,896,384]{2,1,0:T(8,128)(2,1)S(1)} collective-permute-done((bf16[2,896,384]{2,1,0:T(8,128)(2,1)}, bf16[2,896,384]{2,1,0:T(8,128)(2,1)S(1)}, u32[]{:S(2)}, u32[]{:S(2)}) %collective-permute-start.10) | collective-permute-done | bytes 1376288 | tf_op jit(solution)/shard_map/ppermute | solution.py:23
  298.4 1.7 collective-permute-start.11
  300.3 31.9 %collective-permute-done.14.refs_6_ = bf16[2,896,384]{2,1,0:T(8,128)(2,1)S(1)} collective-permute-done((bf16[2,896,384]{2,1,0:T(8,128)(2,1)S(1)}, bf16[2,896,384]{2,1,0:T(8,128)(2,1)S(1)}, u32[]{:S(2)}, u32[]{:S(2)}) %collective-permute-start.14) | collective-permute-done | bytes 1376288 | tf_op jit(solution)/shard_map/ppermute | solution.py:23
  332.2 0.5 collective-permute-start.15
  332.7 0.6 copy-done.5
  333.3 0.5 copy-done.6
  333.8 0.5 copy-done.7
  334.2 1.2 copy-done.8
  335.6 7.3 %shard_map.167 = bf16[16,20,1920]{2,1,0:T(8,128)(2,1)} custom-call(s32[2]{0:T(128)} %pad_add_fusion.place_ref, bf16[8,320,512]{2,1,0:T(8,128)(2,1)} %bitcast.65, bf16[2,896,384]{2,1,0:T(8,128)(2,1)} %get-tuple-element.24.refs_0_, bf16[2,896,384]{2,1,0:T(8,128)(2,1)} %copy-done.6, bf16[2,896,384]{2,1,0:T(8,128)(2,1)} %copy-done.3, ...), custom_call_target="tpu_custom_call" | custom-call | tf_op jit(solution)/shard_map/pallas_call | solution.py:106
  342.9 6.6 %all-to-all-start.6 = ((bf16[16,20,1920]{2,1,0:T(8,128)(2,1)}), bf16[16,20,1920]{2,1,0:T(8,128)(2,1)S(1)}, u32[]{:S(2)}, u32[]{:S(2)}) async-start(bf16[16,20,1920]{2,1,0:T(8,128)(2,1)} %shard_map.167), calls=%async_computation.6 | async-start | bytes 2949120 | tf_op jit(solution)/shard_map/all_to_all | solution.py:340
  349.5 9.4 %shard_map.168 = (bf16[7168,128]{1,0:T(8,128)(2,1)}, bf16[7168,128]{1,0:T(8,128)(2,1)}, bf16[128,7168]{1,0:T(8,128)(2,1)}) custom-call(bf16[8,320,896]{2,1,0:T(8,128)(2,1)} %all-gather.10.cloned.1.call-done.rows_ref, bf16[8,320,896]{2,1,0:T(8,128)(2,1)} %all-gather.12.cloned.1.call-done.grads_ref, bf16[320,512]{1,0:T(8,128)(2,1)} %shard_map.166.hidden_ref), custom_call_target="tpu_custom_call" | custom-call | tf_op jit(solution)/shard_map/pallas_call | solution.py:106
  358.9 11.4 %all-to-all-done.6 = bf16[16,20,1920]{2,1,0:T(8,128)(2,1)S(1)} async-done(((bf16[16,20,1920]{2,1,0:T(8,128)(2,1)}), bf16[16,20,1920]{2,1,0:T(8,128)(2,1)S(1)}, u32[]{:S(2)}, u32[]{:S(2)}) %all-to-all-start.6) | async-done | bytes 1228832 | tf_op jit(solution)/shard_map/all_to_all | solution.py:340
  370.3 0.3 reshape.188
  370.6 0.3 fusion.4
  370.9 0.4 convolution_multiply_fusion.2
  371.4 0.9 fusion.14
  372.3 1.0 fusion.3
  (102 shorter events, 3.8 us)
Async XLA Ops:
  7.2 110.2 %all-gather.8.cloned.1.call-start = ((), (), s32[]{:S(2)}) async-start(), calls=%async_computation.7 | async-start | bytes 4456448 | tf_op jit(solution)/shard_map/all_gather | solution.py:382
  8.1 5.0 %collective-permute-start.1 = (bf16[64,512]{1,0:T(8,128)(2,1)S(1)}, bf16[64,512]{1,0:T(8,128)(2,1)S(1)}, u32[]{:S(2)}, u32[]{:S(2)}) collective-permute-start(bf16[64,512]{1,0:T(8,128)(2,1)S(1)} %get-tuple-element.32), channel_id=1, source_target_pairs={{0,8},{1,33},{2,10},{3,35},{4,12},{5,37},{6,14},{7,39},{8,16},{9,4... | collective-permute-start | bytes 196616 | tf_op jit(solution)/shard_map/ppermute | solution.py:40
  10.2 3.1 collective-permute-start
  13.1 4.0 %collective-permute-start.2 = (bf16[32,512]{1,0:T(8,128)(2,1)S(1)}, bf16[32,512]{1,0:T(8,128)(2,1)S(1)}, u32[]{:S(2)}, u32[]{:S(2)}) collective-permute-start(bf16[32,512]{1,0:T(8,128)(2,1)S(1)} %slice.72), channel_id=1, source_target_pairs={{0,8},{1,33},{2,10},{3,35},{4,12},{5,37},{6,14},{7,39},{8,16},{9,4... | collective-permute-start | bytes 98312 | tf_op jit(solution)/shard_map/ppermute | solution.py:40
  13.3 3.8 collective-permute-start.3
  17.1 17.1 %copy-start.12 = (s32[2048]{0:T(1024)S(1)}, s32[2048]{0:T(1024)}, u32[]{:S(2)}) copy-start(s32[2048]{0:T(1024)} %param.15) | copy-start | bytes 24580
  17.2 6.8 %collective-permute-start.5 = (bf16[4,64,512]{2,1,0:T(8,128)(2,1)S(1)}, bf16[4,64,512]{2,1,0:T(8,128)(2,1)S(1)}, u32[]{:S(2)}, u32[]{:S(2)}) collective-permute-start(bf16[4,64,512]{2,1,0:T(8,128)(2,1)S(1)} %pad_maximum_fusion), channel_id=1, source_target_pairs={{0,32},{1,9},{2,34},{3,11},{4,36},{5,13},{6,38},{7,15},{8,40},{9,1... | collective-permute-start | bytes 786440 | tf_op jit(solution)/shard_map/ppermute | solution.py:40
  18.7 5.3 %collective-permute-start.4 = (bf16[4,64,512]{2,1,0:T(8,128)(2,1)S(1)}, bf16[4,64,512]{2,1,0:T(8,128)(2,1)S(1)}, u32[]{:S(2)}, u32[]{:S(2)}) collective-permute-start(bf16[4,64,512]{2,1,0:T(8,128)(2,1)S(1)} %pad_maximum_fusion), channel_id=1, source_target_pairs={{0,96},{1,25},{2,98},{3,27},{4,100},{5,29},{6,102},{7,31},{8,104},... | collective-permute-start | bytes 786440 | tf_op jit(solution)/shard_map/ppermute | solution.py:40
  23.9 5.1 %collective-permute-start.6 = (bf16[2,64,512]{2,1,0:T(8,128)(2,1)S(1)}, bf16[2,64,512]{2,1,0:T(8,128)(2,1)S(1)}, u32[]{:S(2)}, u32[]{:S(2)}) collective-permute-start(bf16[2,64,512]{2,1,0:T(8,128)(2,1)S(1)} %slice.74), channel_id=1, source_target_pairs={{0,32},{1,9},{2,34},{3,11},{4,36},{5,13},{6,38},{7,15},{8,40},{9,1... | collective-permute-start | bytes 393224 | tf_op jit(solution)/shard_map/ppermute | solution.py:40
  24.1 5.0 %collective-permute-start.7 = (bf16[2,64,512]{2,1,0:T(8,128)(2,1)S(1)}, bf16[2,64,512]{2,1,0:T(8,128)(2,1)S(1)}, u32[]{:S(2)}, u32[]{:S(2)}) collective-permute-start(bf16[2,64,512]{2,1,0:T(8,128)(2,1)S(1)} %slice.75), channel_id=1, source_target_pairs={{0,96},{1,25},{2,98},{3,27},{4,100},{5,29},{6,102},{7,31},{8,104},... | collective-permute-start | bytes 393224 | tf_op jit(solution)/shard_map/ppermute | solution.py:40
  29.1 7.5 %copy-start.9 = (bf16[16,64,512]{2,1,0:T(8,128)(2,1)}, bf16[16,64,512]{2,1,0:T(8,128)(2,1)S(1)}, u32[]{:S(2)}) copy-start(bf16[16,64,512]{2,1,0:T(8,128)(2,1)S(1)} %constant_dynamic-update-slice_fusion) | copy-start | bytes 3145732
  29.1 7.5 %collective-permute-start.8 = (bf16[1024,512]{1,0:T(8,128)(2,1)S(1)}, bf16[1024,512]{1,0:T(8,128)(2,1)S(1)}, u32[]{:S(2)}, u32[]{:S(2)}) collective-permute-start(bf16[1024,512]{1,0:T(8,128)(2,1)S(1)} %bitcast.69), channel_id=1, source_target_pairs={{0,1},{1,0},{2,3},{3,2},{4,5},{5,4},{6,7},{7,6},{8,9},{9,8},{10,11... | collective-permute-start | bytes 3145736 | tf_op jit(solution)/shard_map/ppermute | solution.py:27
  36.6 1.0 copy-start.10
  47.5 14.2 %copy-start.13 = (s32[128,2]{0,1:T(2,128)S(1)}, s32[128,2]{0,1:T(2,128)}, u32[]{:S(2)}) copy-start(s32[128,2]{0,1:T(2,128)} %param.20) | copy-start | bytes 3076
  59.9 2.5 copy-start.14
  60.9 103.9 %all-gather.14.cloned.1.call-start = ((), (), s32[]{:S(2)}) async-start(), calls=%async_computation.10 | async-start | bytes 8257536 | tf_op jit(solution)/shard_map/all_gather | solution.py:59
  61.7 156.6 %all-gather.12.cloned.1.call-start = ((), (), s32[]{:S(2)}) async-start(), calls=%async_computation.9 | async-start | bytes 5160960 | tf_op jit(solution)/shard_map/all_gather | solution.py:59
  63.3 7.7 %copy-start.11 = (bf16[128,896]{1,0:T(8,128)(2,1)S(1)}, bf16[128,896]{1,0:T(8,128)(2,1)}, u32[]{:S(2)}) copy-start(bf16[128,896]{1,0:T(8,128)(2,1)} %param.25) | copy-start | bytes 688132
  91.9 11.5 %all-to-all-start = ((bf16[8,16,896]{2,1,0:T(8,128)(2,1)}), bf16[8,16,896]{2,1,0:T(8,128)(2,1)S(1)}, u32[]{:S(2)}, u32[]{:S(2)}) async-start(bf16[8,16,896]{2,1,0:T(8,128)(2,1)} %bitcast), calls=%async_computation | async-start | bytes 458752 | tf_op jit(solution)/shard_map/all_to_all | solution.py:318
  103.4 61.4 %copy-start = (bf16[8,16,896]{2,1,0:T(8,128)(2,1)}, bf16[8,16,896]{2,1,0:T(8,128)(2,1)S(1)}, u32[]{:S(2)}) copy-start(bf16[8,16,896]{2,1,0:T(8,128)(2,1)S(1)} %all-to-all-done.refs_0_) | copy-start | bytes 688132
  170.4 14.2 %all-to-all-start.3 = ((bf16[16,16,448]{2,1,0:T(8,128)(2,1)}), bf16[16,16,448]{2,1,0:T(8,128)(2,1)S(1)}, u32[]{:S(2)}, u32[]{:S(2)}) async-start(bf16[16,16,448]{2,1,0:T(8,128)(2,1)} %shard_map.165), calls=%async_computation.3 | async-start | bytes 524288 | tf_op jit(solution)/shard_map/all_to_all | solution.py:340
  177.1 8.1 %copy-start.1 = (bf16[8,16,896]{2,1,0:T(8,128)(2,1)S(1)}, bf16[8,16,896]{2,1,0:T(8,128)(2,1)}, u32[]{:S(2)}) copy-start(bf16[8,16,896]{2,1,0:T(8,128)(2,1)} %copy-done) | copy-start | bytes 688132
  186.5 14.8 %all-to-all-start.4 = ((bf16[8,16,1024]{2,1,0:T(8,128)(2,1)}), bf16[8,16,1024]{2,1,0:T(8,128)(2,1)S(1)}, u32[]{:S(2)}, u32[]{:S(2)}) async-start(bf16[8,16,1024]{2,1,0:T(8,128)(2,1)} %pad_maximum_fusion.1), calls=%async_computation.4 | async-start | bytes 524288 | tf_op jit(solution)/shard_map/all_to_all | solution.py:406
  191.6 58.6 %all-gather.10.cloned.1.call-start = ((), (), s32[]{:S(2)}) async-start(), calls=%async_computation.8 | async-start | bytes 5160960 | tf_op jit(solution)/shard_map/all_gather | solution.py:59
  218.1 41.7 %copy-start.15 = (bf16[2,896,384]{2,1,0:T(8,128)(2,1)S(1)}, bf16[2,896,384]{2,1,0:T(8,128)(2,1)}, u32[]{:S(2)}) copy-start(bf16[2,896,384]{2,1,0:T(8,128)(2,1)} %get-tuple-element.27) | copy-start | bytes 4128772
  218.1 42.0 %copy-start.2 = (bf16[2,896,384]{2,1,0:T(8,128)(2,1)S(1)}, bf16[2,896,384]{2,1,0:T(8,128)(2,1)}, u32[]{:S(2)}) copy-start(bf16[2,896,384]{2,1,0:T(8,128)(2,1)} %get-tuple-element.24.refs_0_) | copy-start | bytes 4128772
  218.1 117.4 %all-gather.16.cloned.1.call-start = ((), (), s32[]{:S(2)}) async-start(), calls=%async_computation.11 | async-start | bytes 2949120 | tf_op jit(solution)/shard_map/all_gather | solution.py:59
  257.8 40.6 %collective-permute-start.10 = (bf16[2,896,384]{2,1,0:T(8,128)(2,1)}, bf16[2,896,384]{2,1,0:T(8,128)(2,1)S(1)}, u32[]{:S(2)}, u32[]{:S(2)}) collective-permute-start(bf16[2,896,384]{2,1,0:T(8,128)(2,1)} %get-tuple-element.25), channel_id=1, source_target_pairs={{0,6},{1,7},{2,0},{3,1},{4,2},{5,3},{6,4},{7,5},{8,14},{9,15},{10,... | collective-permute-start | bytes 4128776 | tf_op jit(solution)/shard_map/ppermute | solution.py:23
  258.4 41.8 %collective-permute-start.12 = (bf16[2,896,384]{2,1,0:T(8,128)(2,1)}, bf16[2,896,384]{2,1,0:T(8,128)(2,1)S(1)}, u32[]{:S(2)}, u32[]{:S(2)}) collective-permute-start(bf16[2,896,384]{2,1,0:T(8,128)(2,1)} %get-tuple-element.26), channel_id=1, source_target_pairs={{0,4},{1,5},{2,6},{3,7},{4,0},{5,1},{6,2},{7,3},{8,12},{9,13},{10,... | collective-permute-start | bytes 4128776 | tf_op jit(solution)/shard_map/ppermute | solution.py:23
  259.8 72.4 %collective-permute-start.14 = (bf16[2,896,384]{2,1,0:T(8,128)(2,1)S(1)}, bf16[2,896,384]{2,1,0:T(8,128)(2,1)S(1)}, u32[]{:S(2)}, u32[]{:S(2)}) collective-permute-start(bf16[2,896,384]{2,1,0:T(8,128)(2,1)S(1)} %copy-done.15), channel_id=1, source_target_pairs={{0,2},{1,3},{2,4},{3,5},{4,6},{5,7},{6,0},{7,1},{8,10},{9,11},{10,... | collective-permute-start | bytes 4128776 | tf_op jit(solution)/shard_map/ppermute | solution.py:23
  260.2 72.5 %collective-permute-start.9 = (bf16[2,896,384]{2,1,0:T(8,128)(2,1)S(1)}, bf16[2,896,384]{2,1,0:T(8,128)(2,1)S(1)}, u32[]{:S(2)}, u32[]{:S(2)}) collective-permute-start(bf16[2,896,384]{2,1,0:T(8,128)(2,1)S(1)} %copy-done.2), channel_id=1, source_target_pairs={{0,1},{1,0},{2,3},{3,2},{4,5},{5,4},{6,7},{7,6},{8,9},{9,8},{10,11... | collective-permute-start | bytes 4128776 | tf_op jit(solution)/shard_map/ppermute | solution.py:27
  298.4 34.3 %copy-start.3 = (bf16[2,896,384]{2,1,0:T(8,128)(2,1)}, bf16[2,896,384]{2,1,0:T(8,128)(2,1)S(1)}, u32[]{:S(2)}) copy-start(bf16[2,896,384]{2,1,0:T(8,128)(2,1)S(1)} %collective-permute-done.10.refs_2_) | copy-start | bytes 4128772
  298.4 34.3 %collective-permute-start.11 = (bf16[2,896,384]{2,1,0:T(8,128)(2,1)S(1)}, bf16[2,896,384]{2,1,0:T(8,128)(2,1)S(1)}, u32[]{:S(2)}, u32[]{:S(2)}) collective-permute-start(bf16[2,896,384]{2,1,0:T(8,128)(2,1)S(1)} %collective-permute-done.10.refs_2_), channel_id=1, source_target_pairs={{0,1},{1,0},{2,3},{3,2},{4,5},{5,4},{6,7},{7,6},{8,9},{9,8},{10,11... | collective-permute-start | bytes 4128776 | tf_op jit(solution)/shard_map/ppermute | solution.py:27
  300.2 32.5 %copy-start.4 = (bf16[2,896,384]{2,1,0:T(8,128)(2,1)}, bf16[2,896,384]{2,1,0:T(8,128)(2,1)S(1)}, u32[]{:S(2)}) copy-start(bf16[2,896,384]{2,1,0:T(8,128)(2,1)S(1)} %collective-permute-done.12.refs_4_) | copy-start | bytes 4128772
  300.2 32.5 %collective-permute-start.13 = (bf16[2,896,384]{2,1,0:T(8,128)(2,1)S(1)}, bf16[2,896,384]{2,1,0:T(8,128)(2,1)S(1)}, u32[]{:S(2)}, u32[]{:S(2)}) collective-permute-start(bf16[2,896,384]{2,1,0:T(8,128)(2,1)S(1)} %collective-permute-done.12.refs_4_), channel_id=1, source_target_pairs={{0,1},{1,0},{2,3},{3,2},{4,5},{5,4},{6,7},{7,6},{8,9},{9,8},{10,11... | collective-permute-start | bytes 4128776 | tf_op jit(solution)/shard_map/ppermute | solution.py:27
  332.2 1.1 copy-start.5
  332.2 3.4 collective-permute-start.15
  332.7 1.1 copy-start.6
  332.7 1.5 copy-start.7
  334.2 1.2 copy-start.8
  342.9 27.3 %all-to-all-start.6 = ((bf16[16,20,1920]{2,1,0:T(8,128)(2,1)}), bf16[16,20,1920]{2,1,0:T(8,128)(2,1)S(1)}, u32[]{:S(2)}, u32[]{:S(2)}) async-start(bf16[16,20,1920]{2,1,0:T(8,128)(2,1)} %shard_map.167), calls=%async_computation.6 | async-start | bytes 2949120 | tf_op jit(solution)/shard_map/all_to_all | solution.py:340
Sparse Core Ops, SparseCore 0:
  61.0 56.2 all-gather.7
  119.0 45.7 all-gather.13
  166.5 36.3 all-gather.11
  218.2 31.9 all-gather.9
  257.9 76.8 all-gather.15

commit v2 on v1

--- a/solution.py
+++ b/solution.py
@@ -40,19 +40,10 @@
     return lax.ppermute(block, ALL, pairs)
 
 
-def ring_list(block, shift):
-    half = block.shape[0] // 2
-    before = shift(block, 1)
-    after = shift(block, -1)
-    far = [shift(before[:half], 1), shift(after[half:], -1)]
-    return [block, after, far, before]
-
-
 def ctx_gather(block):
-    own, after, far, before = ring_list(block, lambda b, s: shift_plane(b, 0, s))
-    first = jnp.stack([own, after, jnp.concatenate(far, 0), before])
-    own, after, far, before = ring_list(first, lambda b, s: shift_plane(b, 1, s))
-    return [own, after, *far, before]
+    for phase in range(2):
+        block = jnp.stack([block] + [shift_plane(block, phase, -step) for step in range(1, SIDE)])
+    return block
 
 
 def group_gather(block):
@@ -88,14 +79,14 @@
     return jnp.concatenate([t.reshape(rows, 1) for t in terms] + [blank], 1)
 
 
-def lanes3(value):
+def lanes3(value, kind=BF16):
     lane = lax.broadcasted_iota(jnp.int32, (value.shape[0], LANES), 1)
     high = value.astype(BF16).astype(F32)
     rest = value - high
     middle = rest.astype(BF16).astype(F32)
     low = rest - middle
     wide = jnp.where(lane == 0, high, jnp.where(lane == 1, middle, jnp.where(lane == 2, low, 0.0)))
-    return wide.astype(BF16)
+    return wide.astype(kind)
 
 
 def call(kernel, outs, scalars=0, whole=None, **params):
@@ -223,17 +214,20 @@
     gate_grad = hidden_grad * up_in * gate_sig * (1.0 + gate_in * (1.0 - gate_sig))
     up_grad = hidden_grad * silu
     center = jnp.sum(gate_grad * gate_in + up_grad * up_in, axis=1, keepdims=True)
-    out_ref[:, :hidden] = gate_grad.astype(BF16)
-    out_ref[:, hidden : 2 * hidden] = up_grad.astype(BF16)
-    out_ref[:, 2 * hidden : 3 * hidden] = (silu * up_in).astype(BF16)
-    out_ref[:, 3 * hidden :] = lanes3(center)
+    slots = gate_in.shape[0]
+    out_ref[:slots, :hidden] = gate_grad.astype(BF16)
+    out_ref[:slots, hidden : 2 * hidden] = up_grad.astype(BF16)
+    out_ref[:slots, 2 * hidden :] = (silu * up_in).astype(BF16)
+    out_ref[slots:, :] = jnp.zeros((out_ref.shape[0] - slots, 3 * hidden), BF16)
+    out_ref[slots:, :slots] = lanes3(center, F32).T[: out_ref.shape[0] - slots].astype(BF16)
 
 
 def weight_grad_kernel(rows_ref, grads_ref, hidden_ref, gate_ref, up_ref, down_ref):
     hidden = gate_ref.shape[1]
     members, _, slice_width = rows_ref.shape
-    grads = hidden_ref[:, : 2 * hidden]
-    units = hidden_ref[:, 2 * hidden : 3 * hidden]
+    slots = rows_ref.shape[1]
+    grads = hidden_ref[:slots, : 2 * hidden]
+    units = hidden_ref[:slots, 2 * hidden :]
     for place in range(members):
         part = slice(place * slice_width, (place + 1) * slice_width)
         both = dot(rows_ref[place], grads, ((0,), (0,)))
@@ -254,15 +248,18 @@
     )
     slice_width, wide = weight_refs[0].shape[1:]
     hidden = wide // 3
+    slots = out_ref.shape[0] * out_ref.shape[1]
     rows, grads, center = 0.0, 0.0, 0.0
     for place in range(8):
         for copy in copies:
             copy[place].wait()
-        units = unit_buf[place]
+        units = unit_buf[place, :slots]
         weight = weight_buf[place]
         grads = grads + dot(units[:, : 2 * hidden], weight[:, : 2 * hidden], ((1,), (1,)))
-        rows = rows + dot(units[:, 2 * hidden : 3 * hidden], weight[:, 2 * hidden :], ((1,), (1,)))
-        center = center + jnp.sum(units[:, 3 * hidden :].astype(F32), axis=1, keepdims=True)
+        rows = rows + dot(units[:, 2 * hidden :], weight[:, 2 * hidden :], ((1,), (1,)))
+        center = center + unit_buf[place, slots:].astype(F32)
+    center = jnp.sum(center, axis=0, keepdims=True)
+    center = jnp.broadcast_to(center, (LANES, wide)).T[:slots, :1]
     rows, grads, center = rows.astype(BF16), grads.astype(BF16), lanes3(center)
     sources, capacity = out_ref.shape[:2]
     for source in range(sources):
@@ -340,14 +337,13 @@
         return lax.all_to_all(rows, "ctx", split_axis=0, concat_axis=0, tiled=True)
 
     grad_rows = (dot(pick, grad_out) * slot_weight[:, None]).astype(BF16)
-    grad_rows, *weight_pairs = lax.optimization_barrier((grad_rows, *weight_pairs))
     grad_rows = to_experts(grad_rows)
     out_grad = group_gather(grad_rows)
     slice_weights = group_exchange(weight_pairs)
 
     half = token_count // 2
     own_keys = ctx_gather(lax.dynamic_slice_in_dim(latent, core * half, half, 0))
-    own_keys = jnp.concatenate(own_keys, 0).reshape(ctx_count * half, latent_width)
+    own_keys = own_keys.reshape(ctx_count * half, latent_width)
     other_keys = swap_core(own_keys)
     own_frames = lax.dynamic_slice_in_dim(frames, ctx_place * token_count, token_count)
     frame_grid = frames.reshape(SIDE, SIDE, 2, half)
@@ -359,7 +355,7 @@
         jnp.concatenate([by_x[0].reshape(-1), by_y[1].reshape(-1)]),
         jnp.concatenate([by_y[1].reshape(-1), by_x[0].reshape(-1)]),
     )
-    heads = 2
+    heads = 4
     head_out = pl.pallas_call(
         functools.partial(attend_kernel, latent_width ** (-0.5)),
         out_shape=shape(token_count, head_count * value_width),
@@ -413,7 +409,7 @@
     expert_rows = group_gather(to_experts(dot(pick, normed).astype(BF16)))
     hidden_send = call(
         expert_kernel,
-        shape(slot_total, 3 * hidden_width + LANES),
+        shape(slot_total + 8, 3 * hidden_width),
         1,
         0,
         scratch_shapes=buffers(*[(8, slot_total, slice_width)] * 2, (8, *block)),
@@ -429,7 +425,7 @@
         shape(ctx_count, capacity, 2 * slice_width + LANES),
         1,
         0,
-        scratch_shapes=buffers((8, slot_total, 3 * hidden_width + LANES), (8, *block)),
+        scratch_shapes=buffers((8, slot_total + 8, 3 * hidden_width), (8, *block)),
     )(places, hidden_all, *slice_weights)
     back = to_experts(back).reshape(slot_total, 2 * slice_width + LANES)
 

time: 382 us -> 373 us (0.976)
    all_to_all x1, waiting for transfers between devices: 5.32 us -> 0.01 us  [per_device(): lax.all_to_all(residual.reshape(group_count, part_tokens, slice_width), G...]
    ppermute x3, waiting for transfers between devices: 69.1 us -> 64.3 us  [shift_z(): lax.ppermute(block, GROUP, [(g, (g + 2 * step) % 8) for g in range(8)])]
    ppermute x8 -> x6, waiting for transfers between devices: 8.7 us -> 13 us  [shift_plane(): return lax.ppermute(block, ALL, pairs)]
    ppermute x8 -> x6, starting transfers between devices: 12.1 us -> 8.27 us  [shift_plane(): return lax.ppermute(block, ALL, pairs)]
  transfers between devices with their start and end apart: 25 -> 23, of which waited for: 15 -> 17; matrix products, arithmetic and copies ran while one was open for 2% -> 2% of each run, Pallas kernels for 6% -> 6%
where the time goes in v2:
time: 373 us; the launch traced here: 370 us
  waiting for transfers between devices  203 us (54%)
  Pallas kernels  46.9 us (13%)
  blocking collectives  44.6 us (12%)
  starting transfers between devices  44 us (12%)
  between operations  14.2 us (4%)
  local copies, waits for them, and re-layouts  10.7 us (3%)
  other arithmetic  4.1 us (1%)
    all_gather x4, waiting for transfers between devices, group_gather(): return lax.all_gather(block, GROUP, axis=0)  79.6 us
    ppermute x3, waiting for transfers between devices, shift_z(): lax.ppermute(block, GROUP, [(g, (g + 2 * step) % 8) for g in range(8)])  64.3 us
    pallas_call x5, Pallas kernels, run(): pl.pallas_call(kernel, out_shape=outs, in_specs=[pl.BlockSpec(memory_spac...  37.5 us
    all_to_all x2, blocking collectives, to_experts(): return lax.all_to_all(rows, 'ctx', split_axis=0, concat_axis=0, tiled=True)  32.3 us
    all_to_all x2, waiting for transfers between devices, to_experts(): return lax.all_to_all(rows, 'ctx', split_axis=0, concat_axis=0, tiled=True)  19 us
    all_gather x1, waiting for transfers between devices, per_device(): all_heads = lax.all_gather(head_part, 'ctx', axis=0)  14.2 us
    all_to_all x2, starting transfers between devices, to_experts(): return lax.all_to_all(rows, 'ctx', split_axis=0, concat_axis=0, tiled=True)  13.1 us
    ppermute x6, waiting for transfers between devices, shift_plane(): return lax.ppermute(block, ALL, pairs)  13 us
  transfers between devices with their start and end apart: 23, of which 17 were waited for; matrix products, arithmetic and copies ran while one was open for 2% of the time, Pallas kernels for 6%

profile of v2, /device:TPU:1, one launch (start us, length us, event | category | flops | bytes accessed | tf_op | source)
XLA Modules:
  0.0 370.2 jit_solution(11327110073156913027)
XLA Ops:
  7.2 0.8 copy-done
  8.1 3.3 collective-permute-start
  11.4 0.5 collective-permute-start.1
  11.9 0.6 collective-permute-start.2
  12.7 3.3 collective-permute-done.1
  16.1 0.7 collective-permute-done.2
  16.8 2.8 collective-permute-start.3
  19.6 0.3 collective-permute-start.4
  19.9 0.7 collective-permute-start.5
  20.6 5.1 %collective-permute-done.3 = bf16[4,64,512]{2,1,0:T(8,128)(2,1)S(1)} collective-permute-done((bf16[4,64,512]{2,1,0:T(8,128)(2,1)S(1)}, bf16[4,64,512]{2,1,0:T(8,128)(2,1)S(1)}, u32[]{:S(2)}, u32[]{:S(2)}) %collective-permute-start.3) | collective-permute-done | bytes 262176 | tf_op jit(solution)/shard_map/ppermute | solution.py:40
  25.7 0.9 collective-permute-done.4
  26.6 2.8 collective-permute-done.5
  29.5 3.3 collective-permute-start.6
  33.4 0.7 copy.79.own_frame_ref
  34.1 0.6 broadcast_select_fusion.key_frame_ref
  34.7 0.4 collective-permute-done.6.far_ref
  35.1 1.0 copy-done.12
  36.1 9.4 %attend.1 = bf16[128,1024]{1,0:T(8,128)(2,1)} custom-call(bf16[128,4096]{1,0:T(8,128)(2,1)} %q_ref.1, bf16[1024,512]{1,0:T(8,128)(2,1)} %bitcast.62, bf16[1024,512]{1,0:T(8,128)(2,1)} %copy-done.12, s32[1,2048]{1,0:T(1,128)} %broadcast_select_fusion.key_frame_ref, s32[128,1]{1,0:T(8,128)} %copy.79.own_frame_ref, bf16[8,512,128]{2,1,0:T(8,128)(2,1)} %uv_ref.1), custom_call_target="tpu_custom_call" | custom-call | tf_op jit(solution)/shard_map/attend/pallas_call | solution.py:359
  45.5 12.3 %all_to_all.45 = bf16[8,16,1024]{2,1,0:T(8,128)(2,1)S(1)} all-to-all(bf16[8,16,1024]{2,1,0:T(8,128)(2,1)} %bitcast.71), channel_id=1, replica_groups=mesh['ctx'=16,'role'=2,'exp'=4] {'role','exp'}, dimensions={0} | all-to-all | bytes 524288 | tf_op jit(solution)/shard_map/all_to_all | solution.py:376
  57.9 0.8 all_gather_reshape.3
  58.8 0.7 all-gather.14.cloned.1.call-update
  60.5 0.3 fusion
  61.0 17.2 %all_to_all.46 = bf16[16,20,896]{2,1,0:T(8,128)(2,1)S(1)} all-to-all(bf16[16,20,896]{2,1,0:T(8,128)(2,1)S(1)} %all_to_all.30), channel_id=1, replica_groups=mesh['ctx'=16,'role'=2,'exp'=4] {'ctx'}, dimensions={0} | all-to-all | bytes 1146880 | tf_op jit(solution)/shard_map/all_to_all | solution.py:337
  78.2 0.9 all_gather.32
  79.1 6.1 %all-to-all-start = ((bf16[8,16,896]{2,1,0:T(8,128)(2,1)}), bf16[8,16,896]{2,1,0:T(8,128)(2,1)S(1)}, u32[]{:S(2)}, u32[]{:S(2)}) async-start(bf16[8,16,896]{2,1,0:T(8,128)(2,1)} %bitcast), calls=%async_computation | async-start | bytes 458752 | tf_op jit(solution)/shard_map/all_to_all | solution.py:315
  85.2 0.6 pad_add_fusion.place_ref
  85.8 7.7 %shard_map.164 = (bf16[8,896,384]{2,1,0:T(8,128)(2,1)}, bf16[2,896,384]{2,1,0:T(8,128)(2,1)}, bf16[2,896,384]{2,1,0:T(8,128)(2,1)}, bf16[2,896,384]{2,1,0:T(8,128)(2,1)}, bf16[2,896,384]{2,1,0:T(8,128)(2,1)}) custom-call(s32[2]{0:T(128)} %pad_add_fusion.place_ref, bf16[128,7168]{1,0:T(8,128)(2,1)} %bitcast.68, bf16[7168,128]{1,0:T(8,128)(2,1)} %bitcast.69, ...), custom_call_target="tpu_custom_call" | custom-call | tf_op jit(solution)/shard_map/pallas_call | solution.py:97
  93.5 0.9 all_to_all.32.refs_1_
  94.4 14.2 %all-gather.8.cloned.1.call-done.rows_ref = bf16[16,16,8192]{2,1,0:T(8,128)(2,1)} async-done(((bf16[1,16,8192]{2,1,0:T(8,128)(2,1)}), bf16[16,16,8192]{2,1,0:T(8,128)(2,1)}) %all-gather.8.cloned.1.call-update) | async-done | bytes 4194320 | tf_op jit(solution)/shard_map/all_gather | solution.py:378
  108.6 47.5 %all-gather.14.cloned.1.call-done = bf16[3584,1024]{1,0:T(8,128)(2,1)} async-done(((bf16[448,1024]{1,0:T(8,128)(2,1)}), bf16[3584,1024]{1,0:T(8,128)(2,1)}) %all-gather.14.cloned.1.call-update) | async-done | bytes 7340048 | tf_op jit(solution)/shard_map/all_gather | solution.py:50
  156.1 5.6 %shard_map.165 = bf16[16,16,448]{2,1,0:T(8,128)(2,1)} custom-call(bf16[16,16,8192]{2,1,0:T(8,128)(2,1)} %all-gather.8.cloned.1.call-done.rows_ref, bf16[8,448,1024]{2,1,0:T(8,128)(2,1)} %bitcast.60, bf16[8,16,896]{2,1,0:T(8,128)(2,1)} %copy-done.3, bf16[320,896]{1,0:T(8,128)(2,1)} %all_to_all.32.refs_1_, ...), custom_call_target="tpu_custom_call" | custom-call | tf_op jit(solution)/shard_map/pallas_call | solution.py:97
  161.7 6.5 %all-to-all-start.3 = ((bf16[16,16,448]{2,1,0:T(8,128)(2,1)}), bf16[16,16,448]{2,1,0:T(8,128)(2,1)S(1)}, u32[]{:S(2)}, u32[]{:S(2)}) async-start(bf16[16,16,448]{2,1,0:T(8,128)(2,1)} %shard_map.165), calls=%async_computation.3 | async-start | bytes 524288 | tf_op jit(solution)/shard_map/all_to_all | solution.py:337
  168.3 7.6 %all-to-all-done.3 = bf16[16,16,448]{2,1,0:T(8,128)(2,1)S(1)} async-done(((bf16[16,16,448]{2,1,0:T(8,128)(2,1)}), bf16[16,16,448]{2,1,0:T(8,128)(2,1)S(1)}, u32[]{:S(2)}, u32[]{:S(2)}) %all-to-all-start.3) | async-done | bytes 229408 | tf_op jit(solution)/shard_map/all_to_all | solution.py:337
  176.0 0.3 copy.83
  177.1 0.8 pad_maximum_fusion.2
  177.8 5.1 %all-to-all-start.4 = ((bf16[8,16,1024]{2,1,0:T(8,128)(2,1)}), bf16[8,16,1024]{2,1,0:T(8,128)(2,1)S(1)}, u32[]{:S(2)}, u32[]{:S(2)}) async-start(bf16[8,16,1024]{2,1,0:T(8,128)(2,1)} %pad_maximum_fusion.2), calls=%async_computation.4 | async-start | bytes 524288 | tf_op jit(solution)/shard_map/all_to_all | solution.py:402
  182.9 0.8 dynamic_slice.19
  183.7 8.9 %all-to-all-done.4 = bf16[8,16,1024]{2,1,0:T(8,128)(2,1)S(1)} async-done(((bf16[8,16,1024]{2,1,0:T(8,128)(2,1)}), bf16[8,16,1024]{2,1,0:T(8,128)(2,1)S(1)}, u32[]{:S(2)}, u32[]{:S(2)}) %all-to-all-start.4) | async-done | bytes 262176 | tf_op jit(solution)/shard_map/all_to_all | solution.py:402
  192.7 0.4 convolution_convert_fusion
  193.3 15.1 %all_to_all.47 = bf16[16,20,896]{2,1,0:T(8,128)(2,1)S(1)} all-to-all(bf16[16,20,896]{2,1,0:T(8,128)(2,1)S(1)} %all_to_all.35), channel_id=1, replica_groups=mesh['ctx'=16,'role'=2,'exp'=4] {'ctx'}, dimensions={0} | all-to-all | bytes 1146880 | tf_op jit(solution)/shard_map/all_to_all | solution.py:337
  208.4 1.0 all_gather.30
  209.5 32.1 %all-gather.10.cloned.1.call-done.rows_ref = bf16[8,320,896]{2,1,0:T(8,128)(2,1)} async-done(((bf16[1,320,896]{2,1,0:T(8,128)(2,1)}), bf16[8,320,896]{2,1,0:T(8,128)(2,1)}) %all-gather.10.cloned.1.call-update) | async-done | bytes 4587536 | tf_op jit(solution)/shard_map/all_gather | solution.py:50
  241.6 7.5 %shard_map.166.hidden_ref = bf16[328,384]{1,0:T(8,128)(2,1)} custom-call(s32[2]{0:T(128)} %pad_add_fusion.place_ref, bf16[8,320,896]{2,1,0:T(8,128)(2,1)} %all-gather.10.cloned.1.call-done.rows_ref, bf16[8,320,896]{2,1,0:T(8,128)(2,1)} %all-gather.12.cloned.1.call-done.grads_ref, bf16[8,896,384]{2,1,0:T(8,128)(2,1)} %get-tuple-element.13.refs_2_.weight_ref), custom_call_target="tpu_custom_call" | custom-call | tf_op jit(solution)/shard_map/pallas_call | solution.py:97
  249.1 1.5 collective-permute-start.10
  250.6 2.7 collective-permute-start.8
  253.3 1.1 collective-permute-start.7
  254.4 32.1 %collective-permute-done.10.refs_4_ = bf16[2,896,384]{2,1,0:T(8,128)(2,1)S(1)} collective-permute-done((bf16[2,896,384]{2,1,0:T(8,128)(2,1)}, bf16[2,896,384]{2,1,0:T(8,128)(2,1)S(1)}, u32[]{:S(2)}, u32[]{:S(2)}) %collective-permute-start.10) | collective-permute-done | bytes 1376288 | tf_op jit(solution)/shard_map/ppermute | solution.py:23
  286.5 1.8 collective-permute-start.11
  288.3 32.3 %collective-permute-done.12.refs_6_ = bf16[2,896,384]{2,1,0:T(8,128)(2,1)S(1)} collective-permute-done((bf16[2,896,384]{2,1,0:T(8,128)(2,1)}, bf16[2,896,384]{2,1,0:T(8,128)(2,1)S(1)}, u32[]{:S(2)}, u32[]{:S(2)}) %collective-permute-start.12) | collective-permute-done | bytes 1376288 | tf_op jit(solution)/shard_map/ppermute | solution.py:23
  320.6 0.5 collective-permute-start.13
  321.1 0.3 collective-permute-start.9
  321.4 0.3 copy-done.7
  321.7 2.1 collective-permute-done.13.refs_7_
  323.8 1.1 copy-done.11
  324.9 1.0 collective-permute-done.9.refs_3_
  325.9 7.3 %shard_map.167 = bf16[16,20,1920]{2,1,0:T(8,128)(2,1)} custom-call(s32[2]{0:T(128)} %pad_add_fusion.place_ref, bf16[8,328,384]{2,1,0:T(8,128)(2,1)} %bitcast.67, bf16[2,896,384]{2,1,0:T(8,128)(2,1)} %get-tuple-element.14.refs_0_, bf16[2,896,384]{2,1,0:T(8,128)(2,1)} %copy-done.9, bf16[2,896,384]{2,1,0:T(8,128)(2,1)} %copy-done.8, ...), custom_call_target="tpu_custom_call" | custom-call | tf_op jit(solution)/shard_map/pallas_call | solution.py:97
  333.3 6.5 %all-to-all-start.6 = ((bf16[16,20,1920]{2,1,0:T(8,128)(2,1)}), bf16[16,20,1920]{2,1,0:T(8,128)(2,1)S(1)}, u32[]{:S(2)}, u32[]{:S(2)}) async-start(bf16[16,20,1920]{2,1,0:T(8,128)(2,1)} %shard_map.167), calls=%async_computation.6 | async-start | bytes 2949120 | tf_op jit(solution)/shard_map/all_to_all | solution.py:337
  339.8 9.4 %shard_map.168 = (bf16[7168,128]{1,0:T(8,128)(2,1)}, bf16[7168,128]{1,0:T(8,128)(2,1)}, bf16[128,7168]{1,0:T(8,128)(2,1)}) custom-call(bf16[8,320,896]{2,1,0:T(8,128)(2,1)} %all-gather.10.cloned.1.call-done.rows_ref, bf16[8,320,896]{2,1,0:T(8,128)(2,1)} %all-gather.12.cloned.1.call-done.grads_ref, bf16[328,384]{1,0:T(8,128)(2,1)} %shard_map.166.hidden_ref), custom_call_target="tpu_custom_call" | custom-call | tf_op jit(solution)/shard_map/pallas_call | solution.py:97
  349.2 11.4 %all-to-all-done.6 = bf16[16,20,1920]{2,1,0:T(8,128)(2,1)S(1)} async-done(((bf16[16,20,1920]{2,1,0:T(8,128)(2,1)}), bf16[16,20,1920]{2,1,0:T(8,128)(2,1)S(1)}, u32[]{:S(2)}, u32[]{:S(2)}) %all-to-all-start.6) | async-done | bytes 1228832 | tf_op jit(solution)/shard_map/all_to_all | solution.py:337
  360.6 0.3 reshape.188
  360.9 0.3 fusion.4
  361.3 0.3 convolution_multiply_fusion.2
  361.7 0.9 fusion.14
  362.7 1.0 fusion.3
  (92 shorter events, 3.5 us)
Async XLA Ops:
  7.2 0.9 copy-start
  7.2 101.4 %all-gather.8.cloned.1.call-start = ((), (), s32[]{:S(2)}) async-start(), calls=%async_computation.7 | async-start | bytes 4456448 | tf_op jit(solution)/shard_map/all_gather | solution.py:378
  8.1 4.6 %collective-permute-start = (bf16[64,512]{1,0:T(8,128)(2,1)S(1)}, bf16[64,512]{1,0:T(8,128)(2,1)S(1)}, u32[]{:S(2)}, u32[]{:S(2)}) collective-permute-start(bf16[64,512]{1,0:T(8,128)(2,1)S(1)} %constant_dynamic-slice_fusion), channel_id=1, source_target_pairs={{0,24},{1,97},{2,26},{3,99},{4,28},{5,101},{6,30},{7,103},{8,0},{9... | collective-permute-start | bytes 196616 | tf_op jit(solution)/shard_map/ppermute | solution.py:40
  11.4 4.7 %collective-permute-start.1 = (bf16[64,512]{1,0:T(8,128)(2,1)S(1)}, bf16[64,512]{1,0:T(8,128)(2,1)S(1)}, u32[]{:S(2)}, u32[]{:S(2)}) collective-permute-start(bf16[64,512]{1,0:T(8,128)(2,1)S(1)} %constant_dynamic-slice_fusion), channel_id=1, source_target_pairs={{0,16},{1,65},{2,18},{3,67},{4,20},{5,69},{6,22},{7,71},{8,24},{9,... | collective-permute-start | bytes 196616 | tf_op jit(solution)/shard_map/ppermute | solution.py:40
  11.9 4.8 %collective-permute-start.2 = (bf16[64,512]{1,0:T(8,128)(2,1)S(1)}, bf16[64,512]{1,0:T(8,128)(2,1)S(1)}, u32[]{:S(2)}, u32[]{:S(2)}) collective-permute-start(bf16[64,512]{1,0:T(8,128)(2,1)S(1)} %constant_dynamic-slice_fusion), channel_id=1, source_target_pairs={{0,8},{1,33},{2,10},{3,35},{4,12},{5,37},{6,14},{7,39},{8,16},{9,4... | collective-permute-start | bytes 196616 | tf_op jit(solution)/shard_map/ppermute | solution.py:40
  16.7 16.2 %copy-start.14 = (s32[2048]{0:T(1024)S(1)}, s32[2048]{0:T(1024)}, u32[]{:S(2)}) copy-start(s32[2048]{0:T(1024)} %param.15) | copy-start | bytes 24580
  16.8 8.9 %collective-permute-start.3 = (bf16[4,64,512]{2,1,0:T(8,128)(2,1)S(1)}, bf16[4,64,512]{2,1,0:T(8,128)(2,1)S(1)}, u32[]{:S(2)}, u32[]{:S(2)}) collective-permute-start(bf16[4,64,512]{2,1,0:T(8,128)(2,1)S(1)} %get-tuple-element.24), channel_id=1, source_target_pairs={{0,96},{1,25},{2,98},{3,27},{4,100},{5,29},{6,102},{7,31},{8,104},... | collective-permute-start | bytes 786440 | tf_op jit(solution)/shard_map/ppermute | solution.py:40
  19.6 7.1 %collective-permute-start.4 = (bf16[4,64,512]{2,1,0:T(8,128)(2,1)S(1)}, bf16[4,64,512]{2,1,0:T(8,128)(2,1)S(1)}, u32[]{:S(2)}, u32[]{:S(2)}) collective-permute-start(bf16[4,64,512]{2,1,0:T(8,128)(2,1)S(1)} %get-tuple-element.24), channel_id=1, source_target_pairs={{0,64},{1,17},{2,66},{3,19},{4,68},{5,21},{6,70},{7,23},{8,72},{9,... | collective-permute-start | bytes 786440 | tf_op jit(solution)/shard_map/ppermute | solution.py:40
  19.9 9.5 %collective-permute-start.5 = (bf16[4,64,512]{2,1,0:T(8,128)(2,1)S(1)}, bf16[4,64,512]{2,1,0:T(8,128)(2,1)S(1)}, u32[]{:S(2)}, u32[]{:S(2)}) collective-permute-start(bf16[4,64,512]{2,1,0:T(8,128)(2,1)S(1)} %get-tuple-element.24), channel_id=1, source_target_pairs={{0,32},{1,9},{2,34},{3,11},{4,36},{5,13},{6,38},{7,15},{8,40},{9,1... | collective-permute-start | bytes 786440 | tf_op jit(solution)/shard_map/ppermute | solution.py:40
  29.5 5.6 %copy-start.2 = (bf16[4,4,64,512]{3,2,1,0:T(8,128)(2,1)}, bf16[4,4,64,512]{3,2,1,0:T(8,128)(2,1)S(1)}, u32[]{:S(2)}) copy-start(bf16[4,4,64,512]{3,2,1,0:T(8,128)(2,1)S(1)} %pad_maximum_fusion) | copy-start | bytes 3145732
  29.5 5.6 %collective-permute-start.6 = (bf16[1024,512]{1,0:T(8,128)(2,1)S(1)}, bf16[1024,512]{1,0:T(8,128)(2,1)S(1)}, u32[]{:S(2)}, u32[]{:S(2)}) collective-permute-start(bf16[1024,512]{1,0:T(8,128)(2,1)S(1)} %bitcast.61), channel_id=1, source_target_pairs={{0,1},{1,0},{2,3},{3,2},{4,5},{5,4},{6,7},{7,6},{8,9},{9,8},{10,11... | collective-permute-start | bytes 3145736 | tf_op jit(solution)/shard_map/ppermute | solution.py:27
  35.1 1.0 copy-start.12
  45.5 14.1 %copy-start.15 = (s32[128,2]{0,1:T(2,128)S(1)}, s32[128,2]{0,1:T(2,128)}, u32[]{:S(2)}) copy-start(s32[128,2]{0,1:T(2,128)} %param.20) | copy-start | bytes 3076
  57.8 2.5 copy-start.16
  57.8 2.7 copy-start.13
  58.8 97.3 %all-gather.14.cloned.1.call-start = ((), (), s32[]{:S(2)}) async-start(), calls=%async_computation.10 | async-start | bytes 8257536 | tf_op jit(solution)/shard_map/all_gather | solution.py:50
  59.5 149.9 %all-gather.12.cloned.1.call-start = ((), (), s32[]{:S(2)}) async-start(), calls=%async_computation.9 | async-start | bytes 5160960 | tf_op jit(solution)/shard_map/all_gather | solution.py:50
  79.1 15.3 %all-to-all-start = ((bf16[8,16,896]{2,1,0:T(8,128)(2,1)}), bf16[8,16,896]{2,1,0:T(8,128)(2,1)S(1)}, u32[]{:S(2)}, u32[]{:S(2)}) async-start(bf16[8,16,896]{2,1,0:T(8,128)(2,1)} %bitcast), calls=%async_computation | async-start | bytes 458752 | tf_op jit(solution)/shard_map/all_to_all | solution.py:315
  94.4 61.7 %copy-start.3 = (bf16[8,16,896]{2,1,0:T(8,128)(2,1)}, bf16[8,16,896]{2,1,0:T(8,128)(2,1)S(1)}, u32[]{:S(2)}) copy-start(bf16[8,16,896]{2,1,0:T(8,128)(2,1)S(1)} %all-to-all-done.refs_0_) | copy-start | bytes 688132
  161.7 14.2 %all-to-all-start.3 = ((bf16[16,16,448]{2,1,0:T(8,128)(2,1)}), bf16[16,16,448]{2,1,0:T(8,128)(2,1)S(1)}, u32[]{:S(2)}, u32[]{:S(2)}) async-start(bf16[16,16,448]{2,1,0:T(8,128)(2,1)} %shard_map.165), calls=%async_computation.3 | async-start | bytes 524288 | tf_op jit(solution)/shard_map/all_to_all | solution.py:337
  168.3 8.1 %copy-start.4 = (bf16[8,16,896]{2,1,0:T(8,128)(2,1)S(1)}, bf16[8,16,896]{2,1,0:T(8,128)(2,1)}, u32[]{:S(2)}) copy-start(bf16[8,16,896]{2,1,0:T(8,128)(2,1)} %copy-done.3) | copy-start | bytes 688132
  177.8 14.8 %all-to-all-start.4 = ((bf16[8,16,1024]{2,1,0:T(8,128)(2,1)}), bf16[8,16,1024]{2,1,0:T(8,128)(2,1)S(1)}, u32[]{:S(2)}, u32[]{:S(2)}) async-start(bf16[8,16,1024]{2,1,0:T(8,128)(2,1)} %pad_maximum_fusion.2), calls=%async_computation.4 | async-start | bytes 524288 | tf_op jit(solution)/shard_map/all_to_all | solution.py:402
  182.9 58.6 %all-gather.10.cloned.1.call-start = ((), (), s32[]{:S(2)}) async-start(), calls=%async_computation.8 | async-start | bytes 5160960 | tf_op jit(solution)/shard_map/all_gather | solution.py:50
  209.4 41.2 %copy-start.17 = (bf16[2,896,384]{2,1,0:T(8,128)(2,1)S(1)}, bf16[2,896,384]{2,1,0:T(8,128)(2,1)}, u32[]{:S(2)}) copy-start(bf16[2,896,384]{2,1,0:T(8,128)(2,1)} %get-tuple-element.15) | copy-start | bytes 4128772
  209.4 43.9 %copy-start.5 = (bf16[2,896,384]{2,1,0:T(8,128)(2,1)S(1)}, bf16[2,896,384]{2,1,0:T(8,128)(2,1)}, u32[]{:S(2)}) copy-start(bf16[2,896,384]{2,1,0:T(8,128)(2,1)} %get-tuple-element.14.refs_0_) | copy-start | bytes 4128772
  209.4 116.5 %all-gather.16.cloned.1.call-start = ((), (), s32[]{:S(2)}) async-start(), calls=%async_computation.11 | async-start | bytes 2267136 | tf_op jit(solution)/shard_map/all_gather | solution.py:50
  249.1 37.4 %collective-permute-start.10 = (bf16[2,896,384]{2,1,0:T(8,128)(2,1)}, bf16[2,896,384]{2,1,0:T(8,128)(2,1)S(1)}, u32[]{:S(2)}, u32[]{:S(2)}) collective-permute-start(bf16[2,896,384]{2,1,0:T(8,128)(2,1)} %get-tuple-element.16), channel_id=1, source_target_pairs={{0,4},{1,5},{2,6},{3,7},{4,0},{5,1},{6,2},{7,3},{8,12},{9,13},{10,... | collective-permute-start | bytes 4128776 | tf_op jit(solution)/shard_map/ppermute | solution.py:23
  250.6 70.0 %collective-permute-start.12 = (bf16[2,896,384]{2,1,0:T(8,128)(2,1)}, bf16[2,896,384]{2,1,0:T(8,128)(2,1)S(1)}, u32[]{:S(2)}, u32[]{:S(2)}) collective-permute-start(bf16[2,896,384]{2,1,0:T(8,128)(2,1)} %get-tuple-element.17), channel_id=1, source_target_pairs={{0,2},{1,3},{2,4},{3,5},{4,6},{5,7},{6,0},{7,1},{8,10},{9,11},{10,... | collective-permute-start | bytes 4128776 | tf_op jit(solution)/shard_map/ppermute | solution.py:23
  250.6 70.5 %collective-permute-start.8 = (bf16[2,896,384]{2,1,0:T(8,128)(2,1)S(1)}, bf16[2,896,384]{2,1,0:T(8,128)(2,1)S(1)}, u32[]{:S(2)}, u32[]{:S(2)}) collective-permute-start(bf16[2,896,384]{2,1,0:T(8,128)(2,1)S(1)} %copy-done.17), channel_id=1, source_target_pairs={{0,6},{1,7},{2,0},{3,1},{4,2},{5,3},{6,4},{7,5},{8,14},{9,15},{10,... | collective-permute-start | bytes 4128776 | tf_op jit(solution)/shard_map/ppermute | solution.py:23
  253.3 68.1 %collective-permute-start.7 = (bf16[2,896,384]{2,1,0:T(8,128)(2,1)S(1)}, bf16[2,896,384]{2,1,0:T(8,128)(2,1)S(1)}, u32[]{:S(2)}, u32[]{:S(2)}) collective-permute-start(bf16[2,896,384]{2,1,0:T(8,128)(2,1)S(1)} %copy-done.5), channel_id=1, source_target_pairs={{0,1},{1,0},{2,3},{3,2},{4,5},{5,4},{6,7},{7,6},{8,9},{9,8},{10,11... | collective-permute-start | bytes 4128776 | tf_op jit(solution)/shard_map/ppermute | solution.py:27
  286.5 34.9 %copy-start.6 = (bf16[2,896,384]{2,1,0:T(8,128)(2,1)}, bf16[2,896,384]{2,1,0:T(8,128)(2,1)S(1)}, u32[]{:S(2)}) copy-start(bf16[2,896,384]{2,1,0:T(8,128)(2,1)S(1)} %collective-permute-done.10.refs_4_) | copy-start | bytes 4128772
  286.5 34.9 %collective-permute-start.11 = (bf16[2,896,384]{2,1,0:T(8,128)(2,1)S(1)}, bf16[2,896,384]{2,1,0:T(8,128)(2,1)S(1)}, u32[]{:S(2)}, u32[]{:S(2)}) collective-permute-start(bf16[2,896,384]{2,1,0:T(8,128)(2,1)S(1)} %collective-permute-done.10.refs_4_), channel_id=1, source_target_pairs={{0,1},{1,0},{2,3},{3,2},{4,5},{5,4},{6,7},{7,6},{8,9},{9,8},{10,11... | collective-permute-start | bytes 4128776 | tf_op jit(solution)/shard_map/ppermute | solution.py:27
  320.6 1.1 copy-start.7
  320.6 3.2 collective-permute-start.13
  321.1 2.8 copy-start.8
  321.1 4.8 %collective-permute-start.9 = (bf16[2,896,384]{2,1,0:T(8,128)(2,1)S(1)}, bf16[2,896,384]{2,1,0:T(8,128)(2,1)}, u32[]{:S(2)}, u32[]{:S(2)}) collective-permute-start(bf16[2,896,384]{2,1,0:T(8,128)(2,1)S(1)} %collective-permute-done.8.refs_2_), channel_id=1, source_target_pairs={{0,1},{1,0},{2,3},{3,2},{4,5},{5,4},{6,7},{7,6},{8,9},{9,8},{10,11... | collective-permute-start | bytes 4128776 | tf_op jit(solution)/shard_map/ppermute | solution.py:27
  321.4 2.4 copy-start.9
  321.7 2.2 copy-start.10
  323.8 1.1 copy-start.11
  333.3 27.3 %all-to-all-start.6 = ((bf16[16,20,1920]{2,1,0:T(8,128)(2,1)}), bf16[16,20,1920]{2,1,0:T(8,128)(2,1)S(1)}, u32[]{:S(2)}, u32[]{:S(2)}) async-start(bf16[16,20,1920]{2,1,0:T(8,128)(2,1)} %shard_map.167), calls=%async_computation.6 | async-start | bytes 2949120 | tf_op jit(solution)/shard_map/all_to_all | solution.py:337
  361.3 2.4 copy-start.1
Sparse Core Ops, SparseCore 0:
  58.9 49.6 all-gather.7
  110.3 45.7 all-gather.13
  157.8 36.3 all-gather.11
  209.5 32.0 all-gather.9
  249.2 51.7 all-gather.15

commit v3 on v2

--- a/solution.py
+++ b/solution.py
@@ -40,10 +40,17 @@
     return lax.ppermute(block, ALL, pairs)
 
 
-def ctx_gather(block):
-    for phase in range(2):
-        block = jnp.stack([block] + [shift_plane(block, phase, -step) for step in range(1, SIDE)])
-    return block
+def direct_ring(block, phase):
+    others = [shift_plane(block, phase, -step) for step in range(1, SIDE)]
+    return jnp.stack([block] + others)
+
+
+def halves_ring(block, phase):
+    half = block.shape[0] // 2
+    before = shift_plane(block, phase, 1)
+    after = shift_plane(block, phase, -1)
+    far = [shift_plane(before[:half], phase, 1), shift_plane(after[half:], phase, -1)]
+    return [block, after, *far, before]
 
 
 def group_gather(block):
@@ -169,24 +176,45 @@
         ).astype(BF16)
 
 
-def out_proj_kernel(rows_ref, weight_ref, *refs):
-    out_ref, row_buf, weight_buf, sems = refs[-4:]
+def out_proj_kernel(place_ref, *refs):
+    piece_refs, weight_ref, out_ref, row_buf, weight_buf, sems = refs[:5], *refs[5:]
     members, columns, depth = weight_ref.shape
-    copies = start_copies(
-        [
-            [rows_ref.at[:, :, pl.ds(p * depth, depth)] for p in range(members)],
-            [weight_ref.at[p] for p in range(members)],
-        ],
-        [row_buf, weight_buf],
-        sems,
-    )
-    total = jnp.zeros((rows_ref.shape[0] * rows_ref.shape[1], columns), F32)
+    copies = []
     for place in range(members):
-        for copy in copies:
-            copy[place].wait()
+        part = pl.ds(place * depth, depth)
+        group = [pltpu.make_async_copy(weight_ref.at[place], weight_buf.at[place], sems.at[place, 0])]
+        first = 0
+        for n, ref in enumerate(piece_refs):
+            count = ref.shape[0]
+            group.append(
+                pltpu.make_async_copy(
+                    ref.at[:, :, part],
+                    row_buf.at[place, pl.ds(first, count)],
+                    sems.at[place, n + 1],
+                )
+            )
+            first += count
+        for copy in group:
+            copy.start()
+        copies.append(group)
+    tokens = out_ref.shape[1]
+    total = jnp.zeros((SIDE * SIDE * tokens, columns), F32)
+    for place in range(members):
+        for copy in copies[place]:
+            copy.wait()
         rows = row_buf[place].reshape(total.shape[0], depth)
         total = total + dot(rows, weight_buf[place], ((1,), (1,)))
-    out_ref[...] = total.astype(BF16).reshape(out_ref.shape)
+    total = total.astype(BF16)
+    core = place_ref[1]
+    for i in range(SIDE):
+        for j in range(SIDE):
+            step_x = i + core * (j - i)
+            step_y = j + core * (i - j)
+            owner = lax.rem(place_ref[2] + step_x, SIDE) * SIDE + lax.rem(
+                place_ref[3] + step_y, SIDE
+            )
+            first = (i * SIDE + j) * tokens
+            out_ref[owner] = total[first : first + tokens]
 
 
 def expert_kernel(place_ref, rows_ref, grads_ref, weight_ref, out_ref, *scratch):
@@ -228,12 +256,16 @@
     slots = rows_ref.shape[1]
     grads = hidden_ref[:slots, : 2 * hidden]
     units = hidden_ref[:slots, 2 * hidden :]
-    for place in range(members):
-        part = slice(place * slice_width, (place + 1) * slice_width)
+
+    def block(place, carry):
+        part = pl.ds(pl.multiple_of(place * slice_width, LANES), slice_width)
         both = dot(rows_ref[place], grads, ((0,), (0,)))
         gate_ref[part, :] = both[:, :hidden].astype(BF16)
         up_ref[part, :] = both[:, hidden:].astype(BF16)
         down_ref[:, part] = dot(units, grads_ref[place], ((0,), (0,))).astype(BF16)
+        return carry
+
+    lax.fori_loop(0, members, block, 0)
 
 
 def project_kernel(place_ref, hidden_ref, *refs):
@@ -304,17 +336,13 @@
     def shape(*dims):
         return jax.ShapeDtypeStruct(dims, BF16)
 
-    places = jnp.stack([place_z, core]).astype(jnp.int32)
+    places = jnp.stack([place_z, core, plane_x, plane_y]).astype(jnp.int32)
 
     out_weight = group_gather(w_out.T)
     block = (slice_width, 3 * hidden_width)
     weight_blocks, *weight_pairs = call(
         prepare_kernel, [shape(8, *block)] + [shape(2, *block)] * SIDE, 1
     )(places, w_down[0], w_gate[0], w_up[0])
-
-    residual_part = lax.all_to_all(
-        residual.reshape(group_count, part_tokens, slice_width), GROUP, 0, 0, tiled=True
-    )
 
     chosen = expert_ids.reshape(-1)
     pair_range = jnp.arange(token_count * top_count, dtype=jnp.int32)
@@ -342,9 +370,7 @@
     slice_weights = group_exchange(weight_pairs)
 
     half = token_count // 2
-    own_keys = ctx_gather(lax.dynamic_slice_in_dim(latent, core * half, half, 0))
-    own_keys = own_keys.reshape(ctx_count * half, latent_width)
-    other_keys = swap_core(own_keys)
+    own_keys = lax.dynamic_slice_in_dim(latent, core * half, half, 0)
     own_frames = lax.dynamic_slice_in_dim(frames, ctx_place * token_count, token_count)
     frame_grid = frames.reshape(SIDE, SIDE, 2, half)
     frame_grid = roll_lead(roll_lead(frame_grid, plane_x, 0), plane_y, 1)
@@ -355,6 +381,13 @@
         jnp.concatenate([by_x[0].reshape(-1), by_y[1].reshape(-1)]),
         jnp.concatenate([by_y[1].reshape(-1), by_x[0].reshape(-1)]),
     )
+    own_keys = direct_ring(own_keys, 0)
+    own_keys, key_frames, own_frames = lax.optimization_barrier(
+        (own_keys, key_frames[None], own_frames[:, None])
+    )
+    own_keys = direct_ring(own_keys, 1)
+    own_keys = own_keys.reshape(ctx_count * half, latent_width)
+    other_keys = swap_core(own_keys)
     heads = 4
     head_out = pl.pallas_call(
         functools.partial(attend_kernel, latent_width ** (-0.5)),
@@ -370,22 +403,29 @@
         ],
         out_specs=pl.BlockSpec((token_count, heads * value_width), lambda h: (0, h)),
         name="attend",
-    )(queries, own_keys, other_keys, key_frames[None], own_frames[:, None], w_uv)
+    )(queries, own_keys, other_keys, key_frames, own_frames, w_uv)
     head_out = head_out.reshape(group_count, part_tokens, head_count * value_width)
 
-    head_part = lax.all_to_all(head_out, GROUP, 0, 0, tiled=True)
-    head_part = jnp.transpose(head_part, (1, 0, 2)).reshape(part_tokens, -1)
-    all_heads = lax.all_gather(head_part, "ctx", axis=0)
+    head_width = head_count * value_width
+    exchange = jnp.concatenate(
+        [head_out, residual.reshape(group_count, part_tokens, slice_width)], 2
+    )
+    exchange = lax.all_to_all(exchange, GROUP, 0, 0, tiled=True)
+    exchange = jnp.transpose(exchange, (1, 0, 2))
+    head_part = exchange[:, :, :head_width].reshape(part_tokens, -1)
+    residual_part = exchange[:, :, head_width:].reshape(part_tokens, model_width)
+    pieces = halves_ring(direct_ring(head_part, 0), 1)
     columns = call(
         out_proj_kernel,
         shape(ctx_count, part_tokens, column_width),
+        1,
         whole=0,
-        scratch_shapes=buffers(
-            (group_count, ctx_count, part_tokens, head_count * value_width),
-            (group_count, column_width, head_count * value_width),
-        ),
-    )(all_heads, out_weight, residual_part, grad_rows, weight_blocks)
-    residual_part = jnp.transpose(residual_part, (1, 0, 2)).reshape(part_tokens, model_width)
+        scratch_shapes=[
+            pltpu.VMEM((group_count, ctx_count, part_tokens, head_width), BF16),
+            pltpu.VMEM((group_count, column_width, head_width), BF16),
+            pltpu.SemaphoreType.DMA((group_count, len(pieces) + 1)),
+        ],
+    )(places, *pieces, out_weight)
     columns = to_experts(columns)
     attn_part = jnp.transpose(columns, (1, 0, 2)).reshape(part_tokens, model_width)
     pre_part = (residual_part.astype(F32) + attn_part.astype(F32)).astype(BF16)

time: 373 us -> 340 us (0.912)
  waiting for transfers between devices: 203 us -> 158 us
  starting transfers between devices: 44 us -> 57 us
  blocking collectives: 44.6 us -> 34.3 us
  local copies, waits for them, and re-layouts: 10.7 us -> 14.5 us
    all_gather x4, waiting for transfers between devices: 79.6 us -> 25.8 us  [group_gather(): return lax.all_gather(block, GROUP, axis=0)]
    ppermute x6 -> x13, waiting for transfers between devices: 13 us -> 32.1 us  [shift_plane(): return lax.ppermute(block, ALL, pairs)]
    all_to_all x2 -> x1, blocking collectives: 32.3 us -> 14.5 us  [to_experts(): return lax.all_to_all(rows, 'ctx', split_axis=0, concat_axis=0, tiled=True)]
    all_gather x1 -> x0, waiting for transfers between devices: 14.2 us -> none  [per_device(): all_heads = lax.all_gather(head_part, 'ctx', axis=0)]
    ppermute x6 -> x13, starting transfers between devices: 8.27 us -> 16.6 us  [shift_plane(): return lax.ppermute(block, ALL, pairs)]
    all_to_all x2 -> x3, starting transfers between devices: 13.1 us -> 20.7 us  [to_experts(): return lax.all_to_all(rows, 'ctx', split_axis=0, concat_axis=0, tiled=True)]
    all_to_all x1, blocking collectives: 12.3 us -> 19.8 us  [per_device(): exchange = lax.all_to_all(exchange, GROUP, 0, 0, tiled=True)]
    all_to_all x1 -> x0, starting transfers between devices: 6.08 us -> none  [per_device(): lax.all_to_all(residual.reshape(group_count, part_tokens, slice_width), G...]
  transfers between devices with their start and end apart: 23 -> 29, of which waited for: 17 -> 19; matrix products, arithmetic and copies ran while one was open for 2% -> 4% of each run, Pallas kernels for 6% -> 10%
where the time goes in v3:
time: 340 us; the launch traced here: 338 us
  waiting for transfers between devices  158 us (46%)
  starting transfers between devices  57 us (17%)
  Pallas kernels  49.4 us (15%)
  blocking collectives  34.3 us (10%)
  local copies, waits for them, and re-layouts  14.5 us (4%)
  between operations  14.2 us (4%)
  other arithmetic  7.46 us (2%)
    ppermute x3, waiting for transfers between devices, shift_z(): lax.ppermute(block, GROUP, [(g, (g + 2 * step) % 8) for g in range(8)])  66.3 us
    pallas_call x5, Pallas kernels, run(): pl.pallas_call(kernel, out_shape=outs, in_specs=[pl.BlockSpec(memory_spac...  39.9 us
    ppermute x13, waiting for transfers between devices, shift_plane(): return lax.ppermute(block, ALL, pairs)  32.1 us
    all_gather x4, waiting for transfers between devices, group_gather(): return lax.all_gather(block, GROUP, axis=0)  25.8 us
    all_to_all x3, waiting for transfers between devices, to_experts(): return lax.all_to_all(rows, 'ctx', split_axis=0, concat_axis=0, tiled=True)  24.9 us
    all_to_all x3, starting transfers between devices, to_experts(): return lax.all_to_all(rows, 'ctx', split_axis=0, concat_axis=0, tiled=True)  20.7 us
    all_to_all x1, blocking collectives, per_device(): exchange = lax.all_to_all(exchange, GROUP, 0, 0, tiled=True)  19.8 us
    ppermute x13, starting transfers between devices, shift_plane(): return lax.ppermute(block, ALL, pairs)  16.6 us
  transfers between devices with their start and end apart: 29, of which 19 were waited for; matrix products, arithmetic and copies ran while one was open for 4% of the time, Pallas kernels for 10%

profile of v3, /device:TPU:1, one launch (start us, length us, event | category | flops | bytes accessed | tf_op | source)
XLA Modules:
  0.0 337.9 jit_solution(901448158631382046)
XLA Ops:
  7.2 0.7 all-gather.11.cloned.1.call-update
  7.9 0.8 copy.79
  9.2 0.7 convert_reduce_fusion.2
  10.0 0.7 convert_divide_fusion
  10.7 0.7 multiply_add_fusion
  11.5 1.2 fusion
  12.8 1.0 all_to_all.29
  13.8 7.6 %all-to-all-start.4 = ((bf16[16,20,896]{2,1,0:T(8,128)(2,1)}), bf16[16,20,896]{2,1,0:T(8,128)(2,1)S(1)}, u32[]{:S(2)}, u32[]{:S(2)}) async-start(bf16[16,20,896]{2,1,0:T(8,128)(2,1)} %all_to_all.29), calls=%async_computation.4 | async-start | bytes 1376256 | tf_op jit(solution)/shard_map/all_to_all | solution.py:365
  21.4 2.9 collective-permute-start.1
  24.4 0.9 collective-permute-start
  25.3 0.6 collective-permute-start.2
  26.0 7.1 %all-to-all-done.4 = bf16[16,20,896]{2,1,0:T(8,128)(2,1)S(1)} async-done(((bf16[16,20,896]{2,1,0:T(8,128)(2,1)}), bf16[16,20,896]{2,1,0:T(8,128)(2,1)S(1)}, u32[]{:S(2)}, u32[]{:S(2)}) %all-to-all-start.4) | async-done | bytes 573472 | tf_op jit(solution)/shard_map/all_to_all | solution.py:365
  33.1 0.9 all_gather.28
  34.3 0.6 broadcast_select_fusion.key_frame_ref
  35.4 2.4 collective-permute-start.4
  37.8 1.2 collective-permute-start.3
  39.0 3.0 collective-permute-done.5
  42.0 2.5 collective-permute-done.4
  44.4 1.0 collective-permute-done.3
  45.5 5.0 %collective-permute-start.6 = (bf16[1024,512]{1,0:T(8,128)(2,1)S(1)}, bf16[1024,512]{1,0:T(8,128)(2,1)S(1)}, u32[]{:S(2)}, u32[]{:S(2)}) collective-permute-start(bf16[1024,512]{1,0:T(8,128)(2,1)S(1)} %bitcast.61), channel_id=1, source_target_pairs={{0,1},{1,0},{2,3},{3,2},{4,5},{5,4},{6,7},{7,6},{8,9},{9,8},{10,11... | collective-permute-start | bytes 3145736 | tf_op jit(solution)/shard_map/ppermute | solution.py:27
  50.5 0.7 copy.72.own_frame_ref
  51.3 1.7 collective-permute-done.6.far_ref
  53.0 1.0 copy-done.14
  54.0 9.4 %attend.1 = bf16[128,1024]{1,0:T(8,128)(2,1)} custom-call(bf16[128,4096]{1,0:T(8,128)(2,1)} %q_ref.1, bf16[1024,512]{1,0:T(8,128)(2,1)} %bitcast.62, bf16[1024,512]{1,0:T(8,128)(2,1)} %copy-done.14, s32[1,2048]{1,0:T(1,128)} %broadcast_select_fusion.key_frame_ref, s32[128,1]{1,0:T(8,128)} %copy.72.own_frame_ref, bf16[8,512,128]{2,1,0:T(8,128)(2,1)} %uv_ref.1), custom_call_target="tpu_custom_call" | custom-call | tf_op jit(solution)/shard_map/attend/pallas_call | solution.py:392
  63.4 1.0 pad_maximum_fusion.2
  64.4 19.8 %all_to_all.38 = bf16[8,16,1920]{2,1,0:T(8,128)(2,1)S(1)} all-to-all(bf16[8,16,1920]{2,1,0:T(8,128)(2,1)S(1)} %pad_maximum_fusion.2), channel_id=1, replica_groups=mesh['ctx'=16,'role'=2,'exp'=4] {'role','exp'}, dimensions={0} | all-to-all | bytes 983040 | tf_op jit(solution)/shard_map/all_to_all | solution.py:413
  84.3 0.8 copy-done.6
  85.4 2.7 collective-permute-start.8
  88.2 4.0 %collective-permute-done.9 = bf16[16,8192]{1,0:T(8,128)(2,1)S(1)} collective-permute-done((bf16[16,8192]{1,0:T(8,128)(2,1)S(1)}, bf16[16,8192]{1,0:T(8,128)(2,1)S(1)}, u32[]{:S(2)}, u32[]{:S(2)}) %collective-permute-start.9) | collective-permute-done | bytes 262176 | tf_op jit(solution)/shard_map/ppermute | solution.py:40
  92.2 2.5 collective-permute-done.8
  94.7 0.9 collective-permute-done.7
  95.9 2.7 collective-permute-start.10
  98.5 12.5 %collective-permute-done.11.refs_4_ = bf16[4,16,8192]{2,1,0:T(8,128)(2,1)S(1)} collective-permute-done((bf16[4,16,8192]{2,1,0:T(8,128)(2,1)S(1)}, bf16[4,16,8192]{2,1,0:T(8,128)(2,1)S(1)}, u32[]{:S(2)}, u32[]{:S(2)}) %collective-permute-start.11) | collective-permute-done | bytes 1048608 | tf_op jit(solution)/shard_map/ppermute | solution.py:40
  111.0 0.9 slice.76
  111.9 0.9 slice.77
  112.8 2.7 collective-permute-start.13
  115.5 0.6 pad_add_fusion.place_ref
  116.1 5.7 %collective-permute-done.12.refs_2_ = bf16[2,16,8192]{2,1,0:T(8,128)(2,1)} collective-permute-done((bf16[2,16,8192]{2,1,0:T(8,128)(2,1)}, bf16[2,16,8192]{2,1,0:T(8,128)(2,1)}, u32[]{:S(2)}, u32[]{:S(2)}) %collective-permute-start.12) | collective-permute-done | bytes 524320 | tf_op jit(solution)/shard_map/ppermute | solution.py:40
  121.9 6.5 %shard_map.164 = bf16[16,16,448]{2,1,0:T(8,128)(2,1)} custom-call(s32[4]{0:T(128)} %pad_add_fusion.place_ref, bf16[4,16,8192]{2,1,0:T(8,128)(2,1)} %copy-done.2, bf16[4,16,8192]{2,1,0:T(8,128)(2,1)} %copy-done.5, bf16[2,16,8192]{2,1,0:T(8,128)(2,1)} %collective-permute-done.12.refs_2_, bf16[2,16,8192]{2,1,0:T(8,128)(2,1)} %collective-permute-done.13.refs_3_, ...), custom_call_target="tpu_custom_call" | custom-call | tf_op jit(solution)/shard_map/pallas_call | solution.py:104
  128.5 6.6 %all-to-all-start.1 = ((bf16[16,16,448]{2,1,0:T(8,128)(2,1)}), bf16[16,16,448]{2,1,0:T(8,128)(2,1)S(1)}, u32[]{:S(2)}, u32[]{:S(2)}) async-start(bf16[16,16,448]{2,1,0:T(8,128)(2,1)} %shard_map.164), calls=%async_computation.1 | async-start | bytes 524288 | tf_op jit(solution)/shard_map/all_to_all | solution.py:365
  135.2 7.2 %all-to-all-done.1 = bf16[16,16,448]{2,1,0:T(8,128)(2,1)S(1)} async-done(((bf16[16,16,448]{2,1,0:T(8,128)(2,1)}), bf16[16,16,448]{2,1,0:T(8,128)(2,1)S(1)}, u32[]{:S(2)}, u32[]{:S(2)}) %all-to-all-start.1) | async-done | bytes 229408 | tf_op jit(solution)/shard_map/all_to_all | solution.py:365
  142.9 1.2 fusion.37
  144.5 0.9 copy.78
  145.4 8.8 %all-to-all-start.2 = ((bf16[8,16,1024]{2,1,0:T(8,128)(2,1)}), bf16[8,16,1024]{2,1,0:T(8,128)(2,1)S(1)}, u32[]{:S(2)}, u32[]{:S(2)}) async-start(bf16[8,16,1024]{2,1,0:T(8,128)(2,1)} %copy.78), calls=%async_computation.2 | async-start | bytes 524288 | tf_op jit(solution)/shard_map/all_to_all | solution.py:442
  154.2 0.8 dynamic_slice.19
  155.0 5.7 %all-to-all-done.2 = bf16[8,16,1024]{2,1,0:T(8,128)(2,1)S(1)} async-done(((bf16[8,16,1024]{2,1,0:T(8,128)(2,1)}), bf16[8,16,1024]{2,1,0:T(8,128)(2,1)S(1)}, u32[]{:S(2)}, u32[]{:S(2)}) %all-to-all-start.2) | async-done | bytes 262176 | tf_op jit(solution)/shard_map/all_to_all | solution.py:442
  161.3 14.5 %all_to_all.39 = bf16[16,20,896]{2,1,0:T(8,128)(2,1)S(1)} all-to-all(bf16[16,20,896]{2,1,0:T(8,128)(2,1)S(1)} %all_to_all.27), channel_id=1, replica_groups=mesh['ctx'=16,'role'=2,'exp'=4] {'ctx'}, dimensions={0} | all-to-all | bytes 1146880 | tf_op jit(solution)/shard_map/all_to_all | solution.py:365
  175.8 1.0 all_gather.26
  176.8 7.7 %shard_map.165 = (bf16[8,896,384]{2,1,0:T(8,128)(2,1)}, bf16[2,896,384]{2,1,0:T(8,128)(2,1)}, bf16[2,896,384]{2,1,0:T(8,128)(2,1)}, bf16[2,896,384]{2,1,0:T(8,128)(2,1)}, bf16[2,896,384]{2,1,0:T(8,128)(2,1)}) custom-call(s32[4]{0:T(128)} %pad_add_fusion.place_ref, bf16[128,7168]{1,0:T(8,128)(2,1)} %bitcast.71, bf16[7168,128]{1,0:T(8,128)(2,1)} %bitcast.72, ...), custom_call_target="tpu_custom_call" | custom-call | tf_op jit(solution)/shard_map/pallas_call | solution.py:104
  184.5 25.0 %all-gather.7.cloned.1.call-done.rows_ref = bf16[8,320,896]{2,1,0:T(8,128)(2,1)} async-done(((bf16[1,320,896]{2,1,0:T(8,128)(2,1)}), bf16[8,320,896]{2,1,0:T(8,128)(2,1)}) %all-gather.7.cloned.1.call-update) | async-done | bytes 4587536 | tf_op jit(solution)/shard_map/all_gather | solution.py:57
  209.4 7.7 %shard_map.166.hidden_ref = bf16[328,384]{1,0:T(8,128)(2,1)} custom-call(s32[4]{0:T(128)} %pad_add_fusion.place_ref, bf16[8,320,896]{2,1,0:T(8,128)(2,1)} %all-gather.7.cloned.1.call-done.rows_ref, bf16[8,320,896]{2,1,0:T(8,128)(2,1)} %all-gather.9.cloned.1.call-done.grads_ref, bf16[8,896,384]{2,1,0:T(8,128)(2,1)} %get-tuple-element.19.weight_ref), custom_call_target="tpu_custom_call" | custom-call | tf_op jit(solution)/shard_map/pallas_call | solution.py:104
  217.7 1.4 collective-permute-start.17
  219.5 1.1 collective-permute-start.14
  220.6 35.1 %collective-permute-done.15.refs_2_ = bf16[2,896,384]{2,1,0:T(8,128)(2,1)S(1)} collective-permute-done((bf16[2,896,384]{2,1,0:T(8,128)(2,1)}, bf16[2,896,384]{2,1,0:T(8,128)(2,1)S(1)}, u32[]{:S(2)}, u32[]{:S(2)}) %collective-permute-start.15) | collective-permute-done | bytes 1376288 | tf_op jit(solution)/shard_map/ppermute | solution.py:23
  255.8 1.7 collective-permute-start.16
  257.6 31.2 %collective-permute-done.19.refs_6_ = bf16[2,896,384]{2,1,0:T(8,128)(2,1)S(1)} collective-permute-done((bf16[2,896,384]{2,1,0:T(8,128)(2,1)S(1)}, bf16[2,896,384]{2,1,0:T(8,128)(2,1)S(1)}, u32[]{:S(2)}, u32[]{:S(2)}) %collective-permute-start.19) | collective-permute-done | bytes 1376288 | tf_op jit(solution)/shard_map/ppermute | solution.py:23
  290.8 1.1 copy-done.13
  292.2 0.9 all-gather.13.cloned.1.call-done
  293.1 7.3 %shard_map.167 = bf16[16,20,1920]{2,1,0:T(8,128)(2,1)} custom-call(s32[4]{0:T(128)} %pad_add_fusion.place_ref, bf16[8,328,384]{2,1,0:T(8,128)(2,1)} %bitcast.68, bf16[2,896,384]{2,1,0:T(8,128)(2,1)} %get-tuple-element.20.refs_0_, bf16[2,896,384]{2,1,0:T(8,128)(2,1)} %copy-done.11, bf16[2,896,384]{2,1,0:T(8,128)(2,1)} %copy-done.8, ...), custom_call_target="tpu_custom_call" | custom-call | tf_op jit(solution)/shard_map/pallas_call | solution.py:104
  300.4 6.5 %all-to-all-start.5 = ((bf16[16,20,1920]{2,1,0:T(8,128)(2,1)}), bf16[16,20,1920]{2,1,0:T(8,128)(2,1)S(1)}, u32[]{:S(2)}, u32[]{:S(2)}) async-start(bf16[16,20,1920]{2,1,0:T(8,128)(2,1)} %shard_map.167), calls=%async_computation.5 | async-start | bytes 2949120 | tf_op jit(solution)/shard_map/all_to_all | solution.py:365
  306.9 10.8 %shard_map.168 = (bf16[7168,128]{1,0:T(8,128)(2,1)}, bf16[7168,128]{1,0:T(8,128)(2,1)}, bf16[128,7168]{1,0:T(8,128)(2,1)}) custom-call(bf16[8,320,896]{2,1,0:T(8,128)(2,1)} %all-gather.7.cloned.1.call-done.rows_ref, bf16[8,320,896]{2,1,0:T(8,128)(2,1)} %all-gather.9.cloned.1.call-done.grads_ref, bf16[328,384]{1,0:T(8,128)(2,1)} %shard_map.166.hidden_ref), custom_call_target="tpu_custom_call" | custom-call | tf_op jit(solution)/shard_map/pallas_call | solution.py:104
  317.7 10.6 %all-to-all-done.5 = bf16[16,20,1920]{2,1,0:T(8,128)(2,1)S(1)} async-done(((bf16[16,20,1920]{2,1,0:T(8,128)(2,1)}), bf16[16,20,1920]{2,1,0:T(8,128)(2,1)S(1)}, u32[]{:S(2)}, u32[]{:S(2)}) %all-to-all-start.5) | async-done | bytes 1228832 | tf_op jit(solution)/shard_map/all_to_all | solution.py:365
  329.3 1.0 fusion.3
  330.5 0.9 fusion.14
  (110 shorter events, 8.9 us)
Async XLA Ops:
  7.2 14.3 %copy-start = (bf16[128,512]{1,0:T(8,128)(2,1)S(1)}, bf16[128,512]{1,0:T(8,128)(2,1)}, u32[]{:S(2)}) copy-start(bf16[128,512]{1,0:T(8,128)(2,1)} %param.14) | copy-start | bytes 393220
  7.2 114.7 %all-gather.11.cloned.1.call-start = ((), (), s32[]{:S(2)}) async-start(), calls=%async_computation.8 | async-start | bytes 8257536 | tf_op jit(solution)/shard_map/all_gather | solution.py:57
  12.8 13.1 %copy-start.17 = (s32[2048]{0:T(1024)S(1)}, s32[2048]{0:T(1024)}, u32[]{:S(2)}) copy-start(s32[2048]{0:T(1024)} %param.15) | copy-start | bytes 24580
  13.8 19.3 %all-to-all-start.4 = ((bf16[16,20,896]{2,1,0:T(8,128)(2,1)}), bf16[16,20,896]{2,1,0:T(8,128)(2,1)S(1)}, u32[]{:S(2)}, u32[]{:S(2)}) async-start(bf16[16,20,896]{2,1,0:T(8,128)(2,1)} %all_to_all.29), calls=%async_computation.4 | async-start | bytes 1376256 | tf_op jit(solution)/shard_map/all_to_all | solution.py:365
  21.3 163.1 %all-gather.9.cloned.1.call-start = ((), (), s32[]{:S(2)}) async-start(), calls=%async_computation.7 | async-start | bytes 5160960 | tf_op jit(solution)/shard_map/all_gather | solution.py:57
  21.4 13.5 %collective-permute-start.1 = (bf16[64,512]{1,0:T(8,128)(2,1)S(1)}, bf16[64,512]{1,0:T(8,128)(2,1)S(1)}, u32[]{:S(2)}, u32[]{:S(2)}) collective-permute-start(bf16[64,512]{1,0:T(8,128)(2,1)S(1)} %constant_dynamic-slice_fusion), channel_id=1, source_target_pairs={{0,16},{1,65},{2,18},{3,67},{4,20},{5,69},{6,22},{7,71},{8,24},{9,... | collective-permute-start | bytes 196616 | tf_op jit(solution)/shard_map/ppermute | solution.py:40
  24.4 10.6 %collective-permute-start = (bf16[64,512]{1,0:T(8,128)(2,1)S(1)}, bf16[64,512]{1,0:T(8,128)(2,1)S(1)}, u32[]{:S(2)}, u32[]{:S(2)}) collective-permute-start(bf16[64,512]{1,0:T(8,128)(2,1)S(1)} %constant_dynamic-slice_fusion), channel_id=1, source_target_pairs={{0,24},{1,97},{2,26},{3,99},{4,28},{5,101},{6,30},{7,103},{8,0},{9... | collective-permute-start | bytes 196616 | tf_op jit(solution)/shard_map/ppermute | solution.py:40
  25.3 9.7 %collective-permute-start.2 = (bf16[64,512]{1,0:T(8,128)(2,1)S(1)}, bf16[64,512]{1,0:T(8,128)(2,1)S(1)}, u32[]{:S(2)}, u32[]{:S(2)}) collective-permute-start(bf16[64,512]{1,0:T(8,128)(2,1)S(1)} %constant_dynamic-slice_fusion), channel_id=1, source_target_pairs={{0,8},{1,33},{2,10},{3,35},{4,12},{5,37},{6,14},{7,39},{8,16},{9,4... | collective-permute-start | bytes 196616 | tf_op jit(solution)/shard_map/ppermute | solution.py:40
  35.0 6.9 %collective-permute-start.5 = (bf16[4,64,512]{2,1,0:T(8,128)(2,1)S(1)}, bf16[4,64,512]{2,1,0:T(8,128)(2,1)S(1)}, u32[]{:S(2)}, u32[]{:S(2)}) collective-permute-start(bf16[4,64,512]{2,1,0:T(8,128)(2,1)S(1)} %pad_maximum_fusion.3), channel_id=1, source_target_pairs={{0,32},{1,9},{2,34},{3,11},{4,36},{5,13},{6,38},{7,15},{8,40},{9,1... | collective-permute-start | bytes 786440 | tf_op jit(solution)/shard_map/ppermute | solution.py:40
  35.4 9.0 %collective-permute-start.4 = (bf16[4,64,512]{2,1,0:T(8,128)(2,1)S(1)}, bf16[4,64,512]{2,1,0:T(8,128)(2,1)S(1)}, u32[]{:S(2)}, u32[]{:S(2)}) collective-permute-start(bf16[4,64,512]{2,1,0:T(8,128)(2,1)S(1)} %pad_maximum_fusion.3), channel_id=1, source_target_pairs={{0,64},{1,17},{2,66},{3,19},{4,68},{5,21},{6,70},{7,23},{8,72},{9,... | collective-permute-start | bytes 786440 | tf_op jit(solution)/shard_map/ppermute | solution.py:40
  37.8 7.6 %collective-permute-start.3 = (bf16[4,64,512]{2,1,0:T(8,128)(2,1)S(1)}, bf16[4,64,512]{2,1,0:T(8,128)(2,1)S(1)}, u32[]{:S(2)}, u32[]{:S(2)}) collective-permute-start(bf16[4,64,512]{2,1,0:T(8,128)(2,1)S(1)} %pad_maximum_fusion.3), channel_id=1, source_target_pairs={{0,96},{1,25},{2,98},{3,27},{4,100},{5,29},{6,102},{7,31},{8,104},... | collective-permute-start | bytes 786440 | tf_op jit(solution)/shard_map/ppermute | solution.py:40
  45.5 7.5 %copy-start.3 = (bf16[4,4,64,512]{3,2,1,0:T(8,128)(2,1)}, bf16[4,4,64,512]{3,2,1,0:T(8,128)(2,1)S(1)}, u32[]{:S(2)}) copy-start(bf16[4,4,64,512]{3,2,1,0:T(8,128)(2,1)S(1)} %pad_maximum_fusion) | copy-start | bytes 3145732
  45.5 7.5 %collective-permute-start.6 = (bf16[1024,512]{1,0:T(8,128)(2,1)S(1)}, bf16[1024,512]{1,0:T(8,128)(2,1)S(1)}, u32[]{:S(2)}, u32[]{:S(2)}) collective-permute-start(bf16[1024,512]{1,0:T(8,128)(2,1)S(1)} %bitcast.61), channel_id=1, source_target_pairs={{0,1},{1,0},{2,3},{3,2},{4,5},{5,4},{6,7},{7,6},{8,9},{9,8},{10,11... | collective-permute-start | bytes 3145736 | tf_op jit(solution)/shard_map/ppermute | solution.py:27
  51.3 12.2 %copy-start.16 = (bf16[128,896]{1,0:T(8,128)(2,1)S(1)}, bf16[128,896]{1,0:T(8,128)(2,1)}, u32[]{:S(2)}) copy-start(bf16[128,896]{1,0:T(8,128)(2,1)} %param.18) | copy-start | bytes 688132
  53.0 1.0 copy-start.14
  84.3 0.8 copy-start.6
  85.3 6.9 %collective-permute-start.9 = (bf16[16,8192]{1,0:T(8,128)(2,1)S(1)}, bf16[16,8192]{1,0:T(8,128)(2,1)S(1)}, u32[]{:S(2)}, u32[]{:S(2)}) collective-permute-start(bf16[16,8192]{1,0:T(8,128)(2,1)S(1)} %bitcast.77), channel_id=1, source_target_pairs={{0,8},{1,33},{2,10},{3,35},{4,12},{5,37},{6,14},{7,39},{8,16},{9,4... | collective-permute-start | bytes 786440 | tf_op jit(solution)/shard_map/ppermute | solution.py:40
  85.4 9.3 %collective-permute-start.8 = (bf16[16,8192]{1,0:T(8,128)(2,1)S(1)}, bf16[16,8192]{1,0:T(8,128)(2,1)S(1)}, u32[]{:S(2)}, u32[]{:S(2)}) collective-permute-start(bf16[16,8192]{1,0:T(8,128)(2,1)S(1)} %bitcast.78), channel_id=1, source_target_pairs={{0,16},{1,65},{2,18},{3,67},{4,20},{5,69},{6,22},{7,71},{8,24},{9,... | collective-permute-start | bytes 786440 | tf_op jit(solution)/shard_map/ppermute | solution.py:40
  88.1 7.5 %collective-permute-start.7 = (bf16[16,8192]{1,0:T(8,128)(2,1)S(1)}, bf16[16,8192]{1,0:T(8,128)(2,1)S(1)}, u32[]{:S(2)}, u32[]{:S(2)}) collective-permute-start(bf16[16,8192]{1,0:T(8,128)(2,1)S(1)} %bitcast.79), channel_id=1, source_target_pairs={{0,24},{1,97},{2,26},{3,99},{4,28},{5,101},{6,30},{7,103},{8,0},{9... | collective-permute-start | bytes 786440 | tf_op jit(solution)/shard_map/ppermute | solution.py:40
  95.8 26.2 %copy-start.2 = (bf16[4,16,8192]{2,1,0:T(8,128)(2,1)}, bf16[4,16,8192]{2,1,0:T(8,128)(2,1)S(1)}, u32[]{:S(2)}) copy-start(bf16[4,16,8192]{2,1,0:T(8,128)(2,1)S(1)} %pad_maximum_fusion.1.refs_0_) | copy-start | bytes 3145732
  95.8 15.2 %collective-permute-start.11 = (bf16[4,16,8192]{2,1,0:T(8,128)(2,1)S(1)}, bf16[4,16,8192]{2,1,0:T(8,128)(2,1)S(1)}, u32[]{:S(2)}, u32[]{:S(2)}) collective-permute-start(bf16[4,16,8192]{2,1,0:T(8,128)(2,1)S(1)} %pad_maximum_fusion.1.refs_0_), channel_id=1, source_target_pairs={{0,32},{1,9},{2,34},{3,11},{4,36},{5,13},{6,38},{7,15},{8,40},{9,1... | collective-permute-start | bytes 3145736 | tf_op jit(solution)/shard_map/ppermute | solution.py:40
  95.9 16.1 %collective-permute-start.10 = (bf16[4,16,8192]{2,1,0:T(8,128)(2,1)S(1)}, bf16[4,16,8192]{2,1,0:T(8,128)(2,1)S(1)}, u32[]{:S(2)}, u32[]{:S(2)}) collective-permute-start(bf16[4,16,8192]{2,1,0:T(8,128)(2,1)S(1)} %pad_maximum_fusion.1.refs_0_), channel_id=1, source_target_pairs={{0,96},{1,25},{2,98},{3,27},{4,100},{5,29},{6,102},{7,31},{8,104},... | collective-permute-start | bytes 3145736 | tf_op jit(solution)/shard_map/ppermute | solution.py:40
  111.0 10.9 %copy-start.4 = (bf16[4,16,8192]{2,1,0:T(8,128)(2,1)}, bf16[4,16,8192]{2,1,0:T(8,128)(2,1)S(1)}, u32[]{:S(2)}) copy-start(bf16[4,16,8192]{2,1,0:T(8,128)(2,1)S(1)} %collective-permute-done.11.refs_4_) | copy-start | bytes 3145732
  111.9 9.9 %collective-permute-start.12 = (bf16[2,16,8192]{2,1,0:T(8,128)(2,1)}, bf16[2,16,8192]{2,1,0:T(8,128)(2,1)}, u32[]{:S(2)}, u32[]{:S(2)}) collective-permute-start(bf16[2,16,8192]{2,1,0:T(8,128)(2,1)} %slice.76), channel_id=1, source_target_pairs={{0,32},{1,9},{2,34},{3,11},{4,36},{5,13},{6,38},{7,15},{8,40},{9,1... | collective-permute-start | bytes 1572872 | tf_op jit(solution)/shard_map/ppermute | solution.py:40
  111.9 10.0 %copy-start.5 = (bf16[4,16,8192]{2,1,0:T(8,128)(2,1)}, bf16[4,16,8192]{2,1,0:T(8,128)(2,1)S(1)}, u32[]{:S(2)}) copy-start(bf16[4,16,8192]{2,1,0:T(8,128)(2,1)S(1)} %collective-permute-done.10.refs_1_) | copy-start | bytes 3145732
  112.8 9.1 %collective-permute-start.13 = (bf16[2,16,8192]{2,1,0:T(8,128)(2,1)}, bf16[2,16,8192]{2,1,0:T(8,128)(2,1)}, u32[]{:S(2)}, u32[]{:S(2)}) collective-permute-start(bf16[2,16,8192]{2,1,0:T(8,128)(2,1)} %slice.77), channel_id=1, source_target_pairs={{0,96},{1,25},{2,98},{3,27},{4,100},{5,29},{6,102},{7,31},{8,104},... | collective-permute-start | bytes 1572872 | tf_op jit(solution)/shard_map/ppermute | solution.py:40
  128.5 14.0 %all-to-all-start.1 = ((bf16[16,16,448]{2,1,0:T(8,128)(2,1)}), bf16[16,16,448]{2,1,0:T(8,128)(2,1)S(1)}, u32[]{:S(2)}, u32[]{:S(2)}) async-start(bf16[16,16,448]{2,1,0:T(8,128)(2,1)} %shard_map.164), calls=%async_computation.1 | async-start | bytes 524288 | tf_op jit(solution)/shard_map/all_to_all | solution.py:365
  145.4 15.3 %all-to-all-start.2 = ((bf16[8,16,1024]{2,1,0:T(8,128)(2,1)}), bf16[8,16,1024]{2,1,0:T(8,128)(2,1)S(1)}, u32[]{:S(2)}, u32[]{:S(2)}) async-start(bf16[8,16,1024]{2,1,0:T(8,128)(2,1)} %copy.78), calls=%async_computation.2 | async-start | bytes 524288 | tf_op jit(solution)/shard_map/all_to_all | solution.py:442
  154.2 55.3 %all-gather.7.cloned.1.call-start = ((), (), s32[]{:S(2)}) async-start(), calls=%async_computation.6 | async-start | bytes 5160960 | tf_op jit(solution)/shard_map/all_gather | solution.py:57
  176.8 116.3 %all-gather.13.cloned.1.call-start = ((), (), s32[]{:S(2)}) async-start(), calls=%async_computation.9 | async-start | bytes 2267136 | tf_op jit(solution)/shard_map/all_gather | solution.py:57
  209.4 9.7 %copy-start.18 = (bf16[2,896,384]{2,1,0:T(8,128)(2,1)S(1)}, bf16[2,896,384]{2,1,0:T(8,128)(2,1)}, u32[]{:S(2)}) copy-start(bf16[2,896,384]{2,1,0:T(8,128)(2,1)} %get-tuple-element.23) | copy-start | bytes 4128772
  209.4 10.1 %copy-start.7 = (bf16[2,896,384]{2,1,0:T(8,128)(2,1)S(1)}, bf16[2,896,384]{2,1,0:T(8,128)(2,1)}, u32[]{:S(2)}) copy-start(bf16[2,896,384]{2,1,0:T(8,128)(2,1)} %get-tuple-element.20.refs_0_) | copy-start | bytes 4128772
  217.2 38.6 %collective-permute-start.15 = (bf16[2,896,384]{2,1,0:T(8,128)(2,1)}, bf16[2,896,384]{2,1,0:T(8,128)(2,1)S(1)}, u32[]{:S(2)}, u32[]{:S(2)}) collective-permute-start(bf16[2,896,384]{2,1,0:T(8,128)(2,1)} %get-tuple-element.21), channel_id=1, source_target_pairs={{0,6},{1,7},{2,0},{3,1},{4,2},{5,3},{6,4},{7,5},{8,14},{9,15},{10,... | collective-permute-start | bytes 4128776 | tf_op jit(solution)/shard_map/ppermute | solution.py:23
  217.7 39.8 %collective-permute-start.17 = (bf16[2,896,384]{2,1,0:T(8,128)(2,1)}, bf16[2,896,384]{2,1,0:T(8,128)(2,1)S(1)}, u32[]{:S(2)}, u32[]{:S(2)}) collective-permute-start(bf16[2,896,384]{2,1,0:T(8,128)(2,1)} %get-tuple-element.22), channel_id=1, source_target_pairs={{0,4},{1,5},{2,6},{3,7},{4,0},{5,1},{6,2},{7,3},{8,12},{9,13},{10,... | collective-permute-start | bytes 4128776 | tf_op jit(solution)/shard_map/ppermute | solution.py:23
  219.1 69.7 %collective-permute-start.19 = (bf16[2,896,384]{2,1,0:T(8,128)(2,1)S(1)}, bf16[2,896,384]{2,1,0:T(8,128)(2,1)S(1)}, u32[]{:S(2)}, u32[]{:S(2)}) collective-permute-start(bf16[2,896,384]{2,1,0:T(8,128)(2,1)S(1)} %copy-done.18), channel_id=1, source_target_pairs={{0,2},{1,3},{2,4},{3,5},{4,6},{5,7},{6,0},{7,1},{8,10},{9,11},{10,... | collective-permute-start | bytes 4128776 | tf_op jit(solution)/shard_map/ppermute | solution.py:23
  219.5 69.8 %collective-permute-start.14 = (bf16[2,896,384]{2,1,0:T(8,128)(2,1)S(1)}, bf16[2,896,384]{2,1,0:T(8,128)(2,1)S(1)}, u32[]{:S(2)}, u32[]{:S(2)}) collective-permute-start(bf16[2,896,384]{2,1,0:T(8,128)(2,1)S(1)} %copy-done.7), channel_id=1, source_target_pairs={{0,1},{1,0},{2,3},{3,2},{4,5},{5,4},{6,7},{7,6},{8,9},{9,8},{10,11... | collective-permute-start | bytes 4128776 | tf_op jit(solution)/shard_map/ppermute | solution.py:27
  255.8 33.5 %copy-start.8 = (bf16[2,896,384]{2,1,0:T(8,128)(2,1)}, bf16[2,896,384]{2,1,0:T(8,128)(2,1)S(1)}, u32[]{:S(2)}) copy-start(bf16[2,896,384]{2,1,0:T(8,128)(2,1)S(1)} %collective-permute-done.15.refs_2_) | copy-start | bytes 4128772
  255.8 33.5 %collective-permute-start.16 = (bf16[2,896,384]{2,1,0:T(8,128)(2,1)S(1)}, bf16[2,896,384]{2,1,0:T(8,128)(2,1)S(1)}, u32[]{:S(2)}, u32[]{:S(2)}) collective-permute-start(bf16[2,896,384]{2,1,0:T(8,128)(2,1)S(1)} %collective-permute-done.15.refs_2_), channel_id=1, source_target_pairs={{0,1},{1,0},{2,3},{3,2},{4,5},{5,4},{6,7},{7,6},{8,9},{9,8},{10,11... | collective-permute-start | bytes 4128776 | tf_op jit(solution)/shard_map/ppermute | solution.py:27
  257.5 31.8 %copy-start.9 = (bf16[2,896,384]{2,1,0:T(8,128)(2,1)}, bf16[2,896,384]{2,1,0:T(8,128)(2,1)S(1)}, u32[]{:S(2)}) copy-start(bf16[2,896,384]{2,1,0:T(8,128)(2,1)S(1)} %collective-permute-done.17.refs_4_) | copy-start | bytes 4128772
  257.5 31.8 %collective-permute-start.18 = (bf16[2,896,384]{2,1,0:T(8,128)(2,1)S(1)}, bf16[2,896,384]{2,1,0:T(8,128)(2,1)S(1)}, u32[]{:S(2)}, u32[]{:S(2)}) collective-permute-start(bf16[2,896,384]{2,1,0:T(8,128)(2,1)S(1)} %collective-permute-done.17.refs_4_), channel_id=1, source_target_pairs={{0,1},{1,0},{2,3},{3,2},{4,5},{5,4},{6,7},{7,6},{8,9},{9,8},{10,11... | collective-permute-start | bytes 4128776 | tf_op jit(solution)/shard_map/ppermute | solution.py:27
  288.8 1.1 copy-start.10
  288.8 3.4 %collective-permute-start.20 = (bf16[2,896,384]{2,1,0:T(8,128)(2,1)S(1)}, bf16[2,896,384]{2,1,0:T(8,128)(2,1)}, u32[]{:S(2)}, u32[]{:S(2)}) collective-permute-start(bf16[2,896,384]{2,1,0:T(8,128)(2,1)S(1)} %collective-permute-done.19.refs_6_), channel_id=1, source_target_pairs={{0,1},{1,0},{2,3},{3,2},{4,5},{5,4},{6,7},{7,6},{8,9},{9,8},{10,11... | collective-permute-start | bytes 4128776 | tf_op jit(solution)/shard_map/ppermute | solution.py:27
  289.3 1.1 copy-start.11
  289.3 1.5 copy-start.12
  290.8 1.1 copy-start.13
  300.4 27.9 %all-to-all-start.5 = ((bf16[16,20,1920]{2,1,0:T(8,128)(2,1)}), bf16[16,20,1920]{2,1,0:T(8,128)(2,1)S(1)}, u32[]{:S(2)}, u32[]{:S(2)}) async-start(bf16[16,20,1920]{2,1,0:T(8,128)(2,1)} %shard_map.167), calls=%async_computation.5 | async-start | bytes 2949120 | tf_op jit(solution)/shard_map/all_to_all | solution.py:365
  328.9 1.5 copy-start.15
  329.0 2.4 copy-start.1
Sparse Core Ops, SparseCore 0:
  9.7 49.0 all-gather.10
  60.5 38.9 all-gather.8
  176.9 32.4 all-gather.6
  217.3 75.7 all-gather.12

commit v4 on v3

--- a/solution.py
+++ b/solution.py
@@ -86,8 +86,8 @@
     return jnp.concatenate([t.reshape(rows, 1) for t in terms] + [blank], 1)
 
 
-def lanes3(value, kind=BF16):
-    lane = lax.broadcasted_iota(jnp.int32, (value.shape[0], LANES), 1)
+def lanes3(value, kind=BF16, first=0):
+    lane = lax.broadcasted_iota(jnp.int32, (value.shape[0], LANES), 1) - first
     high = value.astype(BF16).astype(F32)
     rest = value - high
     middle = rest.astype(BF16).astype(F32)
@@ -177,47 +177,36 @@
 
 
 def out_proj_kernel(place_ref, *refs):
-    piece_refs, weight_ref, out_ref, row_buf, weight_buf, sems = refs[:5], *refs[5:]
-    members, columns, depth = weight_ref.shape
-    copies = []
-    for place in range(members):
-        part = pl.ds(place * depth, depth)
-        group = [pltpu.make_async_copy(weight_ref.at[place], weight_buf.at[place], sems.at[place, 0])]
-        first = 0
-        for n, ref in enumerate(piece_refs):
-            count = ref.shape[0]
-            group.append(
-                pltpu.make_async_copy(
-                    ref.at[:, :, part],
-                    row_buf.at[place, pl.ds(first, count)],
-                    sems.at[place, n + 1],
-                )
-            )
-            first += count
-        for copy in group:
-            copy.start()
-        copies.append(group)
+    weight_refs, piece_refs, out_ref, *bufs = refs[:2], refs[2:7], *refs[7:]
+    piece_bufs, sems = bufs[:5], bufs[5]
+    copies = [
+        pltpu.make_async_copy(ref, buf, sems.at[n])
+        for n, (ref, buf) in enumerate(zip(piece_refs, piece_bufs))
+    ]
+    for copy in copies:
+        copy.start()
     tokens = out_ref.shape[1]
-    total = jnp.zeros((SIDE * SIDE * tokens, columns), F32)
-    for place in range(members):
-        for copy in copies[place]:
-            copy.wait()
-        rows = row_buf[place].reshape(total.shape[0], depth)
-        total = total + dot(rows, weight_buf[place], ((1,), (1,)))
-    total = total.astype(BF16)
     core = place_ref[1]
-    for i in range(SIDE):
-        for j in range(SIDE):
+    block = 0
+    for copy, buf in zip(copies, piece_bufs):
+        copy.wait()
+        total = 0.0
+        for other in range(2):
+            rows = buf[:, other].reshape(buf.shape[0] * tokens, buf.shape[3])
+            total = total + dot(rows, weight_refs[other][...], ((1,), (1,)))
+        total = total.astype(BF16)
+        for n in range(buf.shape[0]):
+            i, j = block // SIDE, block % SIDE
             step_x = i + core * (j - i)
             step_y = j + core * (i - j)
             owner = lax.rem(place_ref[2] + step_x, SIDE) * SIDE + lax.rem(
                 place_ref[3] + step_y, SIDE
             )
-            first = (i * SIDE + j) * tokens
-            out_ref[owner] = total[first : first + tokens]
-
-
-def expert_kernel(place_ref, rows_ref, grads_ref, weight_ref, out_ref, *scratch):
+            out_ref[owner] = total[n * tokens : (n + 1) * tokens]
+            block += 1
+
+
+def expert_kernel(place_ref, rows_ref, grads_ref, weight_ref, out_ref, scaled_ref, scale_ref, *scratch):
     row_buf, grad_buf, weight_buf, sems = scratch
     sources = [member(place_ref, p // 2, p % 2) for p in range(8)]
     copies = start_copies(
@@ -230,19 +219,26 @@
         sems,
     )
     hidden = weight_ref.shape[2] // 3
-    both, hidden_grad = 0.0, 0.0
+    width = weight_ref.shape[1]
+    both, hidden_grad, square = 0.0, 0.0, 0.0
     for place in range(8):
         for copy in copies:
             copy[place].wait()
-        both = both + dot(row_buf[place], weight_buf[place, :, : 2 * hidden])
+        both = both + dot(row_buf[place, :, :width], weight_buf[place, :, : 2 * hidden])
+        square = square + row_buf[place, :, width:].astype(F32)
         hidden_grad = hidden_grad + dot(grad_buf[place], weight_buf[place, :, 2 * hidden :])
-    gate_in, up_in = both[:, :hidden], both[:, hidden:]
+    square = jnp.sum(square, axis=1, keepdims=True)
+    inv_scale = lax.rsqrt(square / (8 * width) + 1e-06)
+    gate_in, up_in = both[:, :hidden] * inv_scale, both[:, hidden:] * inv_scale
     gate_sig = 1.0 / (1.0 + jnp.exp(-gate_in))
     silu = gate_in * gate_sig
     gate_grad = hidden_grad * up_in * gate_sig * (1.0 + gate_in * (1.0 - gate_sig))
     up_grad = hidden_grad * silu
     center = jnp.sum(gate_grad * gate_in + up_grad * up_in, axis=1, keepdims=True)
     slots = gate_in.shape[0]
+    scaled_ref[:, :hidden] = (gate_grad * inv_scale).astype(BF16)
+    scaled_ref[:, hidden:] = (up_grad * inv_scale).astype(BF16)
+    scale_ref[...] = lanes3(inv_scale, first=3)
     out_ref[:slots, :hidden] = gate_grad.astype(BF16)
     out_ref[:slots, hidden : 2 * hidden] = up_grad.astype(BF16)
     out_ref[:slots, 2 * hidden :] = (silu * up_in).astype(BF16)
@@ -250,16 +246,15 @@
     out_ref[slots:, :slots] = lanes3(center, F32).T[: out_ref.shape[0] - slots].astype(BF16)
 
 
-def weight_grad_kernel(rows_ref, grads_ref, hidden_ref, gate_ref, up_ref, down_ref):
+def weight_grad_kernel(rows_ref, grads_ref, hidden_ref, scaled_ref, gate_ref, up_ref, down_ref):
     hidden = gate_ref.shape[1]
-    members, _, slice_width = rows_ref.shape
-    slots = rows_ref.shape[1]
-    grads = hidden_ref[:slots, : 2 * hidden]
+    members, slots, slice_width = grads_ref.shape
+    grads = scaled_ref[...]
     units = hidden_ref[:slots, 2 * hidden :]
 
     def block(place, carry):
         part = pl.ds(pl.multiple_of(place * slice_width, LANES), slice_width)
-        both = dot(rows_ref[place], grads, ((0,), (0,)))
+        both = dot(rows_ref[place, :, :slice_width], grads, ((0,), (0,)))
         gate_ref[part, :] = both[:, :hidden].astype(BF16)
         up_ref[part, :] = both[:, hidden:].astype(BF16)
         down_ref[:, part] = dot(units, grads_ref[place], ((0,), (0,))).astype(BF16)
@@ -268,8 +263,8 @@
     lax.fori_loop(0, members, block, 0)
 
 
-def project_kernel(place_ref, hidden_ref, *refs):
-    weight_refs, out_ref, unit_buf, weight_buf, sems = refs[:8], *refs[8:]
+def project_kernel(place_ref, hidden_ref, scale_ref, *refs):
+    weight_refs, out_ref, unit_buf, weight_buf, sems, scale_buf, scale_sem = refs[:8], *refs[8:]
     copies = start_copies(
         [
             [hidden_ref.at[member(place_ref, p // 2, p % 2)] for p in range(8)],
@@ -278,6 +273,8 @@
         [unit_buf, weight_buf],
         sems,
     )
+    scale_copy = pltpu.make_async_copy(scale_ref, scale_buf, scale_sem)
+    scale_copy.start()
     slice_width, wide = weight_refs[0].shape[1:]
     hidden = wide // 3
     slots = out_ref.shape[0] * out_ref.shape[1]
@@ -292,7 +289,8 @@
         center = center + unit_buf[place, slots:].astype(F32)
     center = jnp.sum(center, axis=0, keepdims=True)
     center = jnp.broadcast_to(center, (LANES, wide)).T[:slots, :1]
-    rows, grads, center = rows.astype(BF16), grads.astype(BF16), lanes3(center)
+    scale_copy.wait()
+    rows, grads, center = rows.astype(BF16), grads.astype(BF16), lanes3(center) + scale_buf[...]
     sources, capacity = out_ref.shape[:2]
     for source in range(sources):
         part = slice(source * capacity, (source + 1) * capacity)
@@ -329,7 +327,6 @@
     top_count = expert_ids.shape[1]
     hidden_width = w_gate.shape[2]
     column_width = w_out.shape[1]
-    part_tokens = token_count // group_count
     capacity = token_count * top_count // ctx_count * 5 // 4
     slot_total = ctx_count * capacity
 
@@ -338,7 +335,8 @@
 
     places = jnp.stack([place_z, core, plane_x, plane_y]).astype(jnp.int32)
 
-    out_weight = group_gather(w_out.T)
+    out_weights = [w_out.T]
+    out_weights.append(swap_core(w_out.T))
     block = (slice_width, 3 * hidden_width)
     weight_blocks, *weight_pairs = call(
         prepare_kernel, [shape(8, *block)] + [shape(2, *block)] * SIDE, 1
@@ -404,81 +402,75 @@
         out_specs=pl.BlockSpec((token_count, heads * value_width), lambda h: (0, h)),
         name="attend",
     )(queries, own_keys, other_keys, key_frames, own_frames, w_uv)
-    head_out = head_out.reshape(group_count, part_tokens, head_count * value_width)
-
-    head_width = head_count * value_width
-    exchange = jnp.concatenate(
-        [head_out, residual.reshape(group_count, part_tokens, slice_width)], 2
-    )
-    exchange = lax.all_to_all(exchange, GROUP, 0, 0, tiled=True)
-    exchange = jnp.transpose(exchange, (1, 0, 2))
-    head_part = exchange[:, :, :head_width].reshape(part_tokens, -1)
-    residual_part = exchange[:, :, head_width:].reshape(part_tokens, model_width)
+
+    keep = lax.dynamic_slice_in_dim(head_out, core * half, half, 0)
+    give = lax.dynamic_slice_in_dim(head_out, (1 - core) * half, half, 0)
+    head_part = jnp.stack([keep, swap_core(give)])
     pieces = halves_ring(direct_ring(head_part, 0), 1)
     columns = call(
         out_proj_kernel,
-        shape(ctx_count, part_tokens, column_width),
+        shape(ctx_count, half, column_width),
         1,
-        whole=0,
-        scratch_shapes=[
-            pltpu.VMEM((group_count, ctx_count, part_tokens, head_width), BF16),
-            pltpu.VMEM((group_count, column_width, head_width), BF16),
-            pltpu.SemaphoreType.DMA((group_count, len(pieces) + 1)),
+        whole=2,
+        scratch_shapes=[pltpu.VMEM(piece.shape, BF16) for piece in pieces]
+        + [pltpu.SemaphoreType.DMA((len(pieces),))],
+    )(places, *out_weights, *pieces)
+    columns = to_experts(columns)
+    per_member = ctx_count // group_count
+    parts = lax.all_to_all(
+        columns.reshape(group_count, per_member * half, column_width), GROUP, 0, 0, tiled=True
+    )
+    attn_sum = jnp.sum(
+        parts.reshape(SIDE, 2, per_member, half, column_width).astype(F32), axis=0
+    )
+    attn_sum = jnp.transpose(attn_sum, (0, 2, 1, 3)).reshape(token_count, slice_width)
+    pre_norm = (residual.astype(F32) + attn_sum).astype(BF16).astype(F32)
+    local_gain = lax.dynamic_slice_in_dim(norm_gain, group_place * slice_width, slice_width)
+    square = jnp.sum(pre_norm * pre_norm, axis=1, keepdims=True)
+    rows_out = jnp.concatenate([(pre_norm * local_gain).astype(BF16), pad_lanes(split3(square))], 1)
+
+    expert_rows = group_gather(to_experts(dot(pick, rows_out).astype(BF16)))
+    hidden_send, scaled, slot_scale = call(
+        expert_kernel,
+        [
+            shape(slot_total + 8, 3 * hidden_width),
+            shape(slot_total, 2 * hidden_width),
+            shape(slot_total, LANES),
         ],
-    )(places, *pieces, out_weight)
-    columns = to_experts(columns)
-    attn_part = jnp.transpose(columns, (1, 0, 2)).reshape(part_tokens, model_width)
-    pre_part = (residual_part.astype(F32) + attn_part.astype(F32)).astype(BF16)
-    pre_wide = pre_part.astype(F32)
-    inv_part = lax.rsqrt(jnp.mean(pre_wide * pre_wide, axis=-1, keepdims=True) + 1e-06)
-    inv_lanes = pad_lanes(split3(inv_part))
-    pre_send = jnp.concatenate(
-        [
-            jnp.transpose(pre_part.reshape(part_tokens, group_count, slice_width), (1, 0, 2)),
-            jnp.broadcast_to(inv_lanes[None], (group_count, part_tokens, 128)),
-        ],
-        2,
-    )
-    pre_back = lax.all_to_all(pre_send, GROUP, 0, 0, tiled=True).reshape(token_count, -1)
-    pre_norm = pre_back[:, :slice_width].astype(F32)
-    inv_scale = jnp.sum(pre_back[:, slice_width : slice_width + 3].astype(F32), axis=1, keepdims=True)
-    unit_rows = pre_norm * inv_scale
-    local_gain = lax.dynamic_slice_in_dim(norm_gain, group_place * slice_width, slice_width)
-    normed = (unit_rows * local_gain).astype(BF16)
-
-    expert_rows = group_gather(to_experts(dot(pick, normed).astype(BF16)))
-    hidden_send = call(
-        expert_kernel,
-        shape(slot_total + 8, 3 * hidden_width),
         1,
         0,
-        scratch_shapes=buffers(*[(8, slot_total, slice_width)] * 2, (8, *block)),
+        scratch_shapes=buffers(
+            (8, slot_total, slice_width + LANES), (8, slot_total, slice_width), (8, *block)
+        ),
     )(places, expert_rows, out_grad, weight_blocks)
     hidden_all = group_gather(hidden_send)
     grad_gate, grad_up, grad_down = call(
         weight_grad_kernel,
         [shape(model_width, hidden_width)] * 2 + [shape(hidden_width, model_width)],
-    )(expert_rows, out_grad, hidden_send)
+    )(expert_rows, out_grad, hidden_send, scaled)
     grad_gate, grad_up, grad_down = grad_gate[None], grad_up[None], grad_down[None]
     back = call(
         project_kernel,
         shape(ctx_count, capacity, 2 * slice_width + LANES),
         1,
         0,
-        scratch_shapes=buffers((8, slot_total + 8, 3 * hidden_width), (8, *block)),
-    )(places, hidden_all, *slice_weights)
+        scratch_shapes=buffers((8, slot_total + 8, 3 * hidden_width), (8, *block))
+        + [pltpu.VMEM((slot_total, LANES), BF16), pltpu.SemaphoreType.DMA],
+    )(places, hidden_all, slot_scale, *slice_weights)
     back = to_experts(back).reshape(slot_total, 2 * slice_width + LANES)
 
-    routed = sum(
-        dot(returns[k], back[:, :slice_width]) * mix_weight[:, k : k + 1] for k in range(top_count)
-    )
+    picks = [dot(returns[k], back) for k in range(top_count)]
+    routed = sum(picks[k][:, :slice_width] * mix_weight[:, k : k + 1] for k in range(top_count))
     layer_out = (pre_norm + routed).astype(BF16)
-    summed = dot(returns[0] + returns[1], back[:, slice_width:])
-    normed_grad = summed[:, :slice_width].astype(BF16).astype(F32)
-    center = jnp.sum(summed[:, slice_width : slice_width + 3], axis=1, keepdims=True) / model_width
+    summed = sum(pick[:, slice_width : 2 * slice_width] for pick in picks)
+    normed_grad = summed.astype(BF16).astype(F32)
+    tail = 2 * slice_width
+    center = sum(jnp.sum(pick[:, tail : tail + 3], axis=1, keepdims=True) for pick in picks)
+    center = center / model_width
+    inv_scale = jnp.sum(picks[0][:, tail + 3 : tail + 6], axis=1, keepdims=True)
     scaled_grad = normed_grad * local_gain
     grad_pre_norm = (
-        grad_out.astype(F32) + inv_scale * (scaled_grad - unit_rows * center)
+        grad_out.astype(F32) + inv_scale * (scaled_grad - pre_norm * inv_scale * center)
     ).astype(BF16)
     return (layer_out, grad_pre_norm, grad_gate, grad_up, grad_down)
 

time: 340 us -> 339 us (level)
  starting transfers between devices: 57 us -> 52.3 us
    all_to_all x1 -> x2, blocking collectives: 14.5 us -> 36.6 us  [to_experts(): return lax.all_to_all(rows, 'ctx', split_axis=0, concat_axis=0, tiled=True)]
    all_to_all x1 -> x0, blocking collectives: 19.8 us -> none  [per_device(): exchange = lax.all_to_all(exchange, GROUP, 0, 0, tiled=True)]
    all_to_all x3 -> x2, waiting for transfers between devices: 24.9 us -> 17.4 us  [to_experts(): return lax.all_to_all(rows, 'ctx', split_axis=0, concat_axis=0, tiled=True)]
    all_to_all x1, waiting for transfers between devices: 5.72 us -> 12.8 us  [per_device(): lax.all_to_all(columns.reshape(group_count, per_member * half, column_wid...]
    all_to_all x3 -> x2, starting transfers between devices: 20.7 us -> 14.1 us  [to_experts(): return lax.all_to_all(rows, 'ctx', split_axis=0, concat_axis=0, tiled=True)]
    all_gather x4 -> x3, waiting for transfers between devices: 25.8 us -> 28.5 us  [group_gather(): return lax.all_gather(block, GROUP, axis=0)]
    ppermute x5 -> x7, starting transfers between devices: 8.43 us -> 10.8 us  [swap_core(): return lax.ppermute(block, GROUP, [(g, g ^ 1) for g in range(8)])]
  transfers between devices with their start and end apart: 29 -> 29, of which waited for: 19 -> 18; matrix products, arithmetic and copies ran while one was open for 4% -> 3% of each run, Pallas kernels for 10% -> 11%
where the time goes in v4:
time: 339 us; the launch traced here: 337 us
  waiting for transfers between devices  158 us (47%)
  starting transfers between devices  52.3 us (15%)
  Pallas kernels  51 us (15%)
  blocking collectives  36.6 us (11%)
  local copies, waits for them, and re-layouts  16.1 us (5%)
  between operations  14.2 us (4%)
  other arithmetic  5.82 us (2%)
    ppermute x3, waiting for transfers between devices, shift_z(): lax.ppermute(block, GROUP, [(g, (g + 2 * step) % 8) for g in range(8)])  66.3 us
    pallas_call x5, Pallas kernels, run(): pl.pallas_call(kernel, out_shape=outs, in_specs=[pl.BlockSpec(memory_spac...  41.5 us
    all_to_all x2, blocking collectives, to_experts(): return lax.all_to_all(rows, 'ctx', split_axis=0, concat_axis=0, tiled=True)  36.6 us
    ppermute x13, waiting for transfers between devices, shift_plane(): return lax.ppermute(block, ALL, pairs)  30.3 us
    all_gather x3, waiting for transfers between devices, group_gather(): return lax.all_gather(block, GROUP, axis=0)  28.5 us
    all_to_all x2, waiting for transfers between devices, to_experts(): return lax.all_to_all(rows, 'ctx', split_axis=0, concat_axis=0, tiled=True)  17.4 us
    ppermute x13, starting transfers between devices, shift_plane(): return lax.ppermute(block, ALL, pairs)  16.2 us
    all_to_all x2, starting transfers between devices, to_experts(): return lax.all_to_all(rows, 'ctx', split_axis=0, concat_axis=0, tiled=True)  14.1 us
  transfers between devices with their start and end apart: 29, of which 18 were waited for; matrix products, arithmetic and copies ran while one was open for 3% of the time, Pallas kernels for 11%

profile of v4, /device:TPU:1, one launch (start us, length us, event | category | flops | bytes accessed | tf_op | source)
XLA Modules:
  0.0 336.9 jit_solution(3803129454090070919)
XLA Ops:
  7.2 0.7 convert_reduce_fusion.2
  7.9 0.7 convert_divide_fusion
  8.6 0.8 copy.71
  9.9 0.7 multiply_add_fusion
  10.8 1.2 fusion
  12.1 1.0 all_to_all.25
  13.1 7.6 %all-to-all-start.3 = ((bf16[16,20,896]{2,1,0:T(8,128)(2,1)}), bf16[16,20,896]{2,1,0:T(8,128)(2,1)S(1)}, u32[]{:S(2)}, u32[]{:S(2)}) async-start(bf16[16,20,896]{2,1,0:T(8,128)(2,1)} %all_to_all.25), calls=%async_computation.3 | async-start | bytes 1376256 | tf_op jit(solution)/shard_map/all_to_all | solution.py:363
  20.7 2.9 collective-permute-start.2
  23.7 0.9 collective-permute-start.1
  24.6 0.6 collective-permute-start.3
  25.3 7.1 %all-to-all-done.3 = bf16[16,20,896]{2,1,0:T(8,128)(2,1)S(1)} async-done(((bf16[16,20,896]{2,1,0:T(8,128)(2,1)}), bf16[16,20,896]{2,1,0:T(8,128)(2,1)S(1)}, u32[]{:S(2)}, u32[]{:S(2)}) %all-to-all-start.3) | async-done | bytes 573472 | tf_op jit(solution)/shard_map/all_to_all | solution.py:363
  32.4 0.9 all_gather.20
  33.7 0.6 broadcast_select_fusion.key_frame_ref
  34.8 2.2 collective-permute-start.5
  37.0 1.2 collective-permute-start.4
  38.2 5.8 %collective-permute-done.6 = bf16[4,64,512]{2,1,0:T(8,128)(2,1)S(1)} collective-permute-done((bf16[4,64,512]{2,1,0:T(8,128)(2,1)S(1)}, bf16[4,64,512]{2,1,0:T(8,128)(2,1)S(1)}, u32[]{:S(2)}, u32[]{:S(2)}) %collective-permute-start.6) | collective-permute-done | bytes 262176 | tf_op jit(solution)/shard_map/ppermute | solution.py:40
  44.0 0.6 collective-permute-done.4
  44.8 5.1 %collective-permute-start.7 = (bf16[1024,512]{1,0:T(8,128)(2,1)S(1)}, bf16[1024,512]{1,0:T(8,128)(2,1)S(1)}, u32[]{:S(2)}, u32[]{:S(2)}) collective-permute-start(bf16[1024,512]{1,0:T(8,128)(2,1)S(1)} %bitcast.59), channel_id=1, source_target_pairs={{0,1},{1,0},{2,3},{3,2},{4,5},{5,4},{6,7},{7,6},{8,9},{9,8},{10,11... | collective-permute-start | bytes 3145736 | tf_op jit(solution)/shard_map/ppermute | solution.py:27
  49.9 0.7 copy.67.own_frame_ref
  50.6 1.8 collective-permute-done.7.far_ref
  52.4 1.0 copy-done.13
  53.3 9.4 %attend.1 = bf16[128,1024]{1,0:T(8,128)(2,1)} custom-call(bf16[128,4096]{1,0:T(8,128)(2,1)} %q_ref.1, bf16[1024,512]{1,0:T(8,128)(2,1)} %bitcast.60, bf16[1024,512]{1,0:T(8,128)(2,1)} %copy-done.13, s32[1,2048]{1,0:T(1,128)} %broadcast_select_fusion.key_frame_ref, s32[128,1]{1,0:T(8,128)} %copy.67.own_frame_ref, bf16[8,512,128]{2,1,0:T(8,128)(2,1)} %uv_ref.1), custom_call_target="tpu_custom_call" | custom-call | tf_op jit(solution)/shard_map/attend/pallas_call | solution.py:390
  62.8 1.0 dynamic-slice_bitcast_fusion
  63.8 0.5 collective-permute-start.8
  64.3 1.0 collective-permute-done.8
  65.5 1.9 collective-permute-start.9
  67.8 4.5 %collective-permute-done.10 = bf16[2,64,1024]{2,1,0:T(8,128)(2,1)S(1)} collective-permute-done((bf16[2,64,1024]{2,1,0:T(8,128)(2,1)S(1)}, bf16[2,64,1024]{2,1,0:T(8,128)(2,1)S(1)}, u32[]{:S(2)}, u32[]{:S(2)}) %collective-permute-start.10) | collective-permute-done | bytes 262176 | tf_op jit(solution)/shard_map/ppermute | solution.py:40
  72.4 2.4 collective-permute-done.9
  75.4 2.7 collective-permute-start.12
  78.1 1.8 collective-permute-start
  79.9 10.7 %collective-permute-done.13.refs_6_ = bf16[4,2,64,1024]{3,2,1,0:T(8,128)(2,1)S(1)} collective-permute-done((bf16[4,2,64,1024]{3,2,1,0:T(8,128)(2,1)S(1)}, bf16[4,2,64,1024]{3,2,1,0:T(8,128)(2,1)S(1)}, u32[]{:S(2)}, u32[]{:S(2)}) %collective-permute-start.13) | collective-permute-done | bytes 1048608 | tf_op jit(solution)/shard_map/ppermute | solution.py:40
  90.6 0.9 slice.68
  91.5 0.9 slice.69
  92.4 2.7 collective-permute-start.15
  95.0 0.6 pad_add_fusion.place_ref
  95.7 5.7 %collective-permute-done.14.refs_4_ = bf16[2,2,64,1024]{3,2,1,0:T(8,128)(2,1)} collective-permute-done((bf16[2,2,64,1024]{3,2,1,0:T(8,128)(2,1)}, bf16[2,2,64,1024]{3,2,1,0:T(8,128)(2,1)}, u32[]{:S(2)}, u32[]{:S(2)}) %collective-permute-start.14) | collective-permute-done | bytes 524320 | tf_op jit(solution)/shard_map/ppermute | solution.py:40
  101.5 7.4 %shard_map.164 = bf16[16,64,448]{2,1,0:T(8,128)(2,1)} custom-call(s32[4]{0:T(128)} %pad_add_fusion.place_ref, bf16[448,1024]{1,0:T(8,128)(2,1)} %bitcast.4.refs_0_, bf16[448,1024]{1,0:T(8,128)(2,1)} %collective-permute-done.refs_1_, bf16[4,2,64,1024]{3,2,1,0:T(8,128)(2,1)} %copy-done.2, bf16[4,2,64,1024]{3,2,1,0:T(8,128)(2,1)} %copy-done.5, ...), custom_call_target="tpu_custom_call" | custom-call | tf_op jit(solution)/shard_map/pallas_call | solution.py:104
  108.9 21.1 %all_to_all.33 = bf16[16,64,448]{2,1,0:T(8,128)(2,1)S(1)} all-to-all(bf16[16,64,448]{2,1,0:T(8,128)(2,1)} %shard_map.164), channel_id=1, replica_groups=mesh['ctx'=16,'role'=2,'exp'=4] {'ctx'}, dimensions={0} | all-to-all | bytes 1835008 | tf_op jit(solution)/shard_map/all_to_all | solution.py:363
  130.0 1.3 copy.68
  131.3 8.7 %all-to-all-start.1 = ((bf16[8,128,448]{1,2,0:T(8,128)(2,1)}), bf16[8,128,448]{1,2,0:T(8,128)(2,1)S(1)}, u32[]{:S(2)}, u32[]{:S(2)}) async-start(bf16[8,128,448]{1,2,0:T(8,128)(2,1)} %copy.68), calls=%async_computation.1 | async-start | bytes 1835008 | tf_op jit(solution)/shard_map/all_to_all | solution.py:420
  140.0 0.8 dynamic_slice.27
  140.8 12.8 %all-to-all-done.1 = bf16[8,128,448]{1,2,0:T(8,128)(2,1)S(1)} async-done(((bf16[8,128,448]{1,2,0:T(8,128)(2,1)}), bf16[8,128,448]{1,2,0:T(8,128)(2,1)S(1)}, u32[]{:S(2)}, u32[]{:S(2)}) %all-to-all-start.1) | async-done | bytes 917536 | tf_op jit(solution)/shard_map/all_to_all | solution.py:420
  153.6 0.5 copy.69
  154.7 0.5 reshape.165
  156.5 15.5 %all_to_all.34 = bf16[16,20,1024]{2,1,0:T(8,128)(2,1)S(1)} all-to-all(bf16[16,20,1024]{2,1,0:T(8,128)(2,1)S(1)} %all_to_all.23), channel_id=1, replica_groups=mesh['ctx'=16,'role'=2,'exp'=4] {'ctx'}, dimensions={0} | all-to-all | bytes 1310720 | tf_op jit(solution)/shard_map/all_to_all | solution.py:363
  172.0 1.0 all_gather.18
  173.0 7.6 %shard_map.165 = (bf16[8,896,384]{2,1,0:T(8,128)(2,1)}, bf16[2,896,384]{2,1,0:T(8,128)(2,1)}, bf16[2,896,384]{2,1,0:T(8,128)(2,1)}, bf16[2,896,384]{2,1,0:T(8,128)(2,1)}, bf16[2,896,384]{2,1,0:T(8,128)(2,1)}) custom-call(s32[4]{0:T(128)} %pad_add_fusion.place_ref, bf16[128,7168]{1,0:T(8,128)(2,1)} %bitcast.65, bf16[7168,128]{1,0:T(8,128)(2,1)} %bitcast.66, ...), custom_call_target="tpu_custom_call" | custom-call | tf_op jit(solution)/shard_map/pallas_call | solution.py:104
  180.7 27.6 %all-gather.5.cloned.1.call-done.rows_ref = bf16[8,320,1024]{2,1,0:T(8,128)(2,1)} async-done(((bf16[1,320,1024]{2,1,0:T(8,128)(2,1)}), bf16[8,320,1024]{2,1,0:T(8,128)(2,1)}) %all-gather.5.cloned.1.call-update) | async-done | bytes 5242896 | tf_op jit(solution)/shard_map/all_gather | solution.py:57
  208.3 7.9 %shard_map.166 = (bf16[328,384]{1,0:T(8,128)(2,1)}, bf16[320,256]{1,0:T(8,128)(2,1)}, bf16[320,128]{1,0:T(8,128)(2,1)}) custom-call(s32[4]{0:T(128)} %pad_add_fusion.place_ref, bf16[8,320,1024]{2,1,0:T(8,128)(2,1)} %all-gather.5.cloned.1.call-done.rows_ref, bf16[8,320,896]{2,1,0:T(8,128)(2,1)} %all-gather.7.cloned.1.call-done.grads_ref, ...), custom_call_target="tpu_custom_call" | custom-call | tf_op jit(solution)/shard_map/pallas_call | solution.py:104
  216.3 0.6 collective-permute-start.17
  216.8 1.5 collective-permute-start.19
  218.6 1.1 collective-permute-start.16
  219.8 35.1 %collective-permute-done.17.refs_2_ = bf16[2,896,384]{2,1,0:T(8,128)(2,1)S(1)} collective-permute-done((bf16[2,896,384]{2,1,0:T(8,128)(2,1)}, bf16[2,896,384]{2,1,0:T(8,128)(2,1)S(1)}, u32[]{:S(2)}, u32[]{:S(2)}) %collective-permute-start.17) | collective-permute-done | bytes 1376288 | tf_op jit(solution)/shard_map/ppermute | solution.py:23
  254.9 1.7 collective-permute-start.18
  256.7 31.2 %collective-permute-done.21.refs_6_ = bf16[2,896,384]{2,1,0:T(8,128)(2,1)S(1)} collective-permute-done((bf16[2,896,384]{2,1,0:T(8,128)(2,1)S(1)}, bf16[2,896,384]{2,1,0:T(8,128)(2,1)S(1)}, u32[]{:S(2)}, u32[]{:S(2)}) %collective-permute-start.21) | collective-permute-done | bytes 1376288 | tf_op jit(solution)/shard_map/ppermute | solution.py:23
  288.4 0.5 copy-done.9
  289.0 0.5 copy-done.10
  289.9 1.1 copy-done.12
  291.3 0.9 all-gather.9.cloned.1.call-done
  292.2 7.6 %shard_map.167 = bf16[16,20,1920]{2,1,0:T(8,128)(2,1)} custom-call(s32[4]{0:T(128)} %pad_add_fusion.place_ref, bf16[8,328,384]{2,1,0:T(8,128)(2,1)} %bitcast.64, bf16[320,128]{1,0:T(8,128)(2,1)} %get-tuple-element.24.scale_ref, bf16[2,896,384]{2,1,0:T(8,128)(2,1)} %get-tuple-element.25.refs_0_, bf16[2,896,384]{2,1,0:T(8,128)(2,1)} %copy-done.10, ...), custom_call_target="tpu_custom_call" | custom-call | tf_op jit(solution)/shard_map/pallas_call | solution.py:104
  299.7 6.5 %all-to-all-start.4 = ((bf16[16,20,1920]{2,1,0:T(8,128)(2,1)}), bf16[16,20,1920]{2,1,0:T(8,128)(2,1)S(1)}, u32[]{:S(2)}, u32[]{:S(2)}) async-start(bf16[16,20,1920]{2,1,0:T(8,128)(2,1)} %shard_map.167), calls=%async_computation.4 | async-start | bytes 2949120 | tf_op jit(solution)/shard_map/all_to_all | solution.py:363
  306.3 11.0 %shard_map.168 = (bf16[7168,128]{1,0:T(8,128)(2,1)}, bf16[7168,128]{1,0:T(8,128)(2,1)}, bf16[128,7168]{1,0:T(8,128)(2,1)}) custom-call(bf16[8,320,1024]{2,1,0:T(8,128)(2,1)} %all-gather.5.cloned.1.call-done.rows_ref, bf16[8,320,896]{2,1,0:T(8,128)(2,1)} %all-gather.7.cloned.1.call-done.grads_ref, bf16[328,384]{1,0:T(8,128)(2,1)} %get-tuple-element.23.hidden_ref, ...), custom_call_target="tpu_custom_call" | custom-call | tf_op jit(solution)/shard_map/pallas_call | solution.py:104
  317.3 10.3 %all-to-all-done.4 = bf16[16,20,1920]{2,1,0:T(8,128)(2,1)S(1)} async-done(((bf16[16,20,1920]{2,1,0:T(8,128)(2,1)}), bf16[16,20,1920]{2,1,0:T(8,128)(2,1)S(1)}, u32[]{:S(2)}, u32[]{:S(2)}) %all-to-all-start.4) | async-done | bytes 1228832 | tf_op jit(solution)/shard_map/all_to_all | solution.py:363
  329.4 1.0 fusion.8
  (102 shorter events, 8.7 us)
Async XLA Ops:
  7.2 13.6 %copy-start = (bf16[128,512]{1,0:T(8,128)(2,1)S(1)}, bf16[128,512]{1,0:T(8,128)(2,1)}, u32[]{:S(2)}) copy-start(bf16[128,512]{1,0:T(8,128)(2,1)} %param.14) | copy-start | bytes 393220
  12.1 13.1 %copy-start.16 = (s32[2048]{0:T(1024)S(1)}, s32[2048]{0:T(1024)}, u32[]{:S(2)}) copy-start(s32[2048]{0:T(1024)} %param.15) | copy-start | bytes 24580
  13.1 19.3 %all-to-all-start.3 = ((bf16[16,20,896]{2,1,0:T(8,128)(2,1)}), bf16[16,20,896]{2,1,0:T(8,128)(2,1)S(1)}, u32[]{:S(2)}, u32[]{:S(2)}) async-start(bf16[16,20,896]{2,1,0:T(8,128)(2,1)} %all_to_all.25), calls=%async_computation.3 | async-start | bytes 1376256 | tf_op jit(solution)/shard_map/all_to_all | solution.py:363
  20.6 160.0 %all-gather.7.cloned.1.call-start = ((), (), s32[]{:S(2)}) async-start(), calls=%async_computation.6 | async-start | bytes 5160960 | tf_op jit(solution)/shard_map/all_gather | solution.py:57
  20.7 13.6 %collective-permute-start.2 = (bf16[64,512]{1,0:T(8,128)(2,1)S(1)}, bf16[64,512]{1,0:T(8,128)(2,1)S(1)}, u32[]{:S(2)}, u32[]{:S(2)}) collective-permute-start(bf16[64,512]{1,0:T(8,128)(2,1)S(1)} %constant_dynamic-slice_fusion.1), channel_id=1, source_target_pairs={{0,16},{1,65},{2,18},{3,67},{4,20},{5,69},{6,22},{7,71},{8,24},{9,... | collective-permute-start | bytes 196616 | tf_op jit(solution)/shard_map/ppermute | solution.py:40
  23.7 10.7 %collective-permute-start.1 = (bf16[64,512]{1,0:T(8,128)(2,1)S(1)}, bf16[64,512]{1,0:T(8,128)(2,1)S(1)}, u32[]{:S(2)}, u32[]{:S(2)}) collective-permute-start(bf16[64,512]{1,0:T(8,128)(2,1)S(1)} %constant_dynamic-slice_fusion.1), channel_id=1, source_target_pairs={{0,24},{1,97},{2,26},{3,99},{4,28},{5,101},{6,30},{7,103},{8,0},{9... | collective-permute-start | bytes 196616 | tf_op jit(solution)/shard_map/ppermute | solution.py:40
  24.6 9.8 %collective-permute-start.3 = (bf16[64,512]{1,0:T(8,128)(2,1)S(1)}, bf16[64,512]{1,0:T(8,128)(2,1)S(1)}, u32[]{:S(2)}, u32[]{:S(2)}) collective-permute-start(bf16[64,512]{1,0:T(8,128)(2,1)S(1)} %constant_dynamic-slice_fusion.1), channel_id=1, source_target_pairs={{0,8},{1,33},{2,10},{3,35},{4,12},{5,37},{6,14},{7,39},{8,16},{9,4... | collective-permute-start | bytes 196616 | tf_op jit(solution)/shard_map/ppermute | solution.py:40
  34.4 9.6 %collective-permute-start.6 = (bf16[4,64,512]{2,1,0:T(8,128)(2,1)S(1)}, bf16[4,64,512]{2,1,0:T(8,128)(2,1)S(1)}, u32[]{:S(2)}, u32[]{:S(2)}) collective-permute-start(bf16[4,64,512]{2,1,0:T(8,128)(2,1)S(1)} %pad_maximum_fusion.2), channel_id=1, source_target_pairs={{0,32},{1,9},{2,34},{3,11},{4,36},{5,13},{6,38},{7,15},{8,40},{9,1... | collective-permute-start | bytes 786440 | tf_op jit(solution)/shard_map/ppermute | solution.py:40
  34.8 9.2 %collective-permute-start.5 = (bf16[4,64,512]{2,1,0:T(8,128)(2,1)S(1)}, bf16[4,64,512]{2,1,0:T(8,128)(2,1)S(1)}, u32[]{:S(2)}, u32[]{:S(2)}) collective-permute-start(bf16[4,64,512]{2,1,0:T(8,128)(2,1)S(1)} %pad_maximum_fusion.2), channel_id=1, source_target_pairs={{0,64},{1,17},{2,66},{3,19},{4,68},{5,21},{6,70},{7,23},{8,72},{9,... | collective-permute-start | bytes 786440 | tf_op jit(solution)/shard_map/ppermute | solution.py:40
  37.0 7.6 %collective-permute-start.4 = (bf16[4,64,512]{2,1,0:T(8,128)(2,1)S(1)}, bf16[4,64,512]{2,1,0:T(8,128)(2,1)S(1)}, u32[]{:S(2)}, u32[]{:S(2)}) collective-permute-start(bf16[4,64,512]{2,1,0:T(8,128)(2,1)S(1)} %pad_maximum_fusion.2), channel_id=1, source_target_pairs={{0,96},{1,25},{2,98},{3,27},{4,100},{5,29},{6,102},{7,31},{8,104},... | collective-permute-start | bytes 786440 | tf_op jit(solution)/shard_map/ppermute | solution.py:40
  44.8 7.6 %copy-start.3 = (bf16[4,4,64,512]{3,2,1,0:T(8,128)(2,1)}, bf16[4,4,64,512]{3,2,1,0:T(8,128)(2,1)S(1)}, u32[]{:S(2)}) copy-start(bf16[4,4,64,512]{3,2,1,0:T(8,128)(2,1)S(1)} %pad_maximum_fusion) | copy-start | bytes 3145732
  44.8 7.6 %collective-permute-start.7 = (bf16[1024,512]{1,0:T(8,128)(2,1)S(1)}, bf16[1024,512]{1,0:T(8,128)(2,1)S(1)}, u32[]{:S(2)}, u32[]{:S(2)}) collective-permute-start(bf16[1024,512]{1,0:T(8,128)(2,1)S(1)} %bitcast.59), channel_id=1, source_target_pairs={{0,1},{1,0},{2,3},{3,2},{4,5},{5,4},{6,7},{7,6},{8,9},{9,8},{10,11... | collective-permute-start | bytes 3145736 | tf_op jit(solution)/shard_map/ppermute | solution.py:27
  52.4 1.0 copy-start.13
  63.8 1.5 collective-permute-start.8
  65.3 7.1 %collective-permute-start.10 = (bf16[2,64,1024]{2,1,0:T(8,128)(2,1)S(1)}, bf16[2,64,1024]{2,1,0:T(8,128)(2,1)S(1)}, u32[]{:S(2)}, u32[]{:S(2)}) collective-permute-start(bf16[2,64,1024]{2,1,0:T(8,128)(2,1)S(1)} %get-tuple-element.40), channel_id=1, source_target_pairs={{0,16},{1,65},{2,18},{3,67},{4,20},{5,69},{6,22},{7,71},{8,24},{9,... | collective-permute-start | bytes 786440 | tf_op jit(solution)/shard_map/ppermute | solution.py:40
  65.5 9.2 %collective-permute-start.9 = (bf16[2,64,1024]{2,1,0:T(8,128)(2,1)S(1)}, bf16[2,64,1024]{2,1,0:T(8,128)(2,1)S(1)}, u32[]{:S(2)}, u32[]{:S(2)}) collective-permute-start(bf16[2,64,1024]{2,1,0:T(8,128)(2,1)S(1)} %get-tuple-element.40), channel_id=1, source_target_pairs={{0,24},{1,97},{2,26},{3,99},{4,28},{5,101},{6,30},{7,103},{8,0},{9... | collective-permute-start | bytes 786440 | tf_op jit(solution)/shard_map/ppermute | solution.py:40
  67.4 7.8 %collective-permute-start.11 = (bf16[2,64,1024]{2,1,0:T(8,128)(2,1)S(1)}, bf16[2,64,1024]{2,1,0:T(8,128)(2,1)S(1)}, u32[]{:S(2)}, u32[]{:S(2)}) collective-permute-start(bf16[2,64,1024]{2,1,0:T(8,128)(2,1)S(1)} %get-tuple-element.40), channel_id=1, source_target_pairs={{0,8},{1,33},{2,10},{3,35},{4,12},{5,37},{6,14},{7,39},{8,16},{9,4... | collective-permute-start | bytes 786440 | tf_op jit(solution)/shard_map/ppermute | solution.py:40
  75.3 26.2 %copy-start.2 = (bf16[4,2,64,1024]{3,2,1,0:T(8,128)(2,1)}, bf16[4,2,64,1024]{3,2,1,0:T(8,128)(2,1)S(1)}, u32[]{:S(2)}) copy-start(bf16[4,2,64,1024]{3,2,1,0:T(8,128)(2,1)S(1)} %pad_maximum_fusion.1.refs_2_) | copy-start | bytes 3145732
  75.3 15.2 %collective-permute-start.13 = (bf16[4,2,64,1024]{3,2,1,0:T(8,128)(2,1)S(1)}, bf16[4,2,64,1024]{3,2,1,0:T(8,128)(2,1)S(1)}, u32[]{:S(2)}, u32[]{:S(2)}) collective-permute-start(bf16[4,2,64,1024]{3,2,1,0:T(8,128)(2,1)S(1)} %pad_maximum_fusion.1.refs_2_), channel_id=1, source_target_pairs={{0,32},{1,9},{2,34},{3,11},{4,36},{5,13},{6,38},{7,15},{8,40},{9,1... | collective-permute-start | bytes 3145736 | tf_op jit(solution)/shard_map/ppermute | solution.py:40
  75.4 16.1 %collective-permute-start.12 = (bf16[4,2,64,1024]{3,2,1,0:T(8,128)(2,1)S(1)}, bf16[4,2,64,1024]{3,2,1,0:T(8,128)(2,1)S(1)}, u32[]{:S(2)}, u32[]{:S(2)}) collective-permute-start(bf16[4,2,64,1024]{3,2,1,0:T(8,128)(2,1)S(1)} %pad_maximum_fusion.1.refs_2_), channel_id=1, source_target_pairs={{0,96},{1,25},{2,98},{3,27},{4,100},{5,29},{6,102},{7,31},{8,104},... | collective-permute-start | bytes 3145736 | tf_op jit(solution)/shard_map/ppermute | solution.py:40
  78.1 17.6 %collective-permute-start = (bf16[448,1024]{1,0:T(8,128)(2,1)}, bf16[448,1024]{1,0:T(8,128)(2,1)}, u32[]{:S(2)}, u32[]{:S(2)}) collective-permute-start(bf16[448,1024]{1,0:T(8,128)(2,1)} %bitcast.4.refs_0_), channel_id=1, source_target_pairs={{0,1},{1,0},{2,3},{3,2},{4,5},{5,4},{6,7},{7,6},{8,9},{9,8},{10,11... | collective-permute-start | bytes 2752520 | tf_op jit(solution)/shard_map/ppermute | solution.py:27
  90.6 10.9 %copy-start.4 = (bf16[4,2,64,1024]{3,2,1,0:T(8,128)(2,1)}, bf16[4,2,64,1024]{3,2,1,0:T(8,128)(2,1)S(1)}, u32[]{:S(2)}) copy-start(bf16[4,2,64,1024]{3,2,1,0:T(8,128)(2,1)S(1)} %collective-permute-done.13.refs_6_) | copy-start | bytes 3145732
  91.5 9.9 %collective-permute-start.14 = (bf16[2,2,64,1024]{3,2,1,0:T(8,128)(2,1)}, bf16[2,2,64,1024]{3,2,1,0:T(8,128)(2,1)}, u32[]{:S(2)}, u32[]{:S(2)}) collective-permute-start(bf16[2,2,64,1024]{3,2,1,0:T(8,128)(2,1)} %slice.68), channel_id=1, source_target_pairs={{0,32},{1,9},{2,34},{3,11},{4,36},{5,13},{6,38},{7,15},{8,40},{9,1... | collective-permute-start | bytes 1572872 | tf_op jit(solution)/shard_map/ppermute | solution.py:40
  91.5 10.0 %copy-start.5 = (bf16[4,2,64,1024]{3,2,1,0:T(8,128)(2,1)}, bf16[4,2,64,1024]{3,2,1,0:T(8,128)(2,1)S(1)}, u32[]{:S(2)}) copy-start(bf16[4,2,64,1024]{3,2,1,0:T(8,128)(2,1)S(1)} %collective-permute-done.12.refs_3_) | copy-start | bytes 3145732
  92.4 9.1 %collective-permute-start.15 = (bf16[2,2,64,1024]{3,2,1,0:T(8,128)(2,1)}, bf16[2,2,64,1024]{3,2,1,0:T(8,128)(2,1)}, u32[]{:S(2)}, u32[]{:S(2)}) collective-permute-start(bf16[2,2,64,1024]{3,2,1,0:T(8,128)(2,1)} %slice.69), channel_id=1, source_target_pairs={{0,96},{1,25},{2,98},{3,27},{4,100},{5,29},{6,102},{7,31},{8,104},... | collective-permute-start | bytes 1572872 | tf_op jit(solution)/shard_map/ppermute | solution.py:40
  131.3 22.3 %all-to-all-start.1 = ((bf16[8,128,448]{1,2,0:T(8,128)(2,1)}), bf16[8,128,448]{1,2,0:T(8,128)(2,1)S(1)}, u32[]{:S(2)}, u32[]{:S(2)}) async-start(bf16[8,128,448]{1,2,0:T(8,128)(2,1)} %copy.68), calls=%async_computation.1 | async-start | bytes 1835008 | tf_op jit(solution)/shard_map/all_to_all | solution.py:420
  140.0 68.3 %all-gather.5.cloned.1.call-start = ((), (), s32[]{:S(2)}) async-start(), calls=%async_computation.5 | async-start | bytes 5898240 | tf_op jit(solution)/shard_map/all_gather | solution.py:57
  154.3 0.9 copy-start.15
  173.0 119.2 %all-gather.9.cloned.1.call-start = ((), (), s32[]{:S(2)}) async-start(), calls=%async_computation.7 | async-start | bytes 2267136 | tf_op jit(solution)/shard_map/all_gather | solution.py:57
  208.3 9.9 %copy-start.17 = (bf16[2,896,384]{2,1,0:T(8,128)(2,1)S(1)}, bf16[2,896,384]{2,1,0:T(8,128)(2,1)}, u32[]{:S(2)}) copy-start(bf16[2,896,384]{2,1,0:T(8,128)(2,1)} %get-tuple-element.28) | copy-start | bytes 4128772
  208.3 10.3 %copy-start.6 = (bf16[2,896,384]{2,1,0:T(8,128)(2,1)S(1)}, bf16[2,896,384]{2,1,0:T(8,128)(2,1)}, u32[]{:S(2)}) copy-start(bf16[2,896,384]{2,1,0:T(8,128)(2,1)} %get-tuple-element.25.refs_0_) | copy-start | bytes 4128772
  216.3 38.6 %collective-permute-start.17 = (bf16[2,896,384]{2,1,0:T(8,128)(2,1)}, bf16[2,896,384]{2,1,0:T(8,128)(2,1)S(1)}, u32[]{:S(2)}, u32[]{:S(2)}) collective-permute-start(bf16[2,896,384]{2,1,0:T(8,128)(2,1)} %get-tuple-element.26), channel_id=1, source_target_pairs={{0,6},{1,7},{2,0},{3,1},{4,2},{5,3},{6,4},{7,5},{8,14},{9,15},{10,... | collective-permute-start | bytes 4128776 | tf_op jit(solution)/shard_map/ppermute | solution.py:23
  216.8 39.8 %collective-permute-start.19 = (bf16[2,896,384]{2,1,0:T(8,128)(2,1)}, bf16[2,896,384]{2,1,0:T(8,128)(2,1)S(1)}, u32[]{:S(2)}, u32[]{:S(2)}) collective-permute-start(bf16[2,896,384]{2,1,0:T(8,128)(2,1)} %get-tuple-element.27), channel_id=1, source_target_pairs={{0,4},{1,5},{2,6},{3,7},{4,0},{5,1},{6,2},{7,3},{8,12},{9,13},{10,... | collective-permute-start | bytes 4128776 | tf_op jit(solution)/shard_map/ppermute | solution.py:23
  218.3 69.6 %collective-permute-start.21 = (bf16[2,896,384]{2,1,0:T(8,128)(2,1)S(1)}, bf16[2,896,384]{2,1,0:T(8,128)(2,1)S(1)}, u32[]{:S(2)}, u32[]{:S(2)}) collective-permute-start(bf16[2,896,384]{2,1,0:T(8,128)(2,1)S(1)} %copy-done.17), channel_id=1, source_target_pairs={{0,2},{1,3},{2,4},{3,5},{4,6},{5,7},{6,0},{7,1},{8,10},{9,11},{10,... | collective-permute-start | bytes 4128776 | tf_op jit(solution)/shard_map/ppermute | solution.py:23
  218.6 69.7 %collective-permute-start.16 = (bf16[2,896,384]{2,1,0:T(8,128)(2,1)S(1)}, bf16[2,896,384]{2,1,0:T(8,128)(2,1)S(1)}, u32[]{:S(2)}, u32[]{:S(2)}) collective-permute-start(bf16[2,896,384]{2,1,0:T(8,128)(2,1)S(1)} %copy-done.6), channel_id=1, source_target_pairs={{0,1},{1,0},{2,3},{3,2},{4,5},{5,4},{6,7},{7,6},{8,9},{9,8},{10,11... | collective-permute-start | bytes 4128776 | tf_op jit(solution)/shard_map/ppermute | solution.py:27
  254.9 33.5 %copy-start.7 = (bf16[2,896,384]{2,1,0:T(8,128)(2,1)}, bf16[2,896,384]{2,1,0:T(8,128)(2,1)S(1)}, u32[]{:S(2)}) copy-start(bf16[2,896,384]{2,1,0:T(8,128)(2,1)S(1)} %collective-permute-done.17.refs_2_) | copy-start | bytes 4128772
  254.9 33.5 %collective-permute-start.18 = (bf16[2,896,384]{2,1,0:T(8,128)(2,1)S(1)}, bf16[2,896,384]{2,1,0:T(8,128)(2,1)S(1)}, u32[]{:S(2)}, u32[]{:S(2)}) collective-permute-start(bf16[2,896,384]{2,1,0:T(8,128)(2,1)S(1)} %collective-permute-done.17.refs_2_), channel_id=1, source_target_pairs={{0,1},{1,0},{2,3},{3,2},{4,5},{5,4},{6,7},{7,6},{8,9},{9,8},{10,11... | collective-permute-start | bytes 4128776 | tf_op jit(solution)/shard_map/ppermute | solution.py:27
  256.6 31.8 %copy-start.8 = (bf16[2,896,384]{2,1,0:T(8,128)(2,1)}, bf16[2,896,384]{2,1,0:T(8,128)(2,1)S(1)}, u32[]{:S(2)}) copy-start(bf16[2,896,384]{2,1,0:T(8,128)(2,1)S(1)} %collective-permute-done.19.refs_4_) | copy-start | bytes 4128772
  256.6 31.8 %collective-permute-start.20 = (bf16[2,896,384]{2,1,0:T(8,128)(2,1)S(1)}, bf16[2,896,384]{2,1,0:T(8,128)(2,1)S(1)}, u32[]{:S(2)}, u32[]{:S(2)}) collective-permute-start(bf16[2,896,384]{2,1,0:T(8,128)(2,1)S(1)} %collective-permute-done.19.refs_4_), channel_id=1, source_target_pairs={{0,1},{1,0},{2,3},{3,2},{4,5},{5,4},{6,7},{7,6},{8,9},{9,8},{10,11... | collective-permute-start | bytes 4128776 | tf_op jit(solution)/shard_map/ppermute | solution.py:27
  287.9 1.1 copy-start.9
  287.9 3.4 %collective-permute-start.22 = (bf16[2,896,384]{2,1,0:T(8,128)(2,1)S(1)}, bf16[2,896,384]{2,1,0:T(8,128)(2,1)}, u32[]{:S(2)}, u32[]{:S(2)}) collective-permute-start(bf16[2,896,384]{2,1,0:T(8,128)(2,1)S(1)} %collective-permute-done.21.refs_6_), channel_id=1, source_target_pairs={{0,1},{1,0},{2,3},{3,2},{4,5},{5,4},{6,7},{7,6},{8,9},{9,8},{10,11... | collective-permute-start | bytes 4128776 | tf_op jit(solution)/shard_map/ppermute | solution.py:27
  288.4 1.1 copy-start.10
  288.4 1.5 copy-start.11
  289.9 1.1 copy-start.12
  299.7 27.9 %all-to-all-start.4 = ((bf16[16,20,1920]{2,1,0:T(8,128)(2,1)}), bf16[16,20,1920]{2,1,0:T(8,128)(2,1)S(1)}, u32[]{:S(2)}, u32[]{:S(2)}) async-start(bf16[16,20,1920]{2,1,0:T(8,128)(2,1)} %shard_map.167), calls=%async_computation.4 | async-start | bytes 2949120 | tf_op jit(solution)/shard_map/all_to_all | solution.py:363
  328.4 0.9 copy-start.14
  329.2 1.1 copy-start.1
Sparse Core Ops, SparseCore 0:
  33.5 36.3 all-gather.6
  173.1 35.1 all-gather.4
  216.4 75.7 all-gather.8
